TPU v7x, 32 devices: a whole 2x2x4 slice. The times are simulated.
32 devices in a mesh: dp: 16 (over z, y, x), tensor: 2 (over core).
Axes of the slice: x: 2, y: 2, z: 4, core: 2. Of those that a mesh axis runs over, the one named last changes fastest.
Arguments:
- activations: bfloat16 [8192, 8192], P('dp', 'tensor'), may hold values from -6 to 6
- out_grads: bfloat16 [8192, 16384], P('dp', 'tensor'), may hold values from -0.0625 to 0.0625
- sketch: float32 [8192, 512], P('dp'), may hold values from -6 to 6
- first_moment: float32 [512, 16384], P('dp', 'tensor'), may hold values from -6 to 6
- second_moment: float32 [512, 16384], P('dp', 'tensor'), may hold values from 0.05 to 2
Outputs:
- update: float32 [8192, 16384], P('dp', 'tensor')
- first_new: float32 [512, 16384], P('dp', 'tensor')
- second_new: float32 [512, 16384], P('dp', 'tensor')
All inputs are finite; a program needn't handle non-finite values.
Results may differ from a plain program's by a relative error of at most 0.0041.
Values may be sent and summed in bfloat16 or wider, within the bound.
No kernel may reach another device: no remote copies, remote signals or barrier semaphores. Data moves between devices by JAX's collectives and lax.ppermute only.
A program may use at most 128 MiB of HBM per device.

v0:
```python
import math

import jax
import jax.numpy as jnp
from jax import lax
from jax.sharding import PartitionSpec as P

D = 8192
R = 512


BETA_ONE = 0.9
BETA_TWO = 0.999
CORRECT_ONE = 0.9999999993
CORRECT_TWO = 0.18135117
EPSILON = 1e-08


def local(activations, out_grads, sketch, first_moment, second_moment):
    highest = lax.Precision.HIGHEST
    features = lax.all_gather(activations, "tensor", axis=1, tiled=True)
    local_gram = jnp.dot(sketch.T, sketch, precision=highest, preferred_element_type=jnp.float32)
    sketch_gram = lax.psum(local_gram, "dp")
    cholesky_factor = jnp.linalg.cholesky(sketch_gram)
    own_rows = jax.scipy.linalg.solve_triangular(cholesky_factor, sketch.T, lower=True).T.astype(
        jnp.bfloat16
    )
    basis_full = lax.all_gather(own_rows, "dp", axis=0, tiled=True)
    projected = jnp.dot(features, basis_full, preferred_element_type=jnp.float32).astype(
        jnp.bfloat16
    )
    columns = projected
    grad_low = lax.psum_scatter(
        jnp.dot(columns.T, out_grads, preferred_element_type=jnp.float32),
        "dp",
        scatter_dimension=0,
        tiled=True,
    )
    first_new = BETA_ONE * first_moment + (1.0 - BETA_ONE) * grad_low
    second_new = BETA_TWO * second_moment + (1.0 - BETA_TWO) * grad_low * grad_low
    direction = (first_new / CORRECT_ONE / (jnp.sqrt(second_new / CORRECT_TWO) + EPSILON)).astype(
        jnp.bfloat16
    )
    update_scale = math.sqrt(D / R)
    columns = own_rows
    update = update_scale * jnp.dot(
        columns,
        lax.all_gather(direction, "dp", axis=0, tiled=True),
        preferred_element_type=jnp.float32,
    )
    return (update, first_new, second_new)


def solution(mesh):
    return jax.shard_map(
        local,
        mesh=mesh,
        in_specs=(
            P("dp", "tensor"),
            P("dp", "tensor"),
            P("dp", None),
            P("dp", "tensor"),
            P("dp", "tensor"),
        ),
        out_specs=(P("dp", "tensor"), P("dp", "tensor"), P("dp", "tensor")),
        check_vma=False,
    )
```

profile of v0, /device:TPU:0, one launch (start us, length us, event | category | flops | bytes accessed | tf_op | source)
XLA Modules:
  0.0 897.8 jit_solution(7498624918526684430)
XLA Ops:
  8.0 4.5 fusion.38
  12.6 0.5 all-gather.6.cloned.1.call-update
  13.2 115.9 %all-reduce.3.cloned.1.call-done = f32[512,512]{0,1:T(8,128)} async-done(((f32[512,512]{0,1:T(8,128)}), f32[512,512]{0,1:T(8,128)}) %all-reduce.3.cloned.1.call-update) | async-done | bytes 1048592 | tf_op jit(solution)/shard_map/psum | solution.py:23
  129.1 1.6 copy.9
  130.7 1.4 fusion.2
  132.2 11.7 %cholesky.104 = f32[128,128]{1,0:T(8,128)S(1)} custom-call(f32[128,128]{1,0:T(8,128)S(1)} %cholesky.266), custom_call_target="Cholesky" | custom-call | tf_op jit(solution)/shard_map/jit(cholesky)/cholesky | solution.py:24
  143.9 9.8 %custom-call.31 = f32[1,128,128]{1,2,0:T(8,128)S(1)} custom-call(f32[1,128,128]{2,1,0:T(8,128)S(1)} %get-tuple-element.33), custom_call_target="InvertDiagBlocksLowerTriangular" | custom-call | tf_op jit(solution)/shard_map/jit(cholesky)/cholesky | solution.py:24
  153.7 0.1 cholesky.224
  153.9 0.3 constant_dynamic-update-slice_fusion.3
  154.2 0.3 convolution_subtract_fusion.3
  154.5 11.7 %cholesky.217 = f32[128,128]{1,0:T(8,128)S(1)} custom-call(f32[128,128]{1,0:T(8,128)S(1)} %cholesky.270), custom_call_target="Cholesky" | custom-call | tf_op jit(solution)/shard_map/jit(cholesky)/cholesky | solution.py:24
  166.3 10.1 %custom-call.32 = f32[1,128,128]{1,2,0:T(8,128)S(1)} custom-call(f32[1,128,128]{2,1,0:T(8,128)S(1)} %get-tuple-element.30), custom_call_target="InvertDiagBlocksLowerTriangular" | custom-call | tf_op jit(solution)/shard_map/jit(cholesky)/cholesky | solution.py:24
  176.4 0.3 convolution_dynamic-update-slice_fusion
  176.7 0.4 convolution_subtract_fusion.4
  177.1 11.7 %cholesky.238 = f32[128,128]{1,0:T(8,128)S(1)} custom-call(f32[128,128]{1,0:T(8,128)S(1)} %cholesky.275), custom_call_target="Cholesky" | custom-call | tf_op jit(solution)/shard_map/jit(cholesky)/cholesky | solution.py:24
  188.8 9.8 %custom-call.33 = f32[1,128,128]{1,2,0:T(8,128)S(1)} custom-call(f32[1,128,128]{2,1,0:T(8,128)S(1)} %get-tuple-element.27), custom_call_target="InvertDiagBlocksLowerTriangular" | custom-call | tf_op jit(solution)/shard_map/jit(cholesky)/cholesky | solution.py:24
  198.6 0.2 convolution_dynamic-update-slice_fusion.1
  198.9 0.4 convolution_subtract_fusion.5
  199.2 11.7 %cholesky.255 = f32[128,128]{1,0:T(8,128)S(1)} custom-call(f32[128,128]{1,0:T(8,128)S(1)} %convolution_subtract_fusion.5), custom_call_target="Cholesky" | custom-call | tf_op jit(solution)/shard_map/jit(cholesky)/cholesky | solution.py:24
  211.0 0.7 compare_reduce_fusion.2
  212.9 0.6 compare_reduce_fusion.1
  214.2 0.6 compare_reduce_fusion
  215.5 0.3 select_select_fusion
  215.8 10.4 %while.1 = (s32[]{:T(128)}, f32[512,512]{1,0:T(8,128)S(1)}, s32[4,2]{0,1:T(2,128)S(1)}, f32[4,128,128]{2,1,0:T(8,128)}, s32[]{:T(128)}) while((s32[]{:T(128)}, f32[512,512]{1,0:T(8,128)S(1)}, s32[4,2]{0,1:T(2,128)S(1)}, f32[4,128,128]{2,1,0:T(8,128)}, s32[]{:T(128)}) %tuple.36), condition=%wide.while_cond, body=%wide.while_body.sunk | while | flops 2 | bytes 132205 | solution.py:25
  215.9 0.5 fusion.51
  216.4 2.0 bitcast_dynamic-update-slice_fusion.2
  218.5 0.5 fusion.51
  219.0 2.0 bitcast_dynamic-update-slice_fusion.2
  221.1 0.5 fusion.51
  221.6 2.0 bitcast_dynamic-update-slice_fusion.2
  223.7 0.5 fusion.51
  224.2 2.0 bitcast_dynamic-update-slice_fusion.2
  226.2 40.1 %custom-call.34 = f32[4,128,128]{1,2,0:T(8,128)S(1)} custom-call(f32[4,128,128]{2,1,0:T(8,128)} %get-tuple-element.10), custom_call_target="InvertDiagBlocksLowerTriangular" | custom-call | tf_op jit(solution)/shard_map/jit(_solve_triangular)/triangular_solve | solution.py:25
  266.4 0.4 fusion.37
  266.8 0.6 convolution_subtract_fusion.1
  267.4 0.4 fusion.36
  267.8 1.0 convolution_subtract_fusion
  268.8 0.4 fusion.35
  269.3 1.5 convolution_subtract_fusion.2
  270.7 0.4 convolution_convert_fusion.1
  271.1 0.8 fusion.21
  272.1 120.0 %all-gather.4.cloned.1.call-done = bf16[8192,512]{0,1:T(8,128)(2,1)} async-done(((bf16[512,512]{0,1:T(8,128)(2,1)}), bf16[8192,512]{0,1:T(8,128)(2,1)}) %all-gather.4.cloned.1.call-update) | async-done | bytes 8388624 | tf_op jit(solution)/shard_map/all_gather | solution.py:28
  392.1 19.7 %fusion = f32[512,8192]{1,0:T(8,128)} fusion(bf16[512,8192]{1,0:T(8,128)(2,1)} %param.6, bf16[8192,512]{0,1:T(8,128)(2,1)} %all-gather.4.cloned.1.call-done, bf16[512,8192]{1,0:T(8,128)(2,1)} %all-gather.6.cloned.1.call-done), kind=kOutput, calls=%fused_computation.5 | convolution fusion | flops 8590196736 | bytes 41943040 | tf_op jit(solution)/shard_map/dot_general | solution.py:34
  411.8 0.3 all-gather.8.cloned.1.call-start
  412.1 344.5 %reduce-scatter.2.cloned.1.call-done = f32[32,8192]{1,0:T(8,128)} async-done(((f32[512,8192]{1,0:T(8,128)}), f32[32,8192]{1,0:T(8,128)}) %reduce-scatter.2.cloned.1.call-update) | async-done | bytes 1048592 | tf_op jit(solution)/shard_map/reduce_scatter | solution.py:33
  756.5 3.0 divide_convert_fusion
  759.6 118.5 %all-gather.8.cloned.1.call-done = bf16[512,8192]{1,0:T(8,128)(2,1)} async-done(((bf16[32,8192]{1,0:T(8,128)(2,1)}), bf16[512,8192]{1,0:T(8,128)(2,1)}) %all-gather.8.cloned.1.call-update) | async-done | bytes 8388624 | tf_op jit(solution)/shard_map/all_gather | solution.py:48
  878.1 11.9 %convolution_multiply_fusion = f32[512,8192]{1,0:T(8,128)} fusion(bf16[512,8192]{1,0:T(8,128)(2,1)} %all-gather.8.cloned.1.call-done, bf16[128,512]{1,0:T(8,128)(2,1)S(1)} %convolution_convert_fusion.1, bf16[128,512]{1,0:T(8,128)(2,1)S(1)} %get-tuple-element.36, bf16[128,512]{1,0:T(8,128)(2,1)S(1)} %get-tuple-element.38, ...), kind=kOutput, calls=%fused_computation.2 | convolution fusion | flops 4301258752 | bytes 25690112 | tf_op jit(solution)/shard_map/dot_general | solution.py:46
  (29 shorter events, 0.7 us)
Async XLA Ops:
  8.0 121.1 %all-reduce.3.cloned.1.call-start = ((), (), s32[]{:S(2)}) async-start(), calls=%async_computation.1 | async-start | bytes 2097152 | tf_op jit(solution)/shard_map/psum | solution.py:23
  12.5 253.8 %copy-start = (f32[512,512]{1,0:T(8,128)S(1)}, f32[512,512]{1,0:T(8,128)}, u32[]{:S(2)}) copy-start(f32[512,512]{1,0:T(8,128)} %param.7) | copy-start | bytes 3145732
  12.5 259.5 %all-gather.6.cloned.1.call-start = ((), (), s32[]{:S(2)}) async-start(), calls=%async_computation.3 | async-start | bytes 12582912 | tf_op jit(solution)/shard_map/all_gather | solution.py:21
  13.1 378.9 %all-gather.4.cloned.1.call-start = ((), (), s32[]{:S(2)}) async-start(), calls=%async_computation.2 | async-start | bytes 8912896 | tf_op jit(solution)/shard_map/all_gather | solution.py:28
  272.0 484.5 %reduce-scatter.2.cloned.1.call-start = ((), (), s32[]{:S(2)}) async-start(), calls=%async_computation.4 | async-start | bytes 17825792 | tf_op jit(solution)/shard_map/reduce_scatter | solution.py:33
  411.8 344.8 %copy-start.1 = (f32[32,8192]{1,0:T(8,128)S(1)}, f32[32,8192]{1,0:T(8,128)}, u32[]{:S(2)}) copy-start(f32[32,8192]{1,0:T(8,128)} %param.9) | copy-start | bytes 3145732
  411.8 344.8 %copy-start.2 = (f32[32,8192]{1,0:T(8,128)S(1)}, f32[32,8192]{1,0:T(8,128)}, u32[]{:S(2)}) copy-start(f32[32,8192]{1,0:T(8,128)} %param.8) | copy-start | bytes 3145732
  411.8 466.3 %all-gather.8.cloned.1.call-start = ((), (), s32[]{:S(2)}) async-start(), calls=%async_computation.5 | async-start | bytes 8912896 | tf_op jit(solution)/shard_map/all_gather | solution.py:48
Sparse Core Ops, SparseCore 0:
  14.7 114.4 all-reduce.2
  411.9 344.5 reduce-scatter.1
Sparse Core Ops, SparseCore 1:
  14.6 22.4 all-gather.5
  272.1 119.9 all-gather.3
  759.7 118.3 all-gather.7
where the time goes:
time: 908 us; the launch traced here: 898 us
  waiting for transfers between devices  699 us (77%)
  other arithmetic  124 us (14%)
  matrix products  42.7 us (5%)
  between operations  18.7 us (2%)
  local copies, waits for them, and re-layouts  12.1 us (1%)
    reduce_scatter x1, waiting for transfers between devices, local(): lax.psum_scatter(jnp.dot(columns.T, out_grads, preferred_element_type=jnp...  344 us
    all_gather x1, waiting for transfers between devices, local(): basis_full = lax.all_gather(own_rows, 'dp', axis=0, tiled=True)  120 us
    all_gather x1, waiting for transfers between devices, local(): lax.all_gather(direction, 'dp', axis=0, tiled=True)  118 us
    psum x1, waiting for transfers between devices, local(): sketch_gram = lax.psum(local_gram, 'dp')  116 us
    another operation x14, other arithmetic, local(): cholesky_factor = jnp.linalg.cholesky(sketch_gram)  78.7 us
    another operation x3, other arithmetic, local(): jax.scipy.linalg.solve_triangular(cholesky_factor, sketch.T, lower=True)  40.4 us
    dot_general x1, matrix products, local(): jnp.dot(columns.T, out_grads, preferred_element_type=jnp.float32)  19.7 us
  transfers between devices with their start and end apart: 5, of which 4 were waited for; matrix products, arithmetic and copies ran while one was open for 16% of the time, Pallas kernels for 0%

commit v1 on v0

v1 whole, which is shorter than its diff:
```python
import functools
import itertools
import math

import jax
import jax.numpy as jnp
from jax import lax
from jax.experimental import pallas as pl
from jax.experimental.pallas import tpu as pltpu
from jax.sharding import PartitionSpec as P

BETA_ONE = 0.9
BETA_TWO = 0.999
CORRECT_ONE = 0.9999999993
CORRECT_TWO = 0.18135117
EPSILON = 1e-08

HIGHEST = lax.Precision.HIGHEST
F32 = jnp.float32
BF16 = jnp.bfloat16
BLOCK = 128
PIVOTS = 8
VMEM_LIMIT = 40 << 20

GROUPS = ((2, (2, 1, 0)), (2, (1, 2, 0)), (2, (2, 1, 0)), (2, (1, 2, 0)))


def mesh_dims(devices):
    if devices == 16:
        return (4, 2, 2)
    if devices == 64:
        return (4, 4, 4)
    return (devices, 1, 1)


def shift_pairs(dims, shift):
    pairs = []
    for place in itertools.product(*(range(size) for size in dims)):
        target = [(at + by) % size for at, by, size in zip(place, shift, dims)]
        pairs.append((flat(place, dims), flat(target, dims)))
    return pairs


def flat(place, dims):
    index = 0
    for at, size in zip(place, dims):
        index = index * size + at
    return index


def send(value, dims, shift):
    return lax.ppermute(value, "dp", shift_pairs(dims, shift))


def unit(axis, by):
    return tuple(by if i == axis else 0 for i in range(3))


def dot_nn(a, b):
    return lax.dot_general(
        a, b, (((1,), (0,)), ((), ())), precision=HIGHEST, preferred_element_type=F32
    )


def dot_nt(a, b):
    return lax.dot_general(
        a, b, (((1,), (1,)), ((), ())), precision=HIGHEST, preferred_element_type=F32
    )


def inverse_factor(block):
    size = block.shape[0]
    tiles = size // 8
    lane = lax.broadcasted_iota(jnp.int32, (8, size), 1)
    sub = lax.broadcasted_iota(jnp.int32, (8, size), 0)
    spread = lambda value: jnp.broadcast_to(value, (8, size))
    work = [block[8 * i : 8 * i + 8, :] for i in range(tiles)]
    scale = [jnp.zeros((8, size), F32) for _ in range(tiles)]
    for base in range(0, size, PIVOTS):
        first = base // 8
        cols = {
            (i, k): spread(work[i][:, base + k : base + k + 1])
            for i in range(first, tiles)
            for k in range(PIVOTS)
        }
        for k in range(PIVOTS):
            j = base + k
            r, q = j % 8, j // 8
            pivot = spread(cols[q, k][r : r + 1, :])
            recip = 1.0 / pivot
            row = jnp.where(lane == j, 1.0, spread(work[q][r : r + 1, :]))
            later = {m: spread(cols[q, m][r : r + 1, :]) for m in range(k + 1, PIVOTS)}
            scale[q] = jnp.where(sub == r, pivot, scale[q])
            for i in range(q, tiles):
                ratio = cols[i, k] * recip
                cleared = lane == j
                if i == q:
                    ratio = jnp.where(sub > r, ratio, 0.0)
                    cleared = cleared & (sub > r)
                for m in range(k + 1, PIVOTS):
                    cols[i, m] = cols[i, m] - ratio * later[m]
                work[i] = jnp.where(cleared, 0.0, work[i]) - ratio * row
    out = []
    for i in range(tiles):
        at = sub + 8 * i
        lower = jnp.where(lane == at, 1.0, jnp.where(lane < at, work[i], 0.0))
        out.append(lower * lax.rsqrt(scale[i]))
    return jnp.concatenate(out, axis=0)


def lower_blocks(size):
    return [(i, j) for i in range(size // BLOCK) for j in range(i + 1)]


def factor_kernel(blocks, packed_ref, out_ref, work_ref):
    size = out_ref.shape[0]
    work_ref[...] = jnp.zeros_like(work_ref)
    for at, (i, j) in enumerate(blocks):
        work_ref[i * BLOCK : (i + 1) * BLOCK, j * BLOCK : (j + 1) * BLOCK] = packed_ref[
            at * BLOCK : (at + 1) * BLOCK, :
        ]
    out_ref[...] = jnp.where(
        lax.broadcasted_iota(jnp.int32, (size, size), 0)
        == lax.broadcasted_iota(jnp.int32, (size, size), 1),
        1.0,
        0.0,
    )

    def step(at, carry):
        base = pl.multiple_of(at * BLOCK, BLOCK)
        inverse = inverse_factor(work_ref[pl.ds(base, BLOCK), pl.ds(base, BLOCK)])
        rows = dot_nn(inverse, out_ref[pl.ds(base, BLOCK), :])
        out_ref[pl.ds(base, BLOCK), :] = rows

        @pl.when(at < size // BLOCK - 1)
        def _():
            panel = dot_nt(work_ref[:, pl.ds(base, BLOCK)], inverse)
            below = lax.broadcasted_iota(jnp.int32, (size, BLOCK), 0) >= base + BLOCK
            panel = jnp.where(below, panel, 0.0)
            work_ref[...] -= dot_nt(panel, panel)
            out_ref[...] -= dot_nn(panel, rows)

        return carry

    lax.fori_loop(0, size // BLOCK, step, 0)


def inverse_of_factor(packed, blocks, size):
    return pl.pallas_call(
        functools.partial(factor_kernel, blocks),
        out_shape=jax.ShapeDtypeStruct((size, size), F32),
        in_specs=[pl.BlockSpec(memory_space=pltpu.VMEM)],
        out_specs=pl.BlockSpec(memory_space=pltpu.VMEM),
        scratch_shapes=[pltpu.VMEM((size, size), F32)],
        compiler_params=pltpu.CompilerParams(vmem_limit_bytes=VMEM_LIMIT),
        name="inverse_factor",
    )(packed)


def summed_gram(sketch, dims, own, core):
    size = sketch.shape[1]
    blocks = lower_blocks(size)
    half = len(blocks) // 2
    gram = jnp.dot(sketch.T, sketch, precision=HIGHEST, preferred_element_type=F32)
    tiles = [
        gram[i * BLOCK : (i + 1) * BLOCK, j * BLOCK : (j + 1) * BLOCK] for i, j in blocks
    ]
    mine = jnp.where(
        core == 0, jnp.concatenate(tiles[:half]), jnp.concatenate(tiles[half:])
    )
    plane = dims[1] * dims[2]
    share = mine.shape[0] // plane
    at_of = lambda a, b: ((own[1] + a) % dims[1] * dims[2] + (own[2] + b) % dims[2]) * share
    shifts = list(itertools.product(range(dims[1]), range(dims[2])))
    part = lambda a, b: lax.dynamic_slice_in_dim(mine, at_of(a, b), share, 0)
    total = part(0, 0)
    arrived = [send(part(a, b), dims, (0, a, b)) for a, b in shifts[1:]]
    for piece in arrived:
        total = total + piece
    arrived = [send(total, dims, (by, 0, 0)) for by in range(1, dims[0])]
    places = jnp.stack([total] + arrived)
    order = [(own[0] - z) % dims[0] for z in range(dims[0])]
    total = functools.reduce(
        jnp.add, [lax.dynamic_index_in_dim(places, at, 0, keepdims=False) for at in order]
    )
    whole = lax.dynamic_update_slice_in_dim(
        jnp.zeros_like(mine), total, at_of(0, 0), 0
    )
    arrived = [send(total, dims, (0, -a, -b)) for a, b in shifts[1:]]
    for (a, b), piece in zip(shifts[1:], arrived):
        whole = lax.dynamic_update_slice_in_dim(whole, piece, at_of(a, b), 0)
    other = lax.ppermute(whole, "tensor", [(0, 1), (1, 0)])
    return (
        jnp.where(core == 0, jnp.concatenate([whole, other]), jnp.concatenate([other, whole])),
        blocks,
    )


def update_kernel(scale, count, *refs):
    weight_ref, pieces, out_ref = refs[0], refs[1 : 1 + count], refs[-1]
    rows = pieces[0].shape[0]
    total = None
    for at, piece in enumerate(pieces):
        term = jnp.dot(
            weight_ref[:, at * rows : (at + 1) * rows],
            piece[...],
            preferred_element_type=F32,
        )
        total = term if total is None else total + term
    out_ref[...] = scale * total


def update_columns(weight, pieces, previous, start, width, scale):
    tall, rank = weight.shape
    rows, cols = pieces[0].shape
    wide = min(1024, cols)
    first = start // wide
    in_specs = [pl.BlockSpec((tall, rank), lambda j: (0, 0))]
    in_specs += [pl.BlockSpec((rows, wide), lambda j: (0, j)) for _ in pieces]
    operands = [weight, *pieces]
    aliases = {}
    if previous is not None:
        aliases = {len(operands): 0}
        in_specs.append(pl.BlockSpec(memory_space=pl.ANY))
        operands.append(previous)
    return pl.pallas_call(
        functools.partial(update_kernel, scale, len(pieces)),
        grid=(cols // wide,),
        out_shape=jax.ShapeDtypeStruct((tall, width), F32),
        in_specs=in_specs,
        out_specs=pl.BlockSpec((tall, wide), lambda j: (0, first + j)),
        input_output_aliases=aliases,
        compiler_params=pltpu.CompilerParams(vmem_limit_bytes=VMEM_LIMIT),
        name="update_columns",
    )(*operands)


def selection(dims, own, order, rank, core):
    piece = rank // math.prod(dims)
    index = jnp.zeros((), jnp.int32)
    strides = (dims[1] * dims[2], dims[2], 1)
    for axis in order:
        places = (own[axis] + jnp.arange(dims[axis], dtype=jnp.int32)) % dims[axis]
        index = index[..., None] + places * strides[axis]
    index = index[..., None] * piece + jnp.arange(piece, dtype=jnp.int32)
    index = index.reshape(rank)
    return index


def one_hot(index, rank):
    return (index[:, None] == jnp.arange(rank, dtype=jnp.int32)[None, :]).astype(BF16)


def local(dims, activations, out_grads, sketch, first_moment, second_moment):
    dp = lax.axis_index("dp")
    core = lax.axis_index("tensor")
    own = (dp // (dims[1] * dims[2]), dp // dims[2] % dims[1], dp % dims[2])
    rank = sketch.shape[1]
    width = out_grads.shape[1]
    depth = activations.shape[1] * 2

    features = lax.all_gather(activations, "tensor", axis=1, tiled=True)
    half = lax.dynamic_slice_in_dim(sketch, core * (rank // 2), rank // 2, 1).astype(BF16)
    sketch_half = lax.all_gather(half, "dp", axis=0, tiled=True)
    mixed_half = jnp.dot(features, sketch_half, preferred_element_type=F32)
    mixed_other = lax.ppermute(mixed_half, "tensor", [(0, 1), (1, 0)])
    mixed = jnp.where(
        core == 0,
        jnp.concatenate([mixed_half, mixed_other], axis=1),
        jnp.concatenate([mixed_other, mixed_half], axis=1),
    )

    packed, blocks = summed_gram(sketch, dims, own, core)
    inverse = inverse_of_factor(packed, blocks, rank)
    own_rows = dot_nt(sketch, inverse).astype(BF16)
    projected = dot_nt(inverse, mixed).astype(BF16)

    selections = {}
    for _, order in GROUPS:
        if order not in selections:
            pick = one_hot(selection(dims, own, order, rank, core), rank)
            selections[order] = (
                jnp.dot(pick, projected, preferred_element_type=F32).astype(BF16),
                lax.dot_general(
                    own_rows, pick, (((1,), (1,)), ((), ())), preferred_element_type=F32
                ).astype(BF16),
            )

    update_scale = math.sqrt(depth / rank)
    eighth = width // 8
    start = 0
    states = []
    for share, order in GROUPS:
        cols = share * eighth
        grads = out_grads[:, start : start + cols]
        columns = selections[order][0]
        size = rank // dims[order[0]]
        term = lambda by: jnp.dot(
            columns[by * size : (by + 1) * size], grads, preferred_element_type=F32
        )
        axis = order[0]
        arrived = [
            send(term(by).astype(BF16), dims, unit(axis, by)) for by in range(1, dims[axis])
        ]
        total = term(0)
        for piece in arrived:
            total = total + piece.astype(F32)
        for axis in order[1:]:
            size = size // dims[axis]
            arrived = [
                send(total[by * size : (by + 1) * size].astype(BF16), dims, unit(axis, by))
                for by in range(1, dims[axis])
            ]
            total = total[:size]
            for piece in arrived:
                total = total + piece.astype(F32)
        states.append((start, cols, order, total))
        start += cols

    first_parts, second_parts = [], []
    update = None
    for start, cols, order, grad_low in states:
        first = BETA_ONE * first_moment[:, start : start + cols] + (1.0 - BETA_ONE) * grad_low
        second = (
            BETA_TWO * second_moment[:, start : start + cols]
            + (1.0 - BETA_TWO) * grad_low * grad_low
        )
        direction = (
            first / CORRECT_ONE / (jnp.sqrt(second / CORRECT_TWO) + EPSILON)
        ).astype(BF16)
        first_parts.append(first)
        second_parts.append(second)
        for axis in order[:0:-1]:
            direction = jnp.concatenate(
                [direction]
                + [send(direction, dims, unit(axis, -by)) for by in range(1, dims[axis])]
            )
        axis = order[0]
        pieces = [direction] + [
            send(direction, dims, unit(axis, -by)) for by in range(1, dims[axis])
        ]
        update = update_columns(
            selections[order][1], pieces, update, start, width, update_scale
        )
    return (
        update,
        jnp.concatenate(first_parts, axis=1),
        jnp.concatenate(second_parts, axis=1),
    )


def solution(mesh):
    dims = mesh_dims(mesh.shape["dp"])
    return jax.shard_map(
        functools.partial(local, dims),
        mesh=mesh,
        in_specs=(
            P("dp", "tensor"),
            P("dp", "tensor"),
            P("dp", None),
            P("dp", "tensor"),
            P("dp", "tensor"),
        ),
        out_specs=(P("dp", "tensor"), P("dp", "tensor"), P("dp", "tensor")),
        check_vma=False,
    )
```

time: 908 us -> 375 us (0.41); the launches traced: 898 us -> 374 us
  waiting for transfers between devices: 699 us -> 191 us
  other arithmetic: 124 us -> 4.25 us
  starting transfers between devices: 0.42 us -> 101 us
  Pallas kernels: 0 us -> 36.6 us
  matrix products: 42.7 us -> 24.1 us
  local copies, waits for them, and re-layouts: 12.1 us -> 2.9 us
    reduce_scatter x1 -> x0, waiting for transfers between devices: 344 us -> none  [local(): lax.psum_scatter(jnp.dot(columns.T, out_grads, preferred_element_type=jnp...]
    all_gather x2 -> x1, waiting for transfers between devices: 238 us -> 23.7 us  [local(): sketch_half = lax.all_gather(half, 'dp', axis=0, tiled=True)]
    ppermute x0 -> x51, waiting for transfers between devices: none -> 147 us  [the longest x49 145 us: send(): return lax.ppermute(value, 'dp', shift_pairs(dims, shift))]
    another operation x17 -> x5, other arithmetic: 119 us -> 0.63 us  [the longest x14 78.7 us: local(): cholesky_factor = jnp.linalg.cholesky(sketch_gram)]
    psum x1 -> x0, waiting for transfers between devices: 116 us -> none  [local(): sketch_gram = lax.psum(local_gram, 'dp')]
    ppermute x0 -> x51, starting transfers between devices: none -> 101 us  [the longest x49 100 us: send(): return lax.ppermute(value, 'dp', shift_pairs(dims, shift))]
    pallas_call x0 -> x5, Pallas kernels: none -> 36.6 us  [the longest x1 25 us: inverse_of_factor(): pl.pallas_call(functools.partial(factor_kernel, blocks), out_shape=jax.Sh...]
    all_gather x1, waiting for transfers between devices: 0.03 us -> 20 us  [local(): features = lax.all_gather(activations, 'tensor', axis=1, tiled=True)]
  transfers between devices with their start and end apart: 5 -> 53, of which waited for: 4 -> 24; matrix products, arithmetic and copies ran while one was open for 16% -> 4% of each run, Pallas kernels for 0% -> 9%
where the time goes in v1:
time: 375 us; the launch traced here: 374 us
  waiting for transfers between devices  191 us (51%)
  starting transfers between devices  101 us (27%)
  Pallas kernels  36.6 us (10%)
  matrix products  24.1 us (6%)
  between operations  14.9 us (4%)
  other arithmetic  4.25 us (1%)
    ppermute x49, waiting for transfers between devices, send(): return lax.ppermute(value, 'dp', shift_pairs(dims, shift))  145 us
    ppermute x49, starting transfers between devices, send(): return lax.ppermute(value, 'dp', shift_pairs(dims, shift))  100 us
    pallas_call x1, Pallas kernels, inverse_of_factor(): pl.pallas_call(functools.partial(factor_kernel, blocks), out_shape=jax.Sh...  25 us
    all_gather x1, waiting for transfers between devices, local(): sketch_half = lax.all_gather(half, 'dp', axis=0, tiled=True)  23.7 us
    all_gather x1, waiting for transfers between devices, local(): features = lax.all_gather(activations, 'tensor', axis=1, tiled=True)  20 us
    pallas_call x4, Pallas kernels, update_columns(): pl.pallas_call(functools.partial(update_kernel, scale, len(pieces)), grid...  11.7 us
    dot_general x8, matrix products, local(): jnp.dot(columns[by * size:(by + 1) * size], grads, preferred_element_type...  9.28 us
  transfers between devices with their start and end apart: 53, of which 24 were waited for; matrix products, arithmetic and copies ran while one was open for 4% of the time, Pallas kernels for 9%

profile of v1, /device:TPU:0, one launch (start us, length us, event | category | flops | bytes accessed | tf_op | source)
XLA Modules:
  0.0 374.5 jit_solution(10244102540571621053)
XLA Ops:
  10.0 1.9 fusion.69
  12.1 3.0 collective-permute-start
  17.8 2.6 collective-permute-done.1
  22.0 1.6 collective-permute-start.3
  23.6 2.6 collective-permute-start.4
  27.6 2.9 collective-permute-done.3
  30.5 4.0 %collective-permute-done.4 = f32[160,128]{1,0:T(8,128)S(1)} collective-permute-done((f32[160,128]{1,0:T(8,128)S(1)}, f32[160,128]{1,0:T(8,128)S(1)}, u32[]{:S(2)}, u32[]{:S(2)}) %collective-permute-start.4) | collective-permute-done | bytes 81952 | tf_op jit(solution)/shard_map/ppermute | solution.py:52
  36.5 1.7 collective-permute-start.8
  40.0 1.9 collective-permute-done.8
  43.7 25.0 %inverse_factor.1 = f32[512,512]{1,0:T(8,128)S(1)} custom-call(f32[1280,128]{1,0:T(8,128)S(1)} %maximum_select_fusion.2.packed_ref), custom_call_target="tpu_custom_call" | custom-call | tf_op jit(solution)/shard_map/inverse_factor/pallas_call | solution.py:149
  68.6 23.7 %all-gather.3.cloned.1.call-done = bf16[8192,256]{1,0:T(8,128)(2,1)} async-done(((bf16[512,256]{1,0:T(8,128)(2,1)}), bf16[8192,256]{1,0:T(8,128)(2,1)}) %all-gather.3.cloned.1.call-update) | async-done | bytes 4194320 | tf_op jit(solution)/shard_map/all_gather | solution.py:264
  92.4 20.0 %all-gather.5.cloned.1.call-done = bf16[512,8192]{1,0:T(8,128)(2,1)} async-done(((bf16[512,4096]{1,0:T(8,128)(2,1)}), bf16[512,8192]{1,0:T(8,128)(2,1)}) %all-gather.5.cloned.1.call-update) | async-done | bytes 8388624 | tf_op jit(solution)/shard_map/all_gather | solution.py:262
  112.4 7.0 %convolution_bitcast_fusion = f32[512,256]{0,1:T(8,128)S(1)} fusion(bf16[8192,256]{1,0:T(8,128)(2,1)} %all-gather.3.cloned.1.call-done, bf16[512,8192]{1,0:T(8,128)(2,1)} %all-gather.5.cloned.1.call-done), kind=kOutput, calls=%fused_computation.26 | convolution fusion | flops 2147483648 | bytes 13107200 | tf_op jit(solution)/shard_map/dot_general | solution.py:265
  119.7 1.9 convolution_convert_fusion.9
  122.2 1.9 convolution_convert_fusion.8
  124.6 2.5 convolution_convert_fusion.1
  127.1 2.3 convolution_convert_fusion.3
  129.4 1.9 collective-permute-start.31
  132.7 1.9 collective-permute-start.21
  136.2 19.2 %collective-permute-done.31 = bf16[256,2048]{1,0:T(8,128)(2,1)S(1)} collective-permute-done((bf16[256,2048]{1,0:T(8,128)(2,1)S(1)}, bf16[256,2048]{1,0:T(8,128)(2,1)S(1)}, u32[]{:S(2)}, u32[]{:S(2)}) %collective-permute-start.31) | collective-permute-done | bytes 1048608 | tf_op jit(solution)/shard_map/ppermute | solution.py:52
  156.2 1.9 collective-permute-start.32
  158.1 19.2 %collective-permute-done.11 = bf16[256,2048]{1,0:T(8,128)(2,1)S(1)} collective-permute-done((bf16[256,2048]{1,0:T(8,128)(2,1)S(1)}, bf16[256,2048]{1,0:T(8,128)(2,1)S(1)}, u32[]{:S(2)}, u32[]{:S(2)}) %collective-permute-start.11) | collective-permute-done | bytes 1048608 | tf_op jit(solution)/shard_map/ppermute | solution.py:52
  178.3 1.8 collective-permute-start.12
  184.0 18.6 %collective-permute-done.12 = bf16[128,2048]{1,0:T(8,128)(2,1)S(1)} collective-permute-done((bf16[128,2048]{1,0:T(8,128)(2,1)S(1)}, bf16[128,2048]{1,0:T(8,128)(2,1)S(1)}, u32[]{:S(2)}, u32[]{:S(2)}) %collective-permute-start.12) | collective-permute-done | bytes 524320 | tf_op jit(solution)/shard_map/ppermute | solution.py:52
  202.8 1.7 collective-permute-start.13
  204.5 2.4 collective-permute-start.14
  211.2 2.9 collective-permute-start.25
  214.1 4.2 %collective-permute-done.14 = bf16[32,2048]{1,0:T(8,128)(2,1)S(1)} collective-permute-done((bf16[32,2048]{1,0:T(8,128)(2,1)S(1)}, bf16[32,2048]{1,0:T(8,128)(2,1)S(1)}, u32[]{:S(2)}, u32[]{:S(2)}) %collective-permute-start.14) | collective-permute-done | bytes 131104 | tf_op jit(solution)/shard_map/ppermute | solution.py:52
  218.3 5.3 %collective-permute-start.43 = (bf16[32,2048]{1,0:T(8,128)(2,1)S(1)}, bf16[32,2048]{1,0:T(8,128)(2,1)S(1)}, u32[]{:S(2)}, u32[]{:S(2)}) collective-permute-start(bf16[32,2048]{1,0:T(8,128)(2,1)S(1)} %get-tuple-element.41), channel_id=1, source_target_pairs={{0,8},{2,10},{4,12},{6,14},{8,16},{10,18},{12,20},{14,22},{16,24},... | collective-permute-start | bytes 393224 | tf_op jit(solution)/shard_map/ppermute | solution.py:52
  223.6 3.8 %collective-permute-start.44 = (bf16[32,2048]{1,0:T(8,128)(2,1)S(1)}, bf16[32,2048]{1,0:T(8,128)(2,1)S(1)}, u32[]{:S(2)}, u32[]{:S(2)}) collective-permute-start(bf16[32,2048]{1,0:T(8,128)(2,1)S(1)} %get-tuple-element.43), channel_id=1, source_target_pairs={{0,16},{2,18},{4,20},{6,22},{8,24},{10,26},{12,28},{14,30},{16,0},... | collective-permute-start | bytes 393224 | tf_op jit(solution)/shard_map/ppermute | solution.py:52
  227.5 7.7 %collective-permute-start.33 = (bf16[32,2048]{1,0:T(8,128)(2,1)S(1)}, bf16[32,2048]{1,0:T(8,128)(2,1)S(1)}, u32[]{:S(2)}, u32[]{:S(2)}) collective-permute-start(bf16[32,2048]{1,0:T(8,128)(2,1)S(1)} %get-tuple-element.44), channel_id=1, source_target_pairs={{0,8},{2,10},{4,12},{6,14},{8,16},{10,18},{12,20},{14,22},{16,24},... | collective-permute-start | bytes 393224 | tf_op jit(solution)/shard_map/ppermute | solution.py:52
  235.2 3.4 collective-permute-start.34
  239.4 12.0 %collective-permute-start.46 = (bf16[32,2048]{1,0:T(8,128)(2,1)S(1)}, bf16[32,2048]{1,0:T(8,128)(2,1)S(1)}, u32[]{:S(2)}, u32[]{:S(2)}) collective-permute-start(bf16[32,2048]{1,0:T(8,128)(2,1)S(1)} %get-tuple-element.4), channel_id=1, source_target_pairs={{0,24},{2,26},{4,28},{6,30},{8,0},{10,2},{12,4},{14,6},{16,8},{18,... | collective-permute-start | bytes 393224 | tf_op jit(solution)/shard_map/ppermute | solution.py:52
  252.3 11.3 %collective-permute-start.36 = (bf16[32,2048]{1,0:T(8,128)(2,1)S(1)}, bf16[32,2048]{1,0:T(8,128)(2,1)S(1)}, u32[]{:S(2)}, u32[]{:S(2)}) collective-permute-start(bf16[32,2048]{1,0:T(8,128)(2,1)S(1)} %get-tuple-element.10), channel_id=1, source_target_pairs={{0,24},{2,26},{4,28},{6,30},{8,0},{10,2},{12,4},{14,6},{16,8},{18,... | collective-permute-start | bytes 393224 | tf_op jit(solution)/shard_map/ppermute | solution.py:52
  265.3 2.1 collective-permute-start.26
  268.7 3.8 %collective-permute-start.28 = (bf16[32,2048]{1,0:T(8,128)(2,1)S(1)}, bf16[32,2048]{1,0:T(8,128)(2,1)S(1)}, u32[]{:S(2)}, u32[]{:S(2)}) collective-permute-start(bf16[32,2048]{1,0:T(8,128)(2,1)S(1)} %get-tuple-element.30), channel_id=1, source_target_pairs={{0,8},{2,10},{4,12},{6,14},{8,16},{10,18},{12,20},{14,22},{16,24},... | collective-permute-start | bytes 393224 | tf_op jit(solution)/shard_map/ppermute | solution.py:52
  272.5 6.9 %collective-permute-done.37 = bf16[32,2048]{1,0:T(8,128)(2,1)S(1)} collective-permute-done((bf16[32,2048]{1,0:T(8,128)(2,1)S(1)}, bf16[32,2048]{1,0:T(8,128)(2,1)S(1)}, u32[]{:S(2)}, u32[]{:S(2)}) %collective-permute-start.37) | collective-permute-done | bytes 131104 | tf_op jit(solution)/shard_map/ppermute | solution.py:52
  279.4 2.8 collective-permute-start.17
  282.8 7.9 %collective-permute-done.27 = bf16[32,2048]{1,0:T(8,128)(2,1)S(1)} collective-permute-done((bf16[32,2048]{1,0:T(8,128)(2,1)S(1)}, bf16[32,2048]{1,0:T(8,128)(2,1)S(1)}, u32[]{:S(2)}, u32[]{:S(2)}) %collective-permute-start.27) | collective-permute-done | bytes 131104 | tf_op jit(solution)/shard_map/ppermute | solution.py:52
  294.3 1.9 collective-permute-done.17
  298.0 7.5 %collective-permute-done.49 = bf16[128,2048]{1,0:T(8,128)(2,1)S(1)} collective-permute-done((bf16[128,2048]{1,0:T(8,128)(2,1)S(1)}, bf16[128,2048]{1,0:T(8,128)(2,1)S(1)}, u32[]{:S(2)}, u32[]{:S(2)}) %collective-permute-start.49) | collective-permute-done | bytes 524320 | tf_op jit(solution)/shard_map/ppermute | solution.py:52
  308.6 8.1 %collective-permute-done.29 = bf16[128,2048]{1,0:T(8,128)(2,1)S(1)} collective-permute-done((bf16[128,2048]{1,0:T(8,128)(2,1)S(1)}, bf16[128,2048]{1,0:T(8,128)(2,1)S(1)}, u32[]{:S(2)}, u32[]{:S(2)}) %collective-permute-start.29) | collective-permute-done | bytes 524320 | tf_op jit(solution)/shard_map/ppermute | solution.py:52
  321.9 18.7 %collective-permute-done.50.refs_2_ = bf16[256,2048]{1,0:T(8,128)(2,1)S(1)} collective-permute-done((bf16[256,2048]{1,0:T(8,128)(2,1)S(1)}, bf16[256,2048]{1,0:T(8,128)(2,1)S(1)}, u32[]{:S(2)}, u32[]{:S(2)}) %collective-permute-start.50) | collective-permute-done | bytes 1048608 | tf_op jit(solution)/shard_map/ppermute | solution.py:52
  340.7 2.9 update_columns.4.refs_3_
  343.6 2.9 update_columns.5.refs_3_
  346.5 15.3 %collective-permute-done.30.refs_2_ = bf16[256,2048]{1,0:T(8,128)(2,1)S(1)} collective-permute-done((bf16[256,2048]{1,0:T(8,128)(2,1)S(1)}, bf16[256,2048]{1,0:T(8,128)(2,1)S(1)}, u32[]{:S(2)}, u32[]{:S(2)}) %collective-permute-start.30) | collective-permute-done | bytes 1048608 | tf_op jit(solution)/shard_map/ppermute | solution.py:52
  361.8 2.9 update_columns.6.refs_3_
  364.7 2.9 update_columns.7
  (155 shorter events, 47.1 us)
Async XLA Ops:
  7.2 85.2 %all-gather.3.cloned.1.call-start = ((), (), s32[]{:S(2)}) async-start(), calls=%async_computation | async-start | bytes 4456448 | tf_op jit(solution)/shard_map/all_gather | solution.py:264
  9.2 103.2 %all-gather.5.cloned.1.call-start = ((), (), s32[]{:S(2)}) async-start(), calls=%async_computation.1 | async-start | bytes 12582912 | tf_op jit(solution)/shard_map/all_gather | solution.py:262
  12.1 5.7 %collective-permute-start = (f32[160,128]{1,0:T(8,128)S(1)}, f32[160,128]{1,0:T(8,128)S(1)}, u32[]{:S(2)}, u32[]{:S(2)}) collective-permute-start(f32[160,128]{1,0:T(8,128)S(1)} %get-tuple-element.53), channel_id=1, source_target_pairs={{0,2},{2,0},{4,6},{6,4},{8,10},{10,8},{12,14},{14,12},{16,18},{18,... | collective-permute-start | bytes 245768 | tf_op jit(solution)/shard_map/ppermute | solution.py:52
  16.7 5.3 %collective-permute-start.2 = (f32[160,128]{1,0:T(8,128)S(1)}, f32[160,128]{1,0:T(8,128)S(1)}, u32[]{:S(2)}, u32[]{:S(2)}) collective-permute-start(f32[160,128]{1,0:T(8,128)S(1)} %get-tuple-element.54), channel_id=1, source_target_pairs={{0,6},{2,4},{4,2},{6,0},{8,14},{10,12},{12,10},{14,8},{16,22},{18,... | collective-permute-start | bytes 245768 | tf_op jit(solution)/shard_map/ppermute | solution.py:52
  22.0 8.4 %collective-permute-start.3 = (f32[160,128]{1,0:T(8,128)S(1)}, f32[160,128]{1,0:T(8,128)S(1)}, u32[]{:S(2)}, u32[]{:S(2)}) collective-permute-start(f32[160,128]{1,0:T(8,128)S(1)} %add_add_fusion), channel_id=1, source_target_pairs={{0,8},{2,10},{4,12},{6,14},{8,16},{10,18},{12,20},{14,22},{16,24},... | collective-permute-start | bytes 245768 | tf_op jit(solution)/shard_map/ppermute | solution.py:52
  23.6 10.9 %collective-permute-start.4 = (f32[160,128]{1,0:T(8,128)S(1)}, f32[160,128]{1,0:T(8,128)S(1)}, u32[]{:S(2)}, u32[]{:S(2)}) collective-permute-start(f32[160,128]{1,0:T(8,128)S(1)} %add_add_fusion), channel_id=1, source_target_pairs={{0,16},{2,18},{4,20},{6,22},{8,24},{10,26},{12,28},{14,30},{16,0},... | collective-permute-start | bytes 245768 | tf_op jit(solution)/shard_map/ppermute | solution.py:52
  26.2 8.3 %collective-permute-start.5 = (f32[160,128]{1,0:T(8,128)S(1)}, f32[160,128]{1,0:T(8,128)S(1)}, u32[]{:S(2)}, u32[]{:S(2)}) collective-permute-start(f32[160,128]{1,0:T(8,128)S(1)} %add_add_fusion), channel_id=1, source_target_pairs={{0,24},{2,26},{4,28},{6,30},{8,0},{10,2},{12,4},{14,6},{16,8},{18,... | collective-permute-start | bytes 245768 | tf_op jit(solution)/shard_map/ppermute | solution.py:52
  36.5 5.3 %collective-permute-start.8 = (f32[160,128]{1,0:T(8,128)S(1)}, f32[160,128]{1,0:T(8,128)S(1)}, u32[]{:S(2)}, u32[]{:S(2)}) collective-permute-start(f32[160,128]{1,0:T(8,128)S(1)} %get-tuple-element.28), channel_id=1, source_target_pairs={{0,6},{2,4},{4,2},{6,0},{8,14},{10,12},{12,10},{14,8},{16,22},{18,... | collective-permute-start | bytes 245768 | tf_op jit(solution)/shard_map/ppermute | solution.py:52
  129.4 26.0 %collective-permute-start.31 = (bf16[256,2048]{1,0:T(8,128)(2,1)S(1)}, bf16[256,2048]{1,0:T(8,128)(2,1)S(1)}, u32[]{:S(2)}, u32[]{:S(2)}) collective-permute-start(bf16[256,2048]{1,0:T(8,128)(2,1)S(1)} %convolution_convert_fusion.1), channel_id=1, source_target_pairs={{0,4},{2,6},{4,0},{6,2},{8,12},{10,14},{12,8},{14,10},{16,20},{18,... | collective-permute-start | bytes 3145736 | tf_op jit(solution)/shard_map/ppermute | solution.py:52
  131.3 46.0 %collective-permute-start.11 = (bf16[256,2048]{1,0:T(8,128)(2,1)S(1)}, bf16[256,2048]{1,0:T(8,128)(2,1)S(1)}, u32[]{:S(2)}, u32[]{:S(2)}) collective-permute-start(bf16[256,2048]{1,0:T(8,128)(2,1)S(1)} %convolution_convert_fusion.3), channel_id=1, source_target_pairs={{0,4},{2,6},{4,0},{6,2},{8,12},{10,14},{12,8},{14,10},{16,20},{18,... | collective-permute-start | bytes 3145736 | tf_op jit(solution)/shard_map/ppermute | solution.py:52
  132.7 47.4 %collective-permute-start.21 = (bf16[256,2048]{1,0:T(8,128)(2,1)S(1)}, bf16[256,2048]{1,0:T(8,128)(2,1)S(1)}, u32[]{:S(2)}, u32[]{:S(2)}) collective-permute-start(bf16[256,2048]{1,0:T(8,128)(2,1)S(1)} %convolution_convert_fusion.2), channel_id=1, source_target_pairs={{0,2},{2,0},{4,6},{6,4},{8,10},{10,8},{12,14},{14,12},{16,18},{18,... | collective-permute-start | bytes 3145736 | tf_op jit(solution)/shard_map/ppermute | solution.py:52
  135.9 46.5 %collective-permute-start.41 = (bf16[256,2048]{1,0:T(8,128)(2,1)S(1)}, bf16[256,2048]{1,0:T(8,128)(2,1)S(1)}, u32[]{:S(2)}, u32[]{:S(2)}) collective-permute-start(bf16[256,2048]{1,0:T(8,128)(2,1)S(1)} %convolution_convert_fusion), channel_id=1, source_target_pairs={{0,2},{2,0},{4,6},{6,4},{8,10},{10,8},{12,14},{14,12},{16,18},{18,... | collective-permute-start | bytes 3145736 | tf_op jit(solution)/shard_map/ppermute | solution.py:52
  156.2 52.3 %collective-permute-start.32 = (bf16[128,2048]{1,0:T(8,128)(2,1)S(1)}, bf16[128,2048]{1,0:T(8,128)(2,1)S(1)}, u32[]{:S(2)}, u32[]{:S(2)}) collective-permute-start(bf16[128,2048]{1,0:T(8,128)(2,1)S(1)} %slice.353), channel_id=1, source_target_pairs={{0,2},{2,0},{4,6},{6,4},{8,10},{10,8},{12,14},{14,12},{16,18},{18,... | collective-permute-start | bytes 1572872 | tf_op jit(solution)/shard_map/ppermute | solution.py:52
  178.3 24.3 %collective-permute-start.12 = (bf16[128,2048]{1,0:T(8,128)(2,1)S(1)}, bf16[128,2048]{1,0:T(8,128)(2,1)S(1)}, u32[]{:S(2)}, u32[]{:S(2)}) collective-permute-start(bf16[128,2048]{1,0:T(8,128)(2,1)S(1)} %slice.355), channel_id=1, source_target_pairs={{0,2},{2,0},{4,6},{6,4},{8,10},{10,8},{12,14},{14,12},{16,18},{18,... | collective-permute-start | bytes 1572872 | tf_op jit(solution)/shard_map/ppermute | solution.py:52
  180.9 26.0 %collective-permute-start.22 = (bf16[128,2048]{1,0:T(8,128)(2,1)S(1)}, bf16[128,2048]{1,0:T(8,128)(2,1)S(1)}, u32[]{:S(2)}, u32[]{:S(2)}) collective-permute-start(bf16[128,2048]{1,0:T(8,128)(2,1)S(1)} %slice.354), channel_id=1, source_target_pairs={{0,4},{2,6},{4,0},{6,2},{8,12},{10,14},{12,8},{14,10},{16,20},{18,... | collective-permute-start | bytes 1572872 | tf_op jit(solution)/shard_map/ppermute | solution.py:52
  183.2 26.1 %collective-permute-start.42 = (bf16[128,2048]{1,0:T(8,128)(2,1)S(1)}, bf16[128,2048]{1,0:T(8,128)(2,1)S(1)}, u32[]{:S(2)}, u32[]{:S(2)}) collective-permute-start(bf16[128,2048]{1,0:T(8,128)(2,1)S(1)} %slice.352), channel_id=1, source_target_pairs={{0,4},{2,6},{4,0},{6,2},{8,12},{10,14},{12,8},{14,10},{16,20},{18,... | collective-permute-start | bytes 1572872 | tf_op jit(solution)/shard_map/ppermute | solution.py:52
  202.8 8.4 %collective-permute-start.13 = (bf16[32,2048]{1,0:T(8,128)(2,1)S(1)}, bf16[32,2048]{1,0:T(8,128)(2,1)S(1)}, u32[]{:S(2)}, u32[]{:S(2)}) collective-permute-start(bf16[32,2048]{1,0:T(8,128)(2,1)S(1)} %get-tuple-element.50), channel_id=1, source_target_pairs={{0,8},{2,10},{4,12},{6,14},{8,16},{10,18},{12,20},{14,22},{16,24},... | collective-permute-start | bytes 393224 | tf_op jit(solution)/shard_map/ppermute | solution.py:52
  204.5 13.8 %collective-permute-start.14 = (bf16[32,2048]{1,0:T(8,128)(2,1)S(1)}, bf16[32,2048]{1,0:T(8,128)(2,1)S(1)}, u32[]{:S(2)}, u32[]{:S(2)}) collective-permute-start(bf16[32,2048]{1,0:T(8,128)(2,1)S(1)} %get-tuple-element.52), channel_id=1, source_target_pairs={{0,16},{2,18},{4,20},{6,22},{8,24},{10,26},{12,28},{14,30},{16,0},... | collective-permute-start | bytes 393224 | tf_op jit(solution)/shard_map/ppermute | solution.py:52
  206.9 16.6 %collective-permute-start.15 = (bf16[32,2048]{1,0:T(8,128)(2,1)S(1)}, bf16[32,2048]{1,0:T(8,128)(2,1)S(1)}, u32[]{:S(2)}, u32[]{:S(2)}) collective-permute-start(bf16[32,2048]{1,0:T(8,128)(2,1)S(1)} %get-tuple-element.51), channel_id=1, source_target_pairs={{0,24},{2,26},{4,28},{6,30},{8,0},{10,2},{12,4},{14,6},{16,8},{18,... | collective-permute-start | bytes 393224 | tf_op jit(solution)/shard_map/ppermute | solution.py:52
  208.6 18.8 %collective-permute-start.23 = (bf16[32,2048]{1,0:T(8,128)(2,1)S(1)}, bf16[32,2048]{1,0:T(8,128)(2,1)S(1)}, u32[]{:S(2)}, u32[]{:S(2)}) collective-permute-start(bf16[32,2048]{1,0:T(8,128)(2,1)S(1)} %get-tuple-element.47), channel_id=1, source_target_pairs={{0,8},{2,10},{4,12},{6,14},{8,16},{10,18},{12,20},{14,22},{16,24},... | collective-permute-start | bytes 393224 | tf_op jit(solution)/shard_map/ppermute | solution.py:52
  209.4 18.1 %collective-permute-start.24 = (bf16[32,2048]{1,0:T(8,128)(2,1)S(1)}, bf16[32,2048]{1,0:T(8,128)(2,1)S(1)}, u32[]{:S(2)}, u32[]{:S(2)}) collective-permute-start(bf16[32,2048]{1,0:T(8,128)(2,1)S(1)} %get-tuple-element.49), channel_id=1, source_target_pairs={{0,16},{2,18},{4,20},{6,22},{8,24},{10,26},{12,28},{14,30},{16,0},... | collective-permute-start | bytes 393224 | tf_op jit(solution)/shard_map/ppermute | solution.py:52
  211.2 24.1 %collective-permute-start.25 = (bf16[32,2048]{1,0:T(8,128)(2,1)S(1)}, bf16[32,2048]{1,0:T(8,128)(2,1)S(1)}, u32[]{:S(2)}, u32[]{:S(2)}) collective-permute-start(bf16[32,2048]{1,0:T(8,128)(2,1)S(1)} %get-tuple-element.48), channel_id=1, source_target_pairs={{0,24},{2,26},{4,28},{6,30},{8,0},{10,2},{12,4},{14,6},{16,8},{18,... | collective-permute-start | bytes 393224 | tf_op jit(solution)/shard_map/ppermute | solution.py:52
  218.3 20.4 %collective-permute-start.43 = (bf16[32,2048]{1,0:T(8,128)(2,1)S(1)}, bf16[32,2048]{1,0:T(8,128)(2,1)S(1)}, u32[]{:S(2)}, u32[]{:S(2)}) collective-permute-start(bf16[32,2048]{1,0:T(8,128)(2,1)S(1)} %get-tuple-element.41), channel_id=1, source_target_pairs={{0,8},{2,10},{4,12},{6,14},{8,16},{10,18},{12,20},{14,22},{16,24},... | collective-permute-start | bytes 393224 | tf_op jit(solution)/shard_map/ppermute | solution.py:52
  223.6 15.1 %collective-permute-start.44 = (bf16[32,2048]{1,0:T(8,128)(2,1)S(1)}, bf16[32,2048]{1,0:T(8,128)(2,1)S(1)}, u32[]{:S(2)}, u32[]{:S(2)}) collective-permute-start(bf16[32,2048]{1,0:T(8,128)(2,1)S(1)} %get-tuple-element.43), channel_id=1, source_target_pairs={{0,16},{2,18},{4,20},{6,22},{8,24},{10,26},{12,28},{14,30},{16,0},... | collective-permute-start | bytes 393224 | tf_op jit(solution)/shard_map/ppermute | solution.py:52
  227.4 11.3 %collective-permute-start.45 = (bf16[32,2048]{1,0:T(8,128)(2,1)S(1)}, bf16[32,2048]{1,0:T(8,128)(2,1)S(1)}, u32[]{:S(2)}, u32[]{:S(2)}) collective-permute-start(bf16[32,2048]{1,0:T(8,128)(2,1)S(1)} %get-tuple-element.42), channel_id=1, source_target_pairs={{0,24},{2,26},{4,28},{6,30},{8,0},{10,2},{12,4},{14,6},{16,8},{18,... | collective-permute-start | bytes 393224 | tf_op jit(solution)/shard_map/ppermute | solution.py:52
  227.5 23.9 %collective-permute-start.33 = (bf16[32,2048]{1,0:T(8,128)(2,1)S(1)}, bf16[32,2048]{1,0:T(8,128)(2,1)S(1)}, u32[]{:S(2)}, u32[]{:S(2)}) collective-permute-start(bf16[32,2048]{1,0:T(8,128)(2,1)S(1)} %get-tuple-element.44), channel_id=1, source_target_pairs={{0,8},{2,10},{4,12},{6,14},{8,16},{10,18},{12,20},{14,22},{16,24},... | collective-permute-start | bytes 393224 | tf_op jit(solution)/shard_map/ppermute | solution.py:52
  235.2 16.9 %collective-permute-start.34 = (bf16[32,2048]{1,0:T(8,128)(2,1)S(1)}, bf16[32,2048]{1,0:T(8,128)(2,1)S(1)}, u32[]{:S(2)}, u32[]{:S(2)}) collective-permute-start(bf16[32,2048]{1,0:T(8,128)(2,1)S(1)} %get-tuple-element.46), channel_id=1, source_target_pairs={{0,16},{2,18},{4,20},{6,22},{8,24},{10,26},{12,28},{14,30},{16,0},... | collective-permute-start | bytes 393224 | tf_op jit(solution)/shard_map/ppermute | solution.py:52
  238.7 13.4 %collective-permute-start.35 = (bf16[32,2048]{1,0:T(8,128)(2,1)S(1)}, bf16[32,2048]{1,0:T(8,128)(2,1)S(1)}, u32[]{:S(2)}, u32[]{:S(2)}) collective-permute-start(bf16[32,2048]{1,0:T(8,128)(2,1)S(1)} %get-tuple-element.45), channel_id=1, source_target_pairs={{0,24},{2,26},{4,28},{6,30},{8,0},{10,2},{12,4},{14,6},{16,8},{18,... | collective-permute-start | bytes 393224 | tf_op jit(solution)/shard_map/ppermute | solution.py:52
  239.4 24.3 %collective-permute-start.46 = (bf16[32,2048]{1,0:T(8,128)(2,1)S(1)}, bf16[32,2048]{1,0:T(8,128)(2,1)S(1)}, u32[]{:S(2)}, u32[]{:S(2)}) collective-permute-start(bf16[32,2048]{1,0:T(8,128)(2,1)S(1)} %get-tuple-element.4), channel_id=1, source_target_pairs={{0,24},{2,26},{4,28},{6,30},{8,0},{10,2},{12,4},{14,6},{16,8},{18,... | collective-permute-start | bytes 393224 | tf_op jit(solution)/shard_map/ppermute | solution.py:52
  251.4 13.9 %collective-permute-start.47 = (bf16[32,2048]{1,0:T(8,128)(2,1)S(1)}, bf16[32,2048]{1,0:T(8,128)(2,1)S(1)}, u32[]{:S(2)}, u32[]{:S(2)}) collective-permute-start(bf16[32,2048]{1,0:T(8,128)(2,1)S(1)} %get-tuple-element.4), channel_id=1, source_target_pairs={{0,16},{2,18},{4,20},{6,22},{8,24},{10,26},{12,28},{14,30},{16,0},... | collective-permute-start | bytes 393224 | tf_op jit(solution)/shard_map/ppermute | solution.py:52
  251.4 16.0 %collective-permute-start.48 = (bf16[32,2048]{1,0:T(8,128)(2,1)S(1)}, bf16[32,2048]{1,0:T(8,128)(2,1)S(1)}, u32[]{:S(2)}, u32[]{:S(2)}) collective-permute-start(bf16[32,2048]{1,0:T(8,128)(2,1)S(1)} %get-tuple-element.4), channel_id=1, source_target_pairs={{0,8},{2,10},{4,12},{6,14},{8,16},{10,18},{12,20},{14,22},{16,24},... | collective-permute-start | bytes 393224 | tf_op jit(solution)/shard_map/ppermute | solution.py:52
  252.3 16.3 %collective-permute-start.36 = (bf16[32,2048]{1,0:T(8,128)(2,1)S(1)}, bf16[32,2048]{1,0:T(8,128)(2,1)S(1)}, u32[]{:S(2)}, u32[]{:S(2)}) collective-permute-start(bf16[32,2048]{1,0:T(8,128)(2,1)S(1)} %get-tuple-element.10), channel_id=1, source_target_pairs={{0,24},{2,26},{4,28},{6,30},{8,0},{10,2},{12,4},{14,6},{16,8},{18,... | collective-permute-start | bytes 393224 | tf_op jit(solution)/shard_map/ppermute | solution.py:52
  263.6 15.7 %collective-permute-start.37 = (bf16[32,2048]{1,0:T(8,128)(2,1)S(1)}, bf16[32,2048]{1,0:T(8,128)(2,1)S(1)}, u32[]{:S(2)}, u32[]{:S(2)}) collective-permute-start(bf16[32,2048]{1,0:T(8,128)(2,1)S(1)} %get-tuple-element.10), channel_id=1, source_target_pairs={{0,16},{2,18},{4,20},{6,22},{8,24},{10,26},{12,28},{14,30},{16,0},... | collective-permute-start | bytes 393224 | tf_op jit(solution)/shard_map/ppermute | solution.py:52
  263.7 15.7 %collective-permute-start.38 = (bf16[32,2048]{1,0:T(8,128)(2,1)S(1)}, bf16[32,2048]{1,0:T(8,128)(2,1)S(1)}, u32[]{:S(2)}, u32[]{:S(2)}) collective-permute-start(bf16[32,2048]{1,0:T(8,128)(2,1)S(1)} %get-tuple-element.10), channel_id=1, source_target_pairs={{0,8},{2,10},{4,12},{6,14},{8,16},{10,18},{12,20},{14,22},{16,24},... | collective-permute-start | bytes 393224 | tf_op jit(solution)/shard_map/ppermute | solution.py:52
  265.3 16.9 %collective-permute-start.26 = (bf16[32,2048]{1,0:T(8,128)(2,1)S(1)}, bf16[32,2048]{1,0:T(8,128)(2,1)S(1)}, u32[]{:S(2)}, u32[]{:S(2)}) collective-permute-start(bf16[32,2048]{1,0:T(8,128)(2,1)S(1)} %get-tuple-element.30), channel_id=1, source_target_pairs={{0,24},{2,26},{4,28},{6,30},{8,0},{10,2},{12,4},{14,6},{16,8},{18,... | collective-permute-start | bytes 393224 | tf_op jit(solution)/shard_map/ppermute | solution.py:52
  267.5 23.2 %collective-permute-start.27 = (bf16[32,2048]{1,0:T(8,128)(2,1)S(1)}, bf16[32,2048]{1,0:T(8,128)(2,1)S(1)}, u32[]{:S(2)}, u32[]{:S(2)}) collective-permute-start(bf16[32,2048]{1,0:T(8,128)(2,1)S(1)} %get-tuple-element.30), channel_id=1, source_target_pairs={{0,16},{2,18},{4,20},{6,22},{8,24},{10,26},{12,28},{14,30},{16,0},... | collective-permute-start | bytes 393224 | tf_op jit(solution)/shard_map/ppermute | solution.py:52
  268.7 23.4 %collective-permute-start.28 = (bf16[32,2048]{1,0:T(8,128)(2,1)S(1)}, bf16[32,2048]{1,0:T(8,128)(2,1)S(1)}, u32[]{:S(2)}, u32[]{:S(2)}) collective-permute-start(bf16[32,2048]{1,0:T(8,128)(2,1)S(1)} %get-tuple-element.30), channel_id=1, source_target_pairs={{0,8},{2,10},{4,12},{6,14},{8,16},{10,18},{12,20},{14,22},{16,24},... | collective-permute-start | bytes 393224 | tf_op jit(solution)/shard_map/ppermute | solution.py:52
  279.4 14.3 %collective-permute-start.16 = (bf16[32,2048]{1,0:T(8,128)(2,1)S(1)}, bf16[32,2048]{1,0:T(8,128)(2,1)S(1)}, u32[]{:S(2)}, u32[]{:S(2)}) collective-permute-start(bf16[32,2048]{1,0:T(8,128)(2,1)S(1)} %get-tuple-element.34), channel_id=1, source_target_pairs={{0,24},{2,26},{4,28},{6,30},{8,0},{10,2},{12,4},{14,6},{16,8},{18,... | collective-permute-start | bytes 393224 | tf_op jit(solution)/shard_map/ppermute | solution.py:52
  279.4 16.8 %collective-permute-start.17 = (bf16[32,2048]{1,0:T(8,128)(2,1)S(1)}, bf16[32,2048]{1,0:T(8,128)(2,1)S(1)}, u32[]{:S(2)}, u32[]{:S(2)}) collective-permute-start(bf16[32,2048]{1,0:T(8,128)(2,1)S(1)} %get-tuple-element.34), channel_id=1, source_target_pairs={{0,16},{2,18},{4,20},{6,22},{8,24},{10,26},{12,28},{14,30},{16,0},... | collective-permute-start | bytes 393224 | tf_op jit(solution)/shard_map/ppermute | solution.py:52
  282.2 14.0 %collective-permute-start.18 = (bf16[32,2048]{1,0:T(8,128)(2,1)S(1)}, bf16[32,2048]{1,0:T(8,128)(2,1)S(1)}, u32[]{:S(2)}, u32[]{:S(2)}) collective-permute-start(bf16[32,2048]{1,0:T(8,128)(2,1)S(1)} %get-tuple-element.34), channel_id=1, source_target_pairs={{0,8},{2,10},{4,12},{6,14},{8,16},{10,18},{12,20},{14,22},{16,24},... | collective-permute-start | bytes 393224 | tf_op jit(solution)/shard_map/ppermute | solution.py:52
  290.7 14.8 %collective-permute-start.49 = (bf16[128,2048]{1,0:T(8,128)(2,1)S(1)}, bf16[128,2048]{1,0:T(8,128)(2,1)S(1)}, u32[]{:S(2)}, u32[]{:S(2)}) collective-permute-start(bf16[128,2048]{1,0:T(8,128)(2,1)S(1)} %pad_maximum_fusion.5), channel_id=1, source_target_pairs={{0,4},{2,6},{4,0},{6,2},{8,12},{10,14},{12,8},{14,10},{16,20},{18,... | collective-permute-start | bytes 1572872 | tf_op jit(solution)/shard_map/ppermute | solution.py:52
  292.1 14.9 %collective-permute-start.39 = (bf16[128,2048]{1,0:T(8,128)(2,1)S(1)}, bf16[128,2048]{1,0:T(8,128)(2,1)S(1)}, u32[]{:S(2)}, u32[]{:S(2)}) collective-permute-start(bf16[128,2048]{1,0:T(8,128)(2,1)S(1)} %pad_maximum_fusion.4), channel_id=1, source_target_pairs={{0,2},{2,0},{4,6},{6,4},{8,10},{10,8},{12,14},{14,12},{16,18},{18,... | collective-permute-start | bytes 1572872 | tf_op jit(solution)/shard_map/ppermute | solution.py:52
  293.7 23.0 %collective-permute-start.29 = (bf16[128,2048]{1,0:T(8,128)(2,1)S(1)}, bf16[128,2048]{1,0:T(8,128)(2,1)S(1)}, u32[]{:S(2)}, u32[]{:S(2)}) collective-permute-start(bf16[128,2048]{1,0:T(8,128)(2,1)S(1)} %pad_maximum_fusion.3), channel_id=1, source_target_pairs={{0,4},{2,6},{4,0},{6,2},{8,12},{10,14},{12,8},{14,10},{16,20},{18,... | collective-permute-start | bytes 1572872 | tf_op jit(solution)/shard_map/ppermute | solution.py:52
  296.2 22.0 %collective-permute-start.19 = (bf16[128,2048]{1,0:T(8,128)(2,1)S(1)}, bf16[128,2048]{1,0:T(8,128)(2,1)S(1)}, u32[]{:S(2)}, u32[]{:S(2)}) collective-permute-start(bf16[128,2048]{1,0:T(8,128)(2,1)S(1)} %pad_maximum_fusion.2), channel_id=1, source_target_pairs={{0,2},{2,0},{4,6},{6,4},{8,10},{10,8},{12,14},{14,12},{16,18},{18,... | collective-permute-start | bytes 1572872 | tf_op jit(solution)/shard_map/ppermute | solution.py:52
  305.5 35.2 %collective-permute-start.50 = (bf16[256,2048]{1,0:T(8,128)(2,1)S(1)}, bf16[256,2048]{1,0:T(8,128)(2,1)S(1)}, u32[]{:S(2)}, u32[]{:S(2)}) collective-permute-start(bf16[256,2048]{1,0:T(8,128)(2,1)S(1)} %constant_dynamic-update-slice_fusion.15.refs_1_), channel_id=1, source_target_pairs={{0,2},{2,0},{4,6},{6,4},{8,10},{10,8},{12,14},{14,12},{16,18},{18,... | collective-permute-start | bytes 3145736 | tf_op jit(solution)/shard_map/ppermute | solution.py:52
  307.1 36.5 %collective-permute-start.40 = (bf16[256,2048]{1,0:T(8,128)(2,1)S(1)}, bf16[256,2048]{1,0:T(8,128)(2,1)S(1)}, u32[]{:S(2)}, u32[]{:S(2)}) collective-permute-start(bf16[256,2048]{1,0:T(8,128)(2,1)S(1)} %constant_dynamic-update-slice_fusion.10.refs_1_), channel_id=1, source_target_pairs={{0,4},{2,6},{4,0},{6,2},{8,12},{10,14},{12,8},{14,10},{16,20},{18,... | collective-permute-start | bytes 3145736 | tf_op jit(solution)/shard_map/ppermute | solution.py:52
  316.7 45.0 %collective-permute-start.30 = (bf16[256,2048]{1,0:T(8,128)(2,1)S(1)}, bf16[256,2048]{1,0:T(8,128)(2,1)S(1)}, u32[]{:S(2)}, u32[]{:S(2)}) collective-permute-start(bf16[256,2048]{1,0:T(8,128)(2,1)S(1)} %constant_dynamic-update-slice_fusion.5.refs_1_), channel_id=1, source_target_pairs={{0,2},{2,0},{4,6},{6,4},{8,10},{10,8},{12,14},{14,12},{16,18},{18,... | collective-permute-start | bytes 3145736 | tf_op jit(solution)/shard_map/ppermute | solution.py:52
  318.3 46.4 %collective-permute-start.20 = (bf16[256,2048]{1,0:T(8,128)(2,1)S(1)}, bf16[256,2048]{1,0:T(8,128)(2,1)S(1)}, u32[]{:S(2)}, u32[]{:S(2)}) collective-permute-start(bf16[256,2048]{1,0:T(8,128)(2,1)S(1)} %constant_dynamic-update-slice_fusion.refs_1_), channel_id=1, source_target_pairs={{0,4},{2,6},{4,0},{6,2},{8,12},{10,14},{12,8},{14,10},{16,20},{18,... | collective-permute-start | bytes 3145736 | tf_op jit(solution)/shard_map/ppermute | solution.py:52
  (11 other events, 99.3 us)
Sparse Core Ops, SparseCore 0:
  11.4 80.9 all-gather.2
  93.9 18.4 all-gather.4

commit v2 on v1

--- a/solution.py
+++ b/solution.py
@@ -22,7 +22,16 @@
 PIVOTS = 8
 VMEM_LIMIT = 40 << 20
 
-GROUPS = ((2, (2, 1, 0)), (2, (1, 2, 0)), (2, (2, 1, 0)), (2, (1, 2, 0)))
+GROUPS = ((2, (0, 1, 2, 3)), (2, (2, 3, 1, 0)), (2, (1, 2, 0, 3)), (2, (0, 1, 2, 3)))
+STEPS = ((0, 0), (1, 0), (2, 0), (3, 0), (0, 1), (1, 1), (2, 1), (0, 2), (3, 1), (1, 2), (2, 2), (0, 3), (3, 2), (1, 3), (2, 3), (0, 4), (3, 3), (1, 4), (2, 4), (0, 5), (1, 5), (3, 4), (2, 5), (0, 6), (1, 6), (3, 5), (2, 6), (0, 7), (3, 6), (1, 7), (2, 7), (3, 7), (0, 8), (1, 8), (2, 8), (3, 8))
+
+
+def flip_pairs(devices, bit):
+    return [(at, at ^ (1 << bit)) for at in range(devices)]
+
+
+def flip(value, devices, bit):
+    return lax.ppermute(value, "dp", flip_pairs(devices, bit))
 
 
 def mesh_dims(devices):
@@ -50,10 +59,6 @@
 
 def send(value, dims, shift):
     return lax.ppermute(value, "dp", shift_pairs(dims, shift))
-
-
-def unit(axis, by):
-    return tuple(by if i == axis else 0 for i in range(3))
 
 
 def dot_nn(a, b):
@@ -235,23 +240,25 @@
     )(*operands)
 
 
-def selection(dims, own, order, rank, core):
-    piece = rank // math.prod(dims)
+def selection(devices, dp, order, rank):
     index = jnp.zeros((), jnp.int32)
-    strides = (dims[1] * dims[2], dims[2], 1)
-    for axis in order:
-        places = (own[axis] + jnp.arange(dims[axis], dtype=jnp.int32)) % dims[axis]
-        index = index[..., None] + places * strides[axis]
-    index = index[..., None] * piece + jnp.arange(piece, dtype=jnp.int32)
+    for bit in order:
+        index = index[..., None] | jnp.array([0, 1 << bit], jnp.int32)
+    piece = rank // devices
+    index = (index ^ dp)[..., None] * piece + jnp.arange(piece, dtype=jnp.int32)
     index = index.reshape(rank)
-    return index
-
-
-def one_hot(index, rank):
     return (index[:, None] == jnp.arange(rank, dtype=jnp.int32)[None, :]).astype(BF16)
 
 
+def after(token, values):
+    if token is None:
+        return values
+    return lax.optimization_barrier((*values, token))[:-1]
+
+
 def local(dims, activations, out_grads, sketch, first_moment, second_moment):
+    devices = math.prod(dims)
+    bits = devices.bit_length() - 1
     dp = lax.axis_index("dp")
     core = lax.axis_index("tensor")
     own = (dp // (dims[1] * dims[2]), dp // dims[2] % dims[1], dp % dims[2])
@@ -259,10 +266,13 @@
     width = out_grads.shape[1]
     depth = activations.shape[1] * 2
 
-    features = lax.all_gather(activations, "tensor", axis=1, tiled=True)
+    beside = lax.ppermute(activations, "tensor", [(0, 1), (1, 0)])
     half = lax.dynamic_slice_in_dim(sketch, core * (rank // 2), rank // 2, 1).astype(BF16)
     sketch_half = lax.all_gather(half, "dp", axis=0, tiled=True)
-    mixed_half = jnp.dot(features, sketch_half, preferred_element_type=F32)
+    mid = sketch_half.shape[0] // 2
+    part = lambda at: lax.dynamic_slice_in_dim(sketch_half, at * mid, mid, 0)
+    mixed_half = jnp.dot(activations, part(core), preferred_element_type=F32)
+    mixed_half = mixed_half + jnp.dot(beside, part(1 - core), preferred_element_type=F32)
     mixed_other = lax.ppermute(mixed_half, "tensor", [(0, 1), (1, 0)])
     mixed = jnp.where(
         core == 0,
@@ -275,10 +285,11 @@
     own_rows = dot_nt(sketch, inverse).astype(BF16)
     projected = dot_nt(inverse, mixed).astype(BF16)
 
+    orders = [order + tuple(range(4, bits)) for _, order in GROUPS]
     selections = {}
-    for _, order in GROUPS:
+    for order in orders:
         if order not in selections:
-            pick = one_hot(selection(dims, own, order, rank, core), rank)
+            pick = selection(devices, dp, order, rank)
             selections[order] = (
                 jnp.dot(pick, projected, preferred_element_type=F32).astype(BF16),
                 lax.dot_general(
@@ -288,60 +299,63 @@
 
     update_scale = math.sqrt(depth / rank)
     eighth = width // 8
-    start = 0
-    states = []
-    for share, order in GROUPS:
-        cols = share * eighth
-        grads = out_grads[:, start : start + cols]
-        columns = selections[order][0]
-        size = rank // dims[order[0]]
-        term = lambda by: jnp.dot(
-            columns[by * size : (by + 1) * size], grads, preferred_element_type=F32
-        )
-        axis = order[0]
-        arrived = [
-            send(term(by).astype(BF16), dims, unit(axis, by)) for by in range(1, dims[axis])
-        ]
-        total = term(0)
-        for piece in arrived:
+    starts = [sum(share for share, _ in GROUPS[:g]) * eighth for g in range(len(GROUPS))]
+    kept = [None] * len(GROUPS)
+    arriving = [None] * len(GROUPS)
+    first_parts = [None] * len(GROUPS)
+    second_parts = [None] * len(GROUPS)
+    token = None
+    update = None
+    last = 2 * bits
+    steps = STEPS if STEPS and bits == 4 else [
+        (g, s) for s in range(last + 1) for g in range(len(GROUPS))
+    ]
+    for g, step in steps:
+        order = orders[g]
+        cols = GROUPS[g][0] * eighth
+        start = starts[g]
+        columns = slice(start, start + cols)
+        if step == 0:
+            size = rank // 2
+            left, grads = after(token, (selections[order][0], out_grads))
+            outgoing = jnp.dot(
+                left[size:], grads[:, columns], preferred_element_type=F32
+            ).astype(BF16)
+            kept[g] = jnp.dot(left[:size], grads[:, columns], preferred_element_type=F32)
+            bit = order[0]
+        elif step < bits:
+            total, piece = after(token, (kept[g], arriving[g]))
             total = total + piece.astype(F32)
-        for axis in order[1:]:
-            size = size // dims[axis]
-            arrived = [
-                send(total[by * size : (by + 1) * size].astype(BF16), dims, unit(axis, by))
-                for by in range(1, dims[axis])
-            ]
-            total = total[:size]
-            for piece in arrived:
-                total = total + piece.astype(F32)
-        states.append((start, cols, order, total))
-        start += cols
-
-    first_parts, second_parts = [], []
-    update = None
-    for start, cols, order, grad_low in states:
-        first = BETA_ONE * first_moment[:, start : start + cols] + (1.0 - BETA_ONE) * grad_low
-        second = (
-            BETA_TWO * second_moment[:, start : start + cols]
-            + (1.0 - BETA_TWO) * grad_low * grad_low
-        )
-        direction = (
-            first / CORRECT_ONE / (jnp.sqrt(second / CORRECT_TWO) + EPSILON)
-        ).astype(BF16)
-        first_parts.append(first)
-        second_parts.append(second)
-        for axis in order[:0:-1]:
-            direction = jnp.concatenate(
-                [direction]
-                + [send(direction, dims, unit(axis, -by)) for by in range(1, dims[axis])]
+            size = total.shape[0] // 2
+            outgoing = total[size:].astype(BF16)
+            kept[g] = total[:size]
+            bit = order[step]
+        elif step == bits:
+            total, piece = after(token, (kept[g], arriving[g]))
+            grad_low = total + piece.astype(F32)
+            first = BETA_ONE * first_moment[:, columns] + (1.0 - BETA_ONE) * grad_low
+            second = (
+                BETA_TWO * second_moment[:, columns]
+                + (1.0 - BETA_TWO) * grad_low * grad_low
             )
-        axis = order[0]
-        pieces = [direction] + [
-            send(direction, dims, unit(axis, -by)) for by in range(1, dims[axis])
-        ]
-        update = update_columns(
-            selections[order][1], pieces, update, start, width, update_scale
-        )
+            outgoing = (
+                first / CORRECT_ONE / (jnp.sqrt(second / CORRECT_TWO) + EPSILON)
+            ).astype(BF16)
+            first_parts[g], second_parts[g] = first, second
+            kept[g] = outgoing
+            bit = order[bits - 1]
+        elif step < last:
+            mine, piece = after(token, (kept[g], arriving[g]))
+            outgoing = kept[g] = jnp.concatenate([mine, piece])
+            bit = order[last - 1 - step]
+        else:
+            pieces = after(token, (kept[g], arriving[g]))
+            update = update_columns(
+                selections[order][1], pieces, update, start, width, update_scale
+            )
+            continue
+        arriving[g] = flip(outgoing, devices, bit)
+        token = outgoing
     return (
         update,
         jnp.concatenate(first_parts, axis=1),

time: 375 us -> 277 us (0.74)
  starting transfers between devices: 101 us -> 47.4 us
  waiting for transfers between devices: 191 us -> 144 us
    ppermute x49 -> x9, waiting for transfers between devices: 145 us -> 15.1 us  [send(): return lax.ppermute(value, 'dp', shift_pairs(dims, shift))]
    ppermute x0 -> x33, waiting for transfers between devices: none -> 105 us  [the longest x32 105 us: flip(): return lax.ppermute(value, 'dp', flip_pairs(devices, bit))]
    ppermute x49 -> x9, starting transfers between devices: 100 us -> 13.4 us  [send(): return lax.ppermute(value, 'dp', shift_pairs(dims, shift))]
    ppermute x0 -> x33, starting transfers between devices: none -> 33.9 us  [the longest x32 33.3 us: flip(): return lax.ppermute(value, 'dp', flip_pairs(devices, bit))]
    all_gather x1 -> x0, waiting for transfers between devices: 20 us -> none  [local(): features = lax.all_gather(activations, 'tensor', axis=1, tiled=True)]
    dot_general x9 -> x10, matrix products: 16.3 us -> 13.8 us  [the longest x1 4.26 us: local(): mixed_half = jnp.dot(activations, part(core), preferred_element_type=F32)]
  transfers between devices with their start and end apart: 53 -> 45, of which waited for: 24 -> 29; matrix products, arithmetic and copies ran while one was open for 4% -> 8% of each run, Pallas kernels for 9% -> 12%
where the time goes in v2:
time: 277 us; the launch traced here: 276 us
  waiting for transfers between devices  144 us (52%)
  starting transfers between devices  47.4 us (17%)
  Pallas kernels  36.6 us (13%)
  matrix products  22.7 us (8%)
  between operations  15.2 us (5%)
  other arithmetic  5.73 us (2%)
  local copies, waits for them, and re-layouts  4.74 us (2%)
    ppermute x32, waiting for transfers between devices, flip(): return lax.ppermute(value, 'dp', flip_pairs(devices, bit))  105 us
    ppermute x32, starting transfers between devices, flip(): return lax.ppermute(value, 'dp', flip_pairs(devices, bit))  33.3 us
    pallas_call x1, Pallas kernels, inverse_of_factor(): pl.pallas_call(functools.partial(factor_kernel, blocks), out_shape=jax.Sh...  24.9 us
    all_gather x1, waiting for transfers between devices, local(): sketch_half = lax.all_gather(half, 'dp', axis=0, tiled=True)  22.5 us
    ppermute x9, waiting for transfers between devices, send(): return lax.ppermute(value, 'dp', shift_pairs(dims, shift))  15.1 us
    ppermute x9, starting transfers between devices, send(): return lax.ppermute(value, 'dp', shift_pairs(dims, shift))  13.4 us
    pallas_call x4, Pallas kernels, update_columns(): pl.pallas_call(functools.partial(update_kernel, scale, len(pieces)), grid...  11.7 us
  transfers between devices with their start and end apart: 45, of which 29 were waited for; matrix products, arithmetic and copies ran while one was open for 8% of the time, Pallas kernels for 12%

profile of v2, /device:TPU:0, one launch (start us, length us, event | category | flops | bytes accessed | tf_op | source)
XLA Modules:
  0.0 276.4 jit_solution(1844492466124232308)
XLA Ops:
  9.7 1.9 fusion.56
  11.8 2.7 collective-permute-start
  14.5 1.5 collective-permute-start.1
  17.4 2.3 collective-permute-done.1
  19.7 1.6 collective-permute-done.2
  21.4 1.6 collective-permute-start.3
  23.0 2.6 collective-permute-start.4
  27.1 2.5 collective-permute-done.3
  29.6 4.3 %collective-permute-done.4 = f32[160,128]{1,0:T(8,128)S(1)} collective-permute-done((f32[160,128]{1,0:T(8,128)S(1)}, f32[160,128]{1,0:T(8,128)S(1)}, u32[]{:S(2)}, u32[]{:S(2)}) %collective-permute-start.4) | collective-permute-done | bytes 81952 | tf_op jit(solution)/shard_map/ppermute | solution.py:61
  35.6 2.1 collective-permute-start.8
  42.7 24.9 %inverse_factor.1 = f32[512,512]{1,0:T(8,128)S(1)} custom-call(f32[1280,128]{1,0:T(8,128)S(1)} %maximum_select_fusion.2.packed_ref), custom_call_target="tpu_custom_call" | custom-call | tf_op jit(solution)/shard_map/inverse_factor/pallas_call | solution.py:154
  67.6 1.9 convolution_convert_fusion.11
  69.5 22.5 %all-gather.2.cloned.1.call-done = bf16[8192,256]{1,0:T(8,128)(2,1)} async-done(((bf16[512,256]{1,0:T(8,128)(2,1)}), bf16[8192,256]{1,0:T(8,128)(2,1)}) %all-gather.2.cloned.1.call-update) | async-done | bytes 4194320 | tf_op jit(solution)/shard_map/all_gather | solution.py:271
  92.0 4.3 %fusion.2 = f32[256,512]{1,0:T(8,128)S(1)} fusion(bf16[512,4096]{1,0:T(8,128)(2,1)} %param.17, bf16[8192,256]{1,0:T(8,128)(2,1)} %all-gather.2.cloned.1.call-done, s32[]{:T(128)S(6)} %select_n.162), kind=kOutput, calls=%fused_computation.10 | convolution fusion | flops 1073741824 | bytes 6815748 | tf_op jit(solution)/shard_map/dot_general | solution.py:274
  96.3 3.6 %fusion.19 = f32[512,256]{0,1:T(8,128)S(1)} fusion(f32[256,512]{1,0:T(8,128)S(1)} %fusion.2, bf16[512,4096]{1,0:T(8,128)(2,1)} %collective-permute-done.10, bf16[8192,256]{1,0:T(8,128)(2,1)S(1)} %copy-done.13, s32[]{:T(128)S(6)} %select_n.163), kind=kOutput, calls=%fused_computation.33 | convolution fusion | flops 1073872896 | bytes 7340036 | tf_op jit(solution)/shard_map/dot_general | solution.py:275
  101.9 1.9 convolution_convert_fusion.10
  107.4 1.5 collective-permute-start.13
  109.7 1.5 collective-permute-start.16
  114.3 1.5 collective-permute-start.12
  116.5 17.0 %collective-permute-done.13 = bf16[256,2048]{1,0:T(8,128)(2,1)S(1)} collective-permute-done((bf16[256,2048]{1,0:T(8,128)(2,1)S(1)}, bf16[256,2048]{1,0:T(8,128)(2,1)S(1)}, u32[]{:S(2)}, u32[]{:S(2)}) %collective-permute-start.13) | collective-permute-done | bytes 1048608 | tf_op jit(solution)/shard_map/ppermute | solution.py:34
  133.9 1.5 collective-permute-start.14
  135.9 2.0 collective-permute-start.20
  139.0 9.5 %collective-permute-done.14 = bf16[128,2048]{1,0:T(8,128)(2,1)S(1)} collective-permute-done((bf16[128,2048]{1,0:T(8,128)(2,1)S(1)}, bf16[128,2048]{1,0:T(8,128)(2,1)S(1)}, u32[]{:S(2)}, u32[]{:S(2)}) %collective-permute-start.14) | collective-permute-done | bytes 524320 | tf_op jit(solution)/shard_map/ppermute | solution.py:34
  149.3 6.3 %collective-permute-done.12 = bf16[256,2048]{1,0:T(8,128)(2,1)S(1)} collective-permute-done((bf16[256,2048]{1,0:T(8,128)(2,1)S(1)}, bf16[256,2048]{1,0:T(8,128)(2,1)S(1)}, u32[]{:S(2)}, u32[]{:S(2)}) %collective-permute-start.12) | collective-permute-done | bytes 1048608 | tf_op jit(solution)/shard_map/ppermute | solution.py:34
  158.7 2.3 collective-permute-done.20
  164.1 2.7 collective-permute-done.18
  168.3 3.8 %collective-permute-done.17 = bf16[128,2048]{1,0:T(8,128)(2,1)S(1)} collective-permute-done((bf16[128,2048]{1,0:T(8,128)(2,1)S(1)}, bf16[128,2048]{1,0:T(8,128)(2,1)S(1)}, u32[]{:S(2)}, u32[]{:S(2)}) %collective-permute-start.17) | collective-permute-done | bytes 524320 | tf_op jit(solution)/shard_map/ppermute | solution.py:34
  172.2 1.6 collective-permute-start.21
  173.8 2.6 collective-permute-done.24
  176.4 1.5 collective-permute-start.26
  178.2 2.0 collective-permute-start.29
  181.5 2.0 collective-permute-start.25
  184.3 8.2 %collective-permute-done.29 = bf16[32,2048]{1,0:T(8,128)(2,1)S(1)} collective-permute-done((bf16[32,2048]{1,0:T(8,128)(2,1)S(1)}, bf16[32,2048]{1,0:T(8,128)(2,1)S(1)}, u32[]{:S(2)}, u32[]{:S(2)}) %collective-permute-start.29) | collective-permute-done | bytes 131104 | tf_op jit(solution)/shard_map/ppermute | solution.py:34
  192.8 4.4 %collective-permute-done.28 = bf16[32,2048]{1,0:T(8,128)(2,1)S(1)} collective-permute-done((bf16[32,2048]{1,0:T(8,128)(2,1)S(1)}, bf16[32,2048]{1,0:T(8,128)(2,1)S(1)}, u32[]{:S(2)}, u32[]{:S(2)}) %collective-permute-start.28) | collective-permute-done | bytes 131104 | tf_op jit(solution)/shard_map/ppermute | solution.py:34
  198.0 3.0 %collective-permute-done.25 = bf16[32,2048]{1,0:T(8,128)(2,1)S(1)} collective-permute-done((bf16[32,2048]{1,0:T(8,128)(2,1)S(1)}, bf16[32,2048]{1,0:T(8,128)(2,1)S(1)}, u32[]{:S(2)}, u32[]{:S(2)}) %collective-permute-start.25) | collective-permute-done | bytes 131104 | tf_op jit(solution)/shard_map/ppermute | solution.py:34
  201.3 3.4 %collective-permute-done.33 = bf16[32,2048]{1,0:T(8,128)(2,1)S(1)} collective-permute-done((bf16[32,2048]{1,0:T(8,128)(2,1)S(1)}, bf16[32,2048]{1,0:T(8,128)(2,1)S(1)}, u32[]{:S(2)}, u32[]{:S(2)}) %collective-permute-start.33) | collective-permute-done | bytes 131104 | tf_op jit(solution)/shard_map/ppermute | solution.py:34
  205.4 4.3 %collective-permute-done.32 = bf16[64,2048]{1,0:T(8,128)(2,1)S(1)} collective-permute-done((bf16[64,2048]{1,0:T(8,128)(2,1)S(1)}, bf16[64,2048]{1,0:T(8,128)(2,1)S(1)}, u32[]{:S(2)}, u32[]{:S(2)}) %collective-permute-start.32) | collective-permute-done | bytes 262176 | tf_op jit(solution)/shard_map/ppermute | solution.py:34
  210.6 2.5 collective-permute-start.34
  213.2 7.2 %collective-permute-done.35 = bf16[128,2048]{1,0:T(8,128)(2,1)S(1)} collective-permute-done((bf16[128,2048]{1,0:T(8,128)(2,1)S(1)}, bf16[128,2048]{1,0:T(8,128)(2,1)S(1)}, u32[]{:S(2)}, u32[]{:S(2)}) %collective-permute-start.35) | collective-permute-done | bytes 524320 | tf_op jit(solution)/shard_map/ppermute | solution.py:34
  221.3 7.2 %collective-permute-done.34 = bf16[64,2048]{1,0:T(8,128)(2,1)S(1)} collective-permute-done((bf16[64,2048]{1,0:T(8,128)(2,1)S(1)}, bf16[64,2048]{1,0:T(8,128)(2,1)S(1)}, u32[]{:S(2)}, u32[]{:S(2)}) %collective-permute-start.34) | collective-permute-done | bytes 262176 | tf_op jit(solution)/shard_map/ppermute | solution.py:34
  228.6 1.5 collective-permute-start.37
  230.1 2.3 collective-permute-done.39
  232.7 8.7 %collective-permute-done.38 = bf16[128,2048]{1,0:T(8,128)(2,1)S(1)} collective-permute-done((bf16[128,2048]{1,0:T(8,128)(2,1)S(1)}, bf16[128,2048]{1,0:T(8,128)(2,1)S(1)}, u32[]{:S(2)}, u32[]{:S(2)}) %collective-permute-start.38) | collective-permute-done | bytes 524320 | tf_op jit(solution)/shard_map/ppermute | solution.py:34
  245.9 2.9 %update_columns.4.refs_3_ = f32[512,8192]{1,0:T(8,128)} custom-call(bf16[512,512]{1,0:T(8,128)(2,1)S(1)} %convolution_convert_fusion.9.refs_0_, bf16[256,2048]{1,0:T(8,128)(2,1)S(1)} %constant_dynamic-update-slice_fusion.14.refs_1_, bf16[256,2048]{1,0:T(8,128)(2,1)S(1)} %collective-permute-done.43.refs_2_), custom_call_target="tpu_custom_call" | custom-call | tf_op jit(solution)/shard_map/update_columns/pallas_call | solution.py:231
  248.8 12.0 %collective-permute-done.42.refs_2_ = bf16[256,2048]{1,0:T(8,128)(2,1)S(1)} collective-permute-done((bf16[256,2048]{1,0:T(8,128)(2,1)S(1)}, bf16[256,2048]{1,0:T(8,128)(2,1)S(1)}, u32[]{:S(2)}, u32[]{:S(2)}) %collective-permute-start.42) | collective-permute-done | bytes 1048608 | tf_op jit(solution)/shard_map/ppermute | solution.py:34
  260.8 2.9 %update_columns.5.refs_3_ = f32[512,8192]{1,0:T(8,128)} custom-call(bf16[512,512]{1,0:T(8,128)(2,1)S(1)} %convolution_convert_fusion.4.refs_0_, bf16[256,2048]{1,0:T(8,128)(2,1)S(1)} %constant_dynamic-update-slice_fusion.18.refs_1_, bf16[256,2048]{1,0:T(8,128)(2,1)S(1)} %collective-permute-done.42.refs_2_, ...), custom_call_target="tpu_custom_call", output_to_operand_aliasing={{}: (3, {})} | custom-call | tf_op jit(solution)/shard_map/update_columns/pallas_call | solution.py:231
  263.7 2.9 %update_columns.6.refs_3_ = f32[512,8192]{1,0:T(8,128)} custom-call(bf16[512,512]{1,0:T(8,128)(2,1)S(1)} %convolution_convert_fusion.5.refs_0_, bf16[256,2048]{1,0:T(8,128)(2,1)S(1)} %constant_dynamic-update-slice_fusion.20.refs_1_, bf16[256,2048]{1,0:T(8,128)(2,1)S(1)} %collective-permute-done.41.refs_2_, ...), custom_call_target="tpu_custom_call", output_to_operand_aliasing={{}: (3, {})} | custom-call | tf_op jit(solution)/shard_map/update_columns/pallas_call | solution.py:231
  266.6 2.9 %update_columns.7 = f32[512,8192]{1,0:T(8,128)} custom-call(bf16[512,512]{1,0:T(8,128)(2,1)S(1)} %convolution_convert_fusion.9.refs_0_, bf16[256,2048]{1,0:T(8,128)(2,1)S(1)} %constant_dynamic-update-slice_fusion.22.refs_1_, bf16[256,2048]{1,0:T(8,128)(2,1)S(1)} %collective-permute-done.40.refs_2_, ...), custom_call_target="tpu_custom_call", output_to_operand_aliasing={{}: (3, {})} | custom-call | tf_op jit(solution)/shard_map/update_columns/pallas_call | solution.py:231
  (206 shorter events, 43.5 us)
Async XLA Ops:
  7.2 84.8 %all-gather.2.cloned.1.call-start = ((), (), s32[]{:S(2)}) async-start(), calls=%async_computation | async-start | bytes 4456448 | tf_op jit(solution)/shard_map/all_gather | solution.py:271
  9.2 87.1 %collective-permute-start.10 = (bf16[512,4096]{1,0:T(8,128)(2,1)}, bf16[512,4096]{1,0:T(8,128)(2,1)}, u32[]{:S(2)}, u32[]{:S(2)}) collective-permute-start(bf16[512,4096]{1,0:T(8,128)(2,1)} %param.17), channel_id=1, source_target_pairs={{0,1},{1,0},{2,3},{3,2},{4,5},{5,4},{6,7},{7,6},{8,9},{9,8},{10,11... | collective-permute-start | bytes 12582920 | tf_op jit(solution)/shard_map/ppermute | solution.py:269
  11.8 5.7 %collective-permute-start = (f32[160,128]{1,0:T(8,128)S(1)}, f32[160,128]{1,0:T(8,128)S(1)}, u32[]{:S(2)}, u32[]{:S(2)}) collective-permute-start(f32[160,128]{1,0:T(8,128)S(1)} %get-tuple-element.161), channel_id=1, source_target_pairs={{0,2},{2,0},{4,6},{6,4},{8,10},{10,8},{12,14},{14,12},{16,18},{18,... | collective-permute-start | bytes 245768 | tf_op jit(solution)/shard_map/ppermute | solution.py:61
  14.5 5.3 %collective-permute-start.1 = (f32[160,128]{1,0:T(8,128)S(1)}, f32[160,128]{1,0:T(8,128)S(1)}, u32[]{:S(2)}, u32[]{:S(2)}) collective-permute-start(f32[160,128]{1,0:T(8,128)S(1)} %get-tuple-element.163), channel_id=1, source_target_pairs={{0,4},{2,6},{4,0},{6,2},{8,12},{10,14},{12,8},{14,10},{16,20},{18,... | collective-permute-start | bytes 245768 | tf_op jit(solution)/shard_map/ppermute | solution.py:61
  16.0 5.3 %collective-permute-start.2 = (f32[160,128]{1,0:T(8,128)S(1)}, f32[160,128]{1,0:T(8,128)S(1)}, u32[]{:S(2)}, u32[]{:S(2)}) collective-permute-start(f32[160,128]{1,0:T(8,128)S(1)} %get-tuple-element.162), channel_id=1, source_target_pairs={{0,6},{2,4},{4,2},{6,0},{8,14},{10,12},{12,10},{14,8},{16,22},{18,... | collective-permute-start | bytes 245768 | tf_op jit(solution)/shard_map/ppermute | solution.py:61
  21.4 8.3 %collective-permute-start.3 = (f32[160,128]{1,0:T(8,128)S(1)}, f32[160,128]{1,0:T(8,128)S(1)}, u32[]{:S(2)}, u32[]{:S(2)}) collective-permute-start(f32[160,128]{1,0:T(8,128)S(1)} %add_add_fusion), channel_id=1, source_target_pairs={{0,8},{2,10},{4,12},{6,14},{8,16},{10,18},{12,20},{14,22},{16,24},... | collective-permute-start | bytes 245768 | tf_op jit(solution)/shard_map/ppermute | solution.py:61
  23.0 11.0 %collective-permute-start.4 = (f32[160,128]{1,0:T(8,128)S(1)}, f32[160,128]{1,0:T(8,128)S(1)}, u32[]{:S(2)}, u32[]{:S(2)}) collective-permute-start(f32[160,128]{1,0:T(8,128)S(1)} %add_add_fusion), channel_id=1, source_target_pairs={{0,16},{2,18},{4,20},{6,22},{8,24},{10,26},{12,28},{14,30},{16,0},... | collective-permute-start | bytes 245768 | tf_op jit(solution)/shard_map/ppermute | solution.py:61
  25.6 8.4 %collective-permute-start.5 = (f32[160,128]{1,0:T(8,128)S(1)}, f32[160,128]{1,0:T(8,128)S(1)}, u32[]{:S(2)}, u32[]{:S(2)}) collective-permute-start(f32[160,128]{1,0:T(8,128)S(1)} %add_add_fusion), channel_id=1, source_target_pairs={{0,24},{2,26},{4,28},{6,30},{8,0},{10,2},{12,4},{14,6},{16,8},{18,... | collective-permute-start | bytes 245768 | tf_op jit(solution)/shard_map/ppermute | solution.py:61
  34.0 4.5 %collective-permute-start.6 = (f32[160,128]{1,0:T(8,128)S(1)}, f32[160,128]{1,0:T(8,128)S(1)}, u32[]{:S(2)}, u32[]{:S(2)}) collective-permute-start(f32[160,128]{1,0:T(8,128)S(1)} %get-tuple-element.156), channel_id=1, source_target_pairs={{0,2},{2,0},{4,6},{6,4},{8,10},{10,8},{12,14},{14,12},{16,18},{18,... | collective-permute-start | bytes 245768 | tf_op jit(solution)/shard_map/ppermute | solution.py:61
  35.2 4.4 %collective-permute-start.7 = (f32[160,128]{1,0:T(8,128)S(1)}, f32[160,128]{1,0:T(8,128)S(1)}, u32[]{:S(2)}, u32[]{:S(2)}) collective-permute-start(f32[160,128]{1,0:T(8,128)S(1)} %get-tuple-element.156), channel_id=1, source_target_pairs={{0,4},{2,6},{4,0},{6,2},{8,12},{10,14},{12,8},{14,10},{16,20},{18,... | collective-permute-start | bytes 245768 | tf_op jit(solution)/shard_map/ppermute | solution.py:61
  35.6 5.3 %collective-permute-start.8 = (f32[160,128]{1,0:T(8,128)S(1)}, f32[160,128]{1,0:T(8,128)S(1)}, u32[]{:S(2)}, u32[]{:S(2)}) collective-permute-start(f32[160,128]{1,0:T(8,128)S(1)} %get-tuple-element.156), channel_id=1, source_target_pairs={{0,6},{2,4},{4,2},{6,0},{8,14},{10,12},{12,10},{14,8},{16,22},{18,... | collective-permute-start | bytes 245768 | tf_op jit(solution)/shard_map/ppermute | solution.py:61
  41.0 1.7 collective-permute-start.9
  99.9 2.0 collective-permute-start.11
  107.4 26.0 %collective-permute-start.13 = (bf16[256,2048]{1,0:T(8,128)(2,1)S(1)}, bf16[256,2048]{1,0:T(8,128)(2,1)S(1)}, u32[]{:S(2)}, u32[]{:S(2)}) collective-permute-start(bf16[256,2048]{1,0:T(8,128)(2,1)S(1)} %convolution_convert_fusion.3), channel_id=1, source_target_pairs={{0,2},{2,0},{4,6},{6,4},{8,10},{10,8},{12,14},{14,12},{16,18},{18,... | collective-permute-start | bytes 3145736 | tf_op jit(solution)/shard_map/ppermute | solution.py:34
  109.7 25.8 %collective-permute-start.16 = (bf16[256,2048]{1,0:T(8,128)(2,1)S(1)}, bf16[256,2048]{1,0:T(8,128)(2,1)S(1)}, u32[]{:S(2)}, u32[]{:S(2)}) collective-permute-start(bf16[256,2048]{1,0:T(8,128)(2,1)S(1)} %convolution_convert_fusion.2), channel_id=1, source_target_pairs={{0,8},{2,10},{4,12},{6,14},{8,0},{10,2},{12,4},{14,6},{16,24},{18,... | collective-permute-start | bytes 3145736 | tf_op jit(solution)/shard_map/ppermute | solution.py:34
  112.2 26.1 %collective-permute-start.15 = (bf16[256,2048]{1,0:T(8,128)(2,1)S(1)}, bf16[256,2048]{1,0:T(8,128)(2,1)S(1)}, u32[]{:S(2)}, u32[]{:S(2)}) collective-permute-start(bf16[256,2048]{1,0:T(8,128)(2,1)S(1)} %convolution_convert_fusion.1), channel_id=1, source_target_pairs={{0,4},{2,6},{4,0},{6,2},{8,12},{10,14},{12,8},{14,10},{16,20},{18,... | collective-permute-start | bytes 3145736 | tf_op jit(solution)/shard_map/ppermute | solution.py:34
  114.3 41.2 %collective-permute-start.12 = (bf16[256,2048]{1,0:T(8,128)(2,1)S(1)}, bf16[256,2048]{1,0:T(8,128)(2,1)S(1)}, u32[]{:S(2)}, u32[]{:S(2)}) collective-permute-start(bf16[256,2048]{1,0:T(8,128)(2,1)S(1)} %convolution_convert_fusion), channel_id=1, source_target_pairs={{0,2},{2,0},{4,6},{6,4},{8,10},{10,8},{12,14},{14,12},{16,18},{18,... | collective-permute-start | bytes 3145736 | tf_op jit(solution)/shard_map/ppermute | solution.py:34
  133.9 14.5 %collective-permute-start.14 = (bf16[128,2048]{1,0:T(8,128)(2,1)S(1)}, bf16[128,2048]{1,0:T(8,128)(2,1)S(1)}, u32[]{:S(2)}, u32[]{:S(2)}) collective-permute-start(bf16[128,2048]{1,0:T(8,128)(2,1)S(1)} %slice.325), channel_id=1, source_target_pairs={{0,4},{2,6},{4,0},{6,2},{8,12},{10,14},{12,8},{14,10},{16,20},{18,... | collective-permute-start | bytes 1572872 | tf_op jit(solution)/shard_map/ppermute | solution.py:34
  135.9 25.1 %collective-permute-start.20 = (bf16[128,2048]{1,0:T(8,128)(2,1)S(1)}, bf16[128,2048]{1,0:T(8,128)(2,1)S(1)}, u32[]{:S(2)}, u32[]{:S(2)}) collective-permute-start(bf16[128,2048]{1,0:T(8,128)(2,1)S(1)} %slice.324), channel_id=1, source_target_pairs={{0,16},{2,18},{4,20},{6,22},{8,24},{10,26},{12,28},{14,30},{16,0},... | collective-permute-start | bytes 1572872 | tf_op jit(solution)/shard_map/ppermute | solution.py:34
  138.7 9.9 %copy-start.3 = (f32[256,2048]{1,0:T(8,128)}, f32[256,2048]{1,0:T(8,128)S(1)}, u32[]{:S(2)}) copy-start(f32[256,2048]{1,0:T(8,128)S(1)} %convert_add_fusion.1) | copy-start | bytes 6291460
  138.7 9.8 %slice-start.5 = ((f32[256,2048]{1,0:T(8,128)}), f32[128,2048]{1,0:T(8,128)S(1)}, s32[]{:S(2)}) async-start(f32[256,2048]{1,0:T(8,128)} %copy-done.5), calls=%async_computation.6 | async-start | bytes 2097152 | tf_op jit(solution)/shard_map/slice | solution.py:331
  138.7 23.8 %collective-permute-start.19 = (bf16[128,2048]{1,0:T(8,128)(2,1)S(1)}, bf16[128,2048]{1,0:T(8,128)(2,1)S(1)}, u32[]{:S(2)}, u32[]{:S(2)}) collective-permute-start(bf16[128,2048]{1,0:T(8,128)(2,1)S(1)} %slice.323), channel_id=1, source_target_pairs={{0,8},{2,10},{4,12},{6,14},{8,0},{10,2},{12,4},{14,6},{16,24},{18,... | collective-permute-start | bytes 1572872 | tf_op jit(solution)/shard_map/ppermute | solution.py:34
  148.6 18.2 %collective-permute-start.18 = (bf16[64,2048]{1,0:T(8,128)(2,1)S(1)}, bf16[64,2048]{1,0:T(8,128)(2,1)S(1)}, u32[]{:S(2)}, u32[]{:S(2)}) collective-permute-start(bf16[64,2048]{1,0:T(8,128)(2,1)S(1)} %slice.329), channel_id=1, source_target_pairs={{0,8},{2,10},{4,12},{6,14},{8,0},{10,2},{12,4},{14,6},{16,24},{18,... | collective-permute-start | bytes 786440 | tf_op jit(solution)/shard_map/ppermute | solution.py:34
  157.2 14.8 %collective-permute-start.17 = (bf16[128,2048]{1,0:T(8,128)(2,1)S(1)}, bf16[128,2048]{1,0:T(8,128)(2,1)S(1)}, u32[]{:S(2)}, u32[]{:S(2)}) collective-permute-start(bf16[128,2048]{1,0:T(8,128)(2,1)S(1)} %slice.322), channel_id=1, source_target_pairs={{0,4},{2,6},{4,0},{6,2},{8,12},{10,14},{12,8},{14,10},{16,20},{18,... | collective-permute-start | bytes 1572872 | tf_op jit(solution)/shard_map/ppermute | solution.py:34
  161.2 15.1 %collective-permute-start.24 = (bf16[64,2048]{1,0:T(8,128)(2,1)S(1)}, bf16[64,2048]{1,0:T(8,128)(2,1)S(1)}, u32[]{:S(2)}, u32[]{:S(2)}) collective-permute-start(bf16[64,2048]{1,0:T(8,128)(2,1)S(1)} %slice.328), channel_id=1, source_target_pairs={{0,4},{2,6},{4,0},{6,2},{8,12},{10,14},{12,8},{14,10},{16,20},{18,... | collective-permute-start | bytes 786440 | tf_op jit(solution)/shard_map/ppermute | solution.py:34
  162.7 15.3 %collective-permute-start.23 = (bf16[64,2048]{1,0:T(8,128)(2,1)S(1)}, bf16[64,2048]{1,0:T(8,128)(2,1)S(1)}, u32[]{:S(2)}, u32[]{:S(2)}) collective-permute-start(bf16[64,2048]{1,0:T(8,128)(2,1)S(1)} %slice.327), channel_id=1, source_target_pairs={{0,2},{2,0},{4,6},{6,4},{8,10},{10,8},{12,14},{14,12},{16,18},{18,... | collective-permute-start | bytes 786440 | tf_op jit(solution)/shard_map/ppermute | solution.py:34
  166.9 11.1 %slice-start.8 = ((f32[128,2048]{1,0:T(8,128)}), f32[64,2048]{1,0:T(8,128)S(1)}, s32[]{:S(2)}) async-start(f32[128,2048]{1,0:T(8,128)} %copy-done.8), calls=%async_computation.9 | async-start | bytes 1048576 | tf_op jit(solution)/shard_map/slice | solution.py:331
  166.9 13.2 %collective-permute-start.22 = (bf16[32,2048]{1,0:T(8,128)(2,1)S(1)}, bf16[32,2048]{1,0:T(8,128)(2,1)S(1)}, u32[]{:S(2)}, u32[]{:S(2)}) collective-permute-start(bf16[32,2048]{1,0:T(8,128)(2,1)S(1)} %slice.333), channel_id=1, source_target_pairs={{0,16},{2,18},{4,20},{6,22},{8,24},{10,26},{12,28},{14,30},{16,0},... | collective-permute-start | bytes 393224 | tf_op jit(solution)/shard_map/ppermute | solution.py:34
  172.2 9.2 %collective-permute-start.21 = (bf16[64,2048]{1,0:T(8,128)(2,1)S(1)}, bf16[64,2048]{1,0:T(8,128)(2,1)S(1)}, u32[]{:S(2)}, u32[]{:S(2)}) collective-permute-start(bf16[64,2048]{1,0:T(8,128)(2,1)S(1)} %slice.326), channel_id=1, source_target_pairs={{0,8},{2,10},{4,12},{6,14},{8,0},{10,2},{12,4},{14,6},{16,24},{18,... | collective-permute-start | bytes 786440 | tf_op jit(solution)/shard_map/ppermute | solution.py:34
  176.4 7.0 %collective-permute-start.26 = (bf16[32,2048]{1,0:T(8,128)(2,1)S(1)}, bf16[32,2048]{1,0:T(8,128)(2,1)S(1)}, u32[]{:S(2)}, u32[]{:S(2)}) collective-permute-start(bf16[32,2048]{1,0:T(8,128)(2,1)S(1)} %slice.332), channel_id=1, source_target_pairs={{0,2},{2,0},{4,6},{6,4},{8,10},{10,8},{12,14},{14,12},{16,18},{18,... | collective-permute-start | bytes 393224 | tf_op jit(solution)/shard_map/ppermute | solution.py:34
  178.2 14.4 %collective-permute-start.29 = (bf16[32,2048]{1,0:T(8,128)(2,1)S(1)}, bf16[32,2048]{1,0:T(8,128)(2,1)S(1)}, u32[]{:S(2)}, u32[]{:S(2)}) collective-permute-start(bf16[32,2048]{1,0:T(8,128)(2,1)S(1)} %slice.331), channel_id=1, source_target_pairs={{0,16},{2,18},{4,20},{6,22},{8,24},{10,26},{12,28},{14,30},{16,0},... | collective-permute-start | bytes 393224 | tf_op jit(solution)/shard_map/ppermute | solution.py:34
  180.4 16.9 %collective-permute-start.28 = (bf16[32,2048]{1,0:T(8,128)(2,1)S(1)}, bf16[32,2048]{1,0:T(8,128)(2,1)S(1)}, u32[]{:S(2)}, u32[]{:S(2)}) collective-permute-start(bf16[32,2048]{1,0:T(8,128)(2,1)S(1)} %get-tuple-element.109), channel_id=1, source_target_pairs={{0,16},{2,18},{4,20},{6,22},{8,24},{10,26},{12,28},{14,30},{16,0},... | collective-permute-start | bytes 393224 | tf_op jit(solution)/shard_map/ppermute | solution.py:34
  181.5 19.5 %collective-permute-start.25 = (bf16[32,2048]{1,0:T(8,128)(2,1)S(1)}, bf16[32,2048]{1,0:T(8,128)(2,1)S(1)}, u32[]{:S(2)}, u32[]{:S(2)}) collective-permute-start(bf16[32,2048]{1,0:T(8,128)(2,1)S(1)} %slice.330), channel_id=1, source_target_pairs={{0,16},{2,18},{4,20},{6,22},{8,24},{10,26},{12,28},{14,30},{16,0},... | collective-permute-start | bytes 393224 | tf_op jit(solution)/shard_map/ppermute | solution.py:34
  183.7 13.7 %collective-permute-start.27 = (bf16[32,2048]{1,0:T(8,128)(2,1)S(1)}, bf16[32,2048]{1,0:T(8,128)(2,1)S(1)}, u32[]{:S(2)}, u32[]{:S(2)}) collective-permute-start(bf16[32,2048]{1,0:T(8,128)(2,1)S(1)} %get-tuple-element.111), channel_id=1, source_target_pairs={{0,2},{2,0},{4,6},{6,4},{8,10},{10,8},{12,14},{14,12},{16,18},{18,... | collective-permute-start | bytes 393224 | tf_op jit(solution)/shard_map/ppermute | solution.py:34
  192.8 11.9 %collective-permute-start.33 = (bf16[32,2048]{1,0:T(8,128)(2,1)S(1)}, bf16[32,2048]{1,0:T(8,128)(2,1)S(1)}, u32[]{:S(2)}, u32[]{:S(2)}) collective-permute-start(bf16[32,2048]{1,0:T(8,128)(2,1)S(1)} %get-tuple-element.115), channel_id=1, source_target_pairs={{0,16},{2,18},{4,20},{6,22},{8,24},{10,26},{12,28},{14,30},{16,0},... | collective-permute-start | bytes 393224 | tf_op jit(solution)/shard_map/ppermute | solution.py:34
  197.3 12.5 %collective-permute-start.32 = (bf16[64,2048]{1,0:T(8,128)(2,1)S(1)}, bf16[64,2048]{1,0:T(8,128)(2,1)S(1)}, u32[]{:S(2)}, u32[]{:S(2)}) collective-permute-start(bf16[64,2048]{1,0:T(8,128)(2,1)S(1)} %constant_dynamic-update-slice_fusion), channel_id=1, source_target_pairs={{0,8},{2,10},{4,12},{6,14},{8,0},{10,2},{12,4},{14,6},{16,24},{18,... | collective-permute-start | bytes 786440 | tf_op jit(solution)/shard_map/ppermute | solution.py:34
  197.4 13.0 %collective-permute-start.31 = (bf16[64,2048]{1,0:T(8,128)(2,1)S(1)}, bf16[64,2048]{1,0:T(8,128)(2,1)S(1)}, u32[]{:S(2)}, u32[]{:S(2)}) collective-permute-start(bf16[64,2048]{1,0:T(8,128)(2,1)S(1)} %constant_dynamic-update-slice_fusion.2), channel_id=1, source_target_pairs={{0,4},{2,6},{4,0},{6,2},{8,12},{10,14},{12,8},{14,10},{16,20},{18,... | collective-permute-start | bytes 786440 | tf_op jit(solution)/shard_map/ppermute | solution.py:34
  201.2 9.3 %collective-permute-start.30 = (bf16[32,2048]{1,0:T(8,128)(2,1)S(1)}, bf16[32,2048]{1,0:T(8,128)(2,1)S(1)}, u32[]{:S(2)}, u32[]{:S(2)}) collective-permute-start(bf16[32,2048]{1,0:T(8,128)(2,1)S(1)} %get-tuple-element.121), channel_id=1, source_target_pairs={{0,16},{2,18},{4,20},{6,22},{8,24},{10,26},{12,28},{14,30},{16,0},... | collective-permute-start | bytes 393224 | tf_op jit(solution)/shard_map/ppermute | solution.py:34
  204.7 8.4 %collective-permute-start.36 = (bf16[64,2048]{1,0:T(8,128)(2,1)S(1)}, bf16[64,2048]{1,0:T(8,128)(2,1)S(1)}, u32[]{:S(2)}, u32[]{:S(2)}) collective-permute-start(bf16[64,2048]{1,0:T(8,128)(2,1)S(1)} %constant_dynamic-update-slice_fusion.4), channel_id=1, source_target_pairs={{0,2},{2,0},{4,6},{6,4},{8,10},{10,8},{12,14},{14,12},{16,18},{18,... | collective-permute-start | bytes 786440 | tf_op jit(solution)/shard_map/ppermute | solution.py:34
  209.8 10.6 %collective-permute-start.35 = (bf16[128,2048]{1,0:T(8,128)(2,1)S(1)}, bf16[128,2048]{1,0:T(8,128)(2,1)S(1)}, u32[]{:S(2)}, u32[]{:S(2)}) collective-permute-start(bf16[128,2048]{1,0:T(8,128)(2,1)S(1)} %constant_dynamic-update-slice_fusion.6), channel_id=1, source_target_pairs={{0,4},{2,6},{4,0},{6,2},{8,12},{10,14},{12,8},{14,10},{16,20},{18,... | collective-permute-start | bytes 1572872 | tf_op jit(solution)/shard_map/ppermute | solution.py:34
  210.4 22.0 %collective-permute-start.39 = (bf16[128,2048]{1,0:T(8,128)(2,1)S(1)}, bf16[128,2048]{1,0:T(8,128)(2,1)S(1)}, u32[]{:S(2)}, u32[]{:S(2)}) collective-permute-start(bf16[128,2048]{1,0:T(8,128)(2,1)S(1)} %constant_dynamic-update-slice_fusion.8), channel_id=1, source_target_pairs={{0,16},{2,18},{4,20},{6,22},{8,24},{10,26},{12,28},{14,30},{16,0},... | collective-permute-start | bytes 1572872 | tf_op jit(solution)/shard_map/ppermute | solution.py:34
  210.6 17.9 %collective-permute-start.34 = (bf16[64,2048]{1,0:T(8,128)(2,1)S(1)}, bf16[64,2048]{1,0:T(8,128)(2,1)S(1)}, u32[]{:S(2)}, u32[]{:S(2)}) collective-permute-start(bf16[64,2048]{1,0:T(8,128)(2,1)S(1)} %constant_dynamic-update-slice_fusion.10), channel_id=1, source_target_pairs={{0,8},{2,10},{4,12},{6,14},{8,0},{10,2},{12,4},{14,6},{16,24},{18,... | collective-permute-start | bytes 786440 | tf_op jit(solution)/shard_map/ppermute | solution.py:34
  213.2 28.3 %collective-permute-start.38 = (bf16[128,2048]{1,0:T(8,128)(2,1)S(1)}, bf16[128,2048]{1,0:T(8,128)(2,1)S(1)}, u32[]{:S(2)}, u32[]{:S(2)}) collective-permute-start(bf16[128,2048]{1,0:T(8,128)(2,1)S(1)} %constant_dynamic-update-slice_fusion.12), channel_id=1, source_target_pairs={{0,8},{2,10},{4,12},{6,14},{8,0},{10,2},{12,4},{14,6},{16,24},{18,... | collective-permute-start | bytes 1572872 | tf_op jit(solution)/shard_map/ppermute | solution.py:34
  220.5 25.4 %collective-permute-start.43 = (bf16[256,2048]{1,0:T(8,128)(2,1)S(1)}, bf16[256,2048]{1,0:T(8,128)(2,1)S(1)}, u32[]{:S(2)}, u32[]{:S(2)}) collective-permute-start(bf16[256,2048]{1,0:T(8,128)(2,1)S(1)} %constant_dynamic-update-slice_fusion.14.refs_1_), channel_id=1, source_target_pairs={{0,2},{2,0},{4,6},{6,4},{8,10},{10,8},{12,14},{14,12},{16,18},{18,... | collective-permute-start | bytes 3145736 | tf_op jit(solution)/shard_map/ppermute | solution.py:34
  228.6 14.4 %collective-permute-start.37 = (bf16[128,2048]{1,0:T(8,128)(2,1)S(1)}, bf16[128,2048]{1,0:T(8,128)(2,1)S(1)}, u32[]{:S(2)}, u32[]{:S(2)}) collective-permute-start(bf16[128,2048]{1,0:T(8,128)(2,1)S(1)} %constant_dynamic-update-slice_fusion.16), channel_id=1, source_target_pairs={{0,4},{2,6},{4,0},{6,2},{8,12},{10,14},{12,8},{14,10},{16,20},{18,... | collective-permute-start | bytes 1572872 | tf_op jit(solution)/shard_map/ppermute | solution.py:34
  232.5 28.3 %collective-permute-start.42 = (bf16[256,2048]{1,0:T(8,128)(2,1)S(1)}, bf16[256,2048]{1,0:T(8,128)(2,1)S(1)}, u32[]{:S(2)}, u32[]{:S(2)}) collective-permute-start(bf16[256,2048]{1,0:T(8,128)(2,1)S(1)} %constant_dynamic-update-slice_fusion.18.refs_1_), channel_id=1, source_target_pairs={{0,8},{2,10},{4,12},{6,14},{8,0},{10,2},{12,4},{14,6},{16,24},{18,... | collective-permute-start | bytes 3145736 | tf_op jit(solution)/shard_map/ppermute | solution.py:34
  241.5 19.3 %collective-permute-start.41 = (bf16[256,2048]{1,0:T(8,128)(2,1)S(1)}, bf16[256,2048]{1,0:T(8,128)(2,1)S(1)}, u32[]{:S(2)}, u32[]{:S(2)}) collective-permute-start(bf16[256,2048]{1,0:T(8,128)(2,1)S(1)} %constant_dynamic-update-slice_fusion.20.refs_1_), channel_id=1, source_target_pairs={{0,4},{2,6},{4,0},{6,2},{8,12},{10,14},{12,8},{14,10},{16,20},{18,... | collective-permute-start | bytes 3145736 | tf_op jit(solution)/shard_map/ppermute | solution.py:34
  243.1 23.5 %collective-permute-start.40 = (bf16[256,2048]{1,0:T(8,128)(2,1)S(1)}, bf16[256,2048]{1,0:T(8,128)(2,1)S(1)}, u32[]{:S(2)}, u32[]{:S(2)}) collective-permute-start(bf16[256,2048]{1,0:T(8,128)(2,1)S(1)} %constant_dynamic-update-slice_fusion.22.refs_1_), channel_id=1, source_target_pairs={{0,2},{2,0},{4,6},{6,4},{8,10},{10,8},{12,14},{14,12},{16,18},{18,... | collective-permute-start | bytes 3145736 | tf_op jit(solution)/shard_map/ppermute | solution.py:34
  (22 other events, 105.8 us)
Sparse Core Ops, SparseCore 0:
  11.4 80.5 all-gather.1

commit v3 on v2

--- a/solution.py
+++ b/solution.py
@@ -24,6 +24,9 @@
 
 GROUPS = ((2, (0, 1, 2, 3)), (2, (2, 3, 1, 0)), (2, (1, 2, 0, 3)), (2, (0, 1, 2, 3)))
 STEPS = ((0, 0), (1, 0), (2, 0), (3, 0), (0, 1), (1, 1), (2, 1), (0, 2), (3, 1), (1, 2), (2, 2), (0, 3), (3, 2), (1, 3), (2, 3), (0, 4), (3, 3), (1, 4), (2, 4), (0, 5), (1, 5), (3, 4), (2, 5), (0, 6), (1, 6), (3, 5), (2, 6), (0, 7), (3, 6), (1, 7), (2, 7), (3, 7), (0, 8), (1, 8), (2, 8), (3, 8))
+
+
+GATHER = ((0, 1, 2, 3), (1, 0, 2, 3), (2, 1, 0, 3), (2, 0, 1, 3))
 
 
 def flip_pairs(devices, bit):
@@ -162,43 +165,139 @@
     )(packed)
 
 
-def summed_gram(sketch, dims, own, core):
+def gram_and_sketch(sketch, half, dims, own, core):
+    devices = math.prod(dims)
+    bits = devices.bit_length() - 1
     size = sketch.shape[1]
     blocks = lower_blocks(size)
-    half = len(blocks) // 2
+    split = len(blocks) // 2
     gram = jnp.dot(sketch.T, sketch, precision=HIGHEST, preferred_element_type=F32)
     tiles = [
         gram[i * BLOCK : (i + 1) * BLOCK, j * BLOCK : (j + 1) * BLOCK] for i, j in blocks
     ]
     mine = jnp.where(
-        core == 0, jnp.concatenate(tiles[:half]), jnp.concatenate(tiles[half:])
+        core == 0, jnp.concatenate(tiles[:split]), jnp.concatenate(tiles[split:])
     )
     plane = dims[1] * dims[2]
     share = mine.shape[0] // plane
     at_of = lambda a, b: ((own[1] + a) % dims[1] * dims[2] + (own[2] + b) % dims[2]) * share
     shifts = list(itertools.product(range(dims[1]), range(dims[2])))
     part = lambda a, b: lax.dynamic_slice_in_dim(mine, at_of(a, b), share, 0)
+    outgoing = [part(a, b) for a, b in shifts[1:]]
     total = part(0, 0)
-    arrived = [send(part(a, b), dims, (0, a, b)) for a, b in shifts[1:]]
+    arrived = [send(piece, dims, (0, a, b)) for (a, b), piece in zip(shifts[1:], outgoing)]
+
+    groups = gather_groups(half.shape[0], bits)
+    tall = half.shape[0] // len(groups)
+    (half,) = after(outgoing[-1], (half,))
+    gathered = [half[None, g * tall : (g + 1) * tall] for g in range(len(groups))]
+    moving = [flip(rows, devices, order[-1]) for rows, order in zip(gathered, groups)]
+
+    def widen(stage, token):
+        for g, order in enumerate(groups):
+            rows, piece = after(token, (gathered[g], moving[g]))
+            token = gathered[g] = jnp.concatenate([rows, piece])
+            moving[g] = flip(token, devices, order[-1 - stage])
+        return token
+
+    arrived = after(half, arrived)
     for piece in arrived:
         total = total + piece
     arrived = [send(total, dims, (by, 0, 0)) for by in range(1, dims[0])]
-    places = jnp.stack([total] + arrived)
+    token = widen(1, total)
+    arrived = after(token, arrived)
+    places = jnp.stack([total, *arrived])
     order = [(own[0] - z) % dims[0] for z in range(dims[0])]
     total = functools.reduce(
         jnp.add, [lax.dynamic_index_in_dim(places, at, 0, keepdims=False) for at in order]
     )
+    arrived = [send(total, dims, (0, -a, -b)) for a, b in shifts[1:]]
+    token = widen(2, total)
+    arrived = after(token, arrived)
     whole = lax.dynamic_update_slice_in_dim(
         jnp.zeros_like(mine), total, at_of(0, 0), 0
     )
-    arrived = [send(total, dims, (0, -a, -b)) for a, b in shifts[1:]]
     for (a, b), piece in zip(shifts[1:], arrived):
         whole = lax.dynamic_update_slice_in_dim(whole, piece, at_of(a, b), 0)
     other = lax.ppermute(whole, "tensor", [(0, 1), (1, 0)])
-    return (
-        jnp.where(core == 0, jnp.concatenate([whole, other]), jnp.concatenate([other, whole])),
-        blocks,
-    )
+    token = whole
+    for stage in range(3, bits):
+        token = widen(stage, token)
+    whole, other = after(token, (whole, other))
+    packed = jnp.where(
+        core == 0, jnp.concatenate([whole, other]), jnp.concatenate([other, whole])
+    )
+    return packed, blocks, groups, gathered, moving
+
+
+def gather_groups(rows, bits):
+    count = max(1, min(len(GATHER), rows // BLOCK))
+    return [order + tuple(range(4, bits)) for order in GATHER[:count]]
+
+
+def mix_kernel(groups, limit, table_ref, left_ref, right_ref, *refs):
+    at = pl.program_id(0)
+    out_ref = refs[-1]
+    tall = refs[0].shape[1]
+    total = None
+    for side, source in enumerate((left_ref, right_ref)):
+        for g in range(groups):
+            near, far = refs[2 * (side * groups + g)], refs[2 * (side * groups + g) + 1]
+            place = table_ref[side, g, at]
+            rows = jnp.where(place < limit, near[0], far[0])
+            term = jnp.dot(
+                source[:, g * tall : (g + 1) * tall], rows, preferred_element_type=F32
+            )
+            total = term if total is None else total + term
+
+    @pl.when(at == 0)
+    def _():
+        out_ref[...] = total
+
+    @pl.when(at > 0)
+    def _():
+        out_ref[...] += total
+
+
+def mix(left, right, near, far, groups, dp, core):
+    limit, tall, cols = near[0].shape
+    bits = limit.bit_length()
+    count = len(groups)
+    blocks = jnp.arange(limit, dtype=jnp.int32)
+    table = []
+    for side in (core, 1 - core):
+        apart = (side * limit + blocks) ^ dp
+        row = []
+        for order in groups:
+            place = jnp.zeros_like(apart)
+            for bit in order:
+                place = place * 2 + ((apart >> bit) & 1)
+            row.append(place)
+        table.append(jnp.stack(row))
+    table = jnp.stack(table)
+    block = left.shape[1] // limit
+    in_specs = [pl.BlockSpec((left.shape[0], block), lambda i, t: (0, i))] * 2
+    operands = [left, right]
+    for side in range(2):
+        for g in range(count):
+            spec = pl.BlockSpec(
+                (1, tall, cols),
+                lambda i, t, side=side, g=g: (t[side, g, i] % limit, 0, 0),
+            )
+            in_specs += [spec, spec]
+            operands += [near[g], far[g]]
+    return pl.pallas_call(
+        functools.partial(mix_kernel, count, limit),
+        grid_spec=pltpu.PrefetchScalarGridSpec(
+            num_scalar_prefetch=1,
+            grid=(limit,),
+            in_specs=in_specs,
+            out_specs=pl.BlockSpec((left.shape[0], cols), lambda i, t: (0, 0)),
+        ),
+        out_shape=jax.ShapeDtypeStruct((left.shape[0], cols), F32),
+        compiler_params=pltpu.CompilerParams(vmem_limit_bytes=VMEM_LIMIT),
+        name="mix",
+    )(table, *operands)
 
 
 def update_kernel(scale, count, *refs):
@@ -268,11 +367,10 @@
 
     beside = lax.ppermute(activations, "tensor", [(0, 1), (1, 0)])
     half = lax.dynamic_slice_in_dim(sketch, core * (rank // 2), rank // 2, 1).astype(BF16)
-    sketch_half = lax.all_gather(half, "dp", axis=0, tiled=True)
-    mid = sketch_half.shape[0] // 2
-    part = lambda at: lax.dynamic_slice_in_dim(sketch_half, at * mid, mid, 0)
-    mixed_half = jnp.dot(activations, part(core), preferred_element_type=F32)
-    mixed_half = mixed_half + jnp.dot(beside, part(1 - core), preferred_element_type=F32)
+    packed, blocks, groups, near, far = gram_and_sketch(sketch, half, dims, own, core)
+    inverse = inverse_of_factor(packed, blocks, rank)
+    *far, activations = after(inverse, (*far, activations))
+    mixed_half = mix(activations, beside, near, far, groups, dp, core)
     mixed_other = lax.ppermute(mixed_half, "tensor", [(0, 1), (1, 0)])
     mixed = jnp.where(
         core == 0,
@@ -280,23 +378,9 @@
         jnp.concatenate([mixed_other, mixed_half], axis=1),
     )
 
-    packed, blocks = summed_gram(sketch, dims, own, core)
-    inverse = inverse_of_factor(packed, blocks, rank)
-    own_rows = dot_nt(sketch, inverse).astype(BF16)
-    projected = dot_nt(inverse, mixed).astype(BF16)
-
     orders = [order + tuple(range(4, bits)) for _, order in GROUPS]
-    selections = {}
-    for order in orders:
-        if order not in selections:
-            pick = selection(devices, dp, order, rank)
-            selections[order] = (
-                jnp.dot(pick, projected, preferred_element_type=F32).astype(BF16),
-                lax.dot_general(
-                    own_rows, pick, (((1,), (1,)), ((), ())), preferred_element_type=F32
-                ).astype(BF16),
-            )
-
+    picks = {order: selection(devices, dp, order, rank) for order in orders}
+    projected, weights = {}, {}
     update_scale = math.sqrt(depth / rank)
     eighth = width // 8
     starts = [sum(share for share, _ in GROUPS[:g]) * eighth for g in range(len(GROUPS))]
@@ -312,12 +396,36 @@
     ]
     for g, step in steps:
         order = orders[g]
+        if step == 1 and not weights:
+            rows, factor = after(token, (sketch, inverse))
+            own_rows = dot_nt(rows, factor).astype(BF16)
+            for each, pick in picks.items():
+                weights[each] = lax.dot_general(
+                    own_rows, pick, (((1,), (1,)), ((), ())), preferred_element_type=F32
+                ).astype(BF16)
+            token = tuple(weights.values())
         cols = GROUPS[g][0] * eighth
         start = starts[g]
         columns = slice(start, start + cols)
         if step == 0:
             size = rank // 2
-            left, grads = after(token, (selections[order][0], out_grads))
+            factor, grads = after(token, (inverse, out_grads))
+            if order not in projected:
+                turned = lax.dot_general(
+                    picks[order].astype(F32),
+                    factor,
+                    (((1,), (0,)), ((), ())),
+                    precision=lax.Precision.HIGH,
+                    preferred_element_type=F32,
+                )
+                projected[order] = lax.dot_general(
+                    turned,
+                    mixed,
+                    (((1,), (1,)), ((), ())),
+                    precision=lax.Precision.HIGH,
+                    preferred_element_type=F32,
+                ).astype(BF16)
+            left = projected[order]
             outgoing = jnp.dot(
                 left[size:], grads[:, columns], preferred_element_type=F32
             ).astype(BF16)
@@ -351,7 +459,7 @@
         else:
             pieces = after(token, (kept[g], arriving[g]))
             update = update_columns(
-                selections[order][1], pieces, update, start, width, update_scale
+                weights[order], pieces, update, start, width, update_scale
             )
             continue
         arriving[g] = flip(outgoing, devices, bit)

time: 277 us -> 265 us (0.957)
  waiting for transfers between devices: 144 us -> 123 us
  starting transfers between devices: 47.4 us -> 63.3 us
  between operations: 15.2 us -> 2.16 us
  Pallas kernels: 36.6 us -> 45.6 us
    all_gather x1 -> x0, waiting for transfers between devices: 22.5 us -> none  [local(): sketch_half = lax.all_gather(half, 'dp', axis=0, tiled=True)]
    ppermute x32 -> x48, starting transfers between devices: 33.3 us -> 49.6 us  [flip(): return lax.ppermute(value, 'dp', flip_pairs(devices, bit))]
    ppermute x32 -> x48, waiting for transfers between devices: 105 us -> 120 us  [flip(): return lax.ppermute(value, 'dp', flip_pairs(devices, bit))]
    ppermute x9, waiting for transfers between devices: 15.1 us -> 1.51 us  [send(): return lax.ppermute(value, 'dp', shift_pairs(dims, shift))]
    pallas_call x0 -> x1, Pallas kernels: none -> 9.11 us  [mix(): pl.pallas_call(functools.partial(mix_kernel, count, limit), grid_spec=plt...]
    dot_general x6 -> x7, matrix products: 11.2 us -> 7.32 us  [the longest x3 3.13 us: local(): lax.dot_general(turned, mixed, (((1,), (1,)), ((), ())), precision=lax.Pr...]
  transfers between devices with their start and end apart: 45 -> 60, of which waited for: 29 -> 30; matrix products, arithmetic and copies ran while one was open for 8% -> 7% of each run, Pallas kernels for 12% -> 13%
where the time goes in v3:
time: 265 us; the launch traced here: 264 us
  waiting for transfers between devices  123 us (46%)
  starting transfers between devices  63.3 us (24%)
  Pallas kernels  45.6 us (17%)
  matrix products  20.6 us (8%)
  other arithmetic  5.84 us (2%)
  local copies, waits for them, and re-layouts  4.25 us (2%)
    ppermute x48, waiting for transfers between devices, flip(): return lax.ppermute(value, 'dp', flip_pairs(devices, bit))  120 us
    ppermute x48, starting transfers between devices, flip(): return lax.ppermute(value, 'dp', flip_pairs(devices, bit))  49.6 us
    pallas_call x1, Pallas kernels, inverse_of_factor(): pl.pallas_call(functools.partial(factor_kernel, blocks), out_shape=jax.Sh...  24.8 us
    ppermute x9, starting transfers between devices, send(): return lax.ppermute(value, 'dp', shift_pairs(dims, shift))  13.6 us
    pallas_call x4, Pallas kernels, update_columns(): pl.pallas_call(functools.partial(update_kernel, scale, len(pieces)), grid...  11.7 us
    pallas_call x1, Pallas kernels, mix(): pl.pallas_call(functools.partial(mix_kernel, count, limit), grid_spec=plt...  9.11 us
  transfers between devices with their start and end apart: 60, of which 30 were waited for; matrix products, arithmetic and copies ran while one was open for 7% of the time, Pallas kernels for 13%

profile of v3, /device:TPU:0, one launch (start us, length us, event | category | flops | bytes accessed | tf_op | source)
XLA Modules:
  0.0 264.3 jit_solution(8810087347840240254)
XLA Ops:
  1.9 1.9 fusion.43
  4.0 3.0 %collective-permute-start = (f32[160,128]{1,0:T(8,128)S(1)}, f32[160,128]{1,0:T(8,128)S(1)}, u32[]{:S(2)}, u32[]{:S(2)}) collective-permute-start(f32[160,128]{1,0:T(8,128)S(1)} %get-tuple-element.251), channel_id=1, source_target_pairs={{0,2},{2,0},{4,6},{6,4},{8,10},{10,8},{12,14},{14,12},{16,18},{18,... | collective-permute-start | bytes 245768 | tf_op jit(solution)/shard_map/ppermute | solution.py:64
  7.0 1.5 collective-permute-start.1
  8.6 3.1 %collective-permute-start.9 = (bf16[1,128,256]{2,1,0:T(8,128)(2,1)S(1)}, bf16[1,128,256]{2,1,0:T(8,128)(2,1)S(1)}, u32[]{:S(2)}, u32[]{:S(2)}) collective-permute-start(bf16[1,128,256]{2,1,0:T(8,128)(2,1)S(1)} %get-tuple-element.119), channel_id=1, source_target_pairs={{0,16},{2,18},{4,20},{6,22},{8,24},{10,26},{12,28},{14,30},{16,0},... | collective-permute-start | bytes 196616 | tf_op jit(solution)/shard_map/ppermute | solution.py:37
  12.5 2.8 %collective-permute-start.7 = (bf16[1,128,256]{2,1,0:T(8,128)(2,1)S(1)}, bf16[1,128,256]{2,1,0:T(8,128)(2,1)S(1)}, u32[]{:S(2)}, u32[]{:S(2)}) collective-permute-start(bf16[1,128,256]{2,1,0:T(8,128)(2,1)S(1)} %get-tuple-element.123), channel_id=1, source_target_pairs={{0,16},{2,18},{4,20},{6,22},{8,24},{10,26},{12,28},{14,30},{16,0},... | collective-permute-start | bytes 196616 | tf_op jit(solution)/shard_map/ppermute | solution.py:37
  16.4 3.4 %collective-permute-start.3 = (f32[160,128]{1,0:T(8,128)S(1)}, f32[160,128]{1,0:T(8,128)S(1)}, u32[]{:S(2)}, u32[]{:S(2)}) collective-permute-start(f32[160,128]{1,0:T(8,128)S(1)} %add_add_fusion), channel_id=1, source_target_pairs={{0,8},{2,10},{4,12},{6,14},{8,16},{10,18},{12,20},{14,22},{16,24},... | collective-permute-start | bytes 245768 | tf_op jit(solution)/shard_map/ppermute | solution.py:64
  19.9 3.4 %collective-permute-done.8 = bf16[1,128,256]{2,1,0:T(8,128)(2,1)S(1)} collective-permute-done((bf16[1,128,256]{2,1,0:T(8,128)(2,1)S(1)}, bf16[1,128,256]{2,1,0:T(8,128)(2,1)S(1)}, u32[]{:S(2)}, u32[]{:S(2)}) %collective-permute-start.8) | collective-permute-done | bytes 65568 | tf_op jit(solution)/shard_map/ppermute | solution.py:37
  23.8 2.6 collective-permute-done.7
  27.0 1.6 collective-permute-done.6
  28.7 2.1 collective-permute-start.15
  32.3 1.5 collective-permute-start.13
  36.7 1.6 collective-permute-start.11
  39.7 1.6 collective-permute-start.21
  46.0 3.6 %collective-permute-done.21 = bf16[4,128,256]{2,1,0:T(8,128)(2,1)S(1)} collective-permute-done((bf16[4,128,256]{2,1,0:T(8,128)(2,1)S(1)}, bf16[4,128,256]{2,1,0:T(8,128)(2,1)S(1)}, u32[]{:S(2)}, u32[]{:S(2)}) %collective-permute-start.21) | collective-permute-done | bytes 262176 | tf_op jit(solution)/shard_map/ppermute | solution.py:37
  51.3 2.7 %collective-permute-done.19 = bf16[4,128,256]{2,1,0:T(8,128)(2,1)S(1)} collective-permute-done((bf16[4,128,256]{2,1,0:T(8,128)(2,1)S(1)}, bf16[4,128,256]{2,1,0:T(8,128)(2,1)S(1)}, u32[]{:S(2)}, u32[]{:S(2)}) %collective-permute-start.19) | collective-permute-done | bytes 262176 | tf_op jit(solution)/shard_map/ppermute | solution.py:37
  55.1 2.1 collective-permute-start.25
  57.3 24.8 %inverse_factor.1 = f32[512,512]{1,0:T(8,128)S(1)} custom-call(f32[1280,128]{1,0:T(8,128)S(1)} %maximum_select_fusion.1.packed_ref), custom_call_target="tpu_custom_call" | custom-call | tf_op jit(solution)/shard_map/inverse_factor/pallas_call | solution.py:157
  82.2 9.1 %mix.1 = f32[512,256]{1,0:T(8,128)S(1)} custom-call(s32[2,4,8]{2,1,0:T(4,128)S(1)} %pad_add_fusion.table_ref, bf16[512,4096]{1,0:T(8,128)(2,1)S(1)} %copy-done.2, bf16[512,4096]{1,0:T(8,128)(2,1)} %collective-permute-done.26.right_ref, bf16[8,128,256]{2,1,0:T(8,128)(2,1)S(1)} %constant_dynamic-update-slice_fusion.21.refs_0_.refs_8_, ...), custom_call_target="tpu_custom_call" | custom-call | tf_op jit(solution)/shard_map/mix/pallas_call | solution.py:289
  94.3 2.5 convolution_convert_fusion.3
  98.7 2.3 fusion.6
  107.3 1.9 convolution_convert_fusion.7
  114.8 13.1 %collective-permute-done.29 = bf16[256,2048]{1,0:T(8,128)(2,1)S(1)} collective-permute-done((bf16[256,2048]{1,0:T(8,128)(2,1)S(1)}, bf16[256,2048]{1,0:T(8,128)(2,1)S(1)}, u32[]{:S(2)}, u32[]{:S(2)}) %collective-permute-start.29) | collective-permute-done | bytes 1048608 | tf_op jit(solution)/shard_map/ppermute | solution.py:37
  129.6 5.8 %collective-permute-done.32 = bf16[256,2048]{1,0:T(8,128)(2,1)S(1)} collective-permute-done((bf16[256,2048]{1,0:T(8,128)(2,1)S(1)}, bf16[256,2048]{1,0:T(8,128)(2,1)S(1)}, u32[]{:S(2)}, u32[]{:S(2)}) %collective-permute-start.32) | collective-permute-done | bytes 1048608 | tf_op jit(solution)/shard_map/ppermute | solution.py:37
  137.7 1.8 collective-permute-start.35
  139.5 7.2 %collective-permute-done.30 = bf16[128,2048]{1,0:T(8,128)(2,1)S(1)} collective-permute-done((bf16[128,2048]{1,0:T(8,128)(2,1)S(1)}, bf16[128,2048]{1,0:T(8,128)(2,1)S(1)}, u32[]{:S(2)}, u32[]{:S(2)}) %collective-permute-start.30) | collective-permute-done | bytes 524320 | tf_op jit(solution)/shard_map/ppermute | solution.py:37
  146.9 1.7 collective-permute-start.34
  152.4 8.5 %collective-permute-done.36 = bf16[128,2048]{1,0:T(8,128)(2,1)S(1)} collective-permute-done((bf16[128,2048]{1,0:T(8,128)(2,1)S(1)}, bf16[128,2048]{1,0:T(8,128)(2,1)S(1)}, u32[]{:S(2)}, u32[]{:S(2)}) %collective-permute-start.36) | collective-permute-done | bytes 524320 | tf_op jit(solution)/shard_map/ppermute | solution.py:37
  162.0 1.7 collective-permute-done.35
  164.5 2.7 %collective-permute-done.34 = bf16[64,2048]{1,0:T(8,128)(2,1)S(1)} collective-permute-done((bf16[64,2048]{1,0:T(8,128)(2,1)S(1)}, bf16[64,2048]{1,0:T(8,128)(2,1)S(1)}, u32[]{:S(2)}, u32[]{:S(2)}) %collective-permute-start.34) | collective-permute-done | bytes 262176 | tf_op jit(solution)/shard_map/ppermute | solution.py:37
  167.7 2.5 collective-permute-start.37
  172.8 2.1 collective-permute-done.38
  175.1 5.7 %collective-permute-done.37 = bf16[64,2048]{1,0:T(8,128)(2,1)S(1)} collective-permute-done((bf16[64,2048]{1,0:T(8,128)(2,1)S(1)}, bf16[64,2048]{1,0:T(8,128)(2,1)S(1)}, u32[]{:S(2)}, u32[]{:S(2)}) %collective-permute-start.37) | collective-permute-done | bytes 262176 | tf_op jit(solution)/shard_map/ppermute | solution.py:37
  181.6 6.8 %collective-permute-done.45 = bf16[32,2048]{1,0:T(8,128)(2,1)S(1)} collective-permute-done((bf16[32,2048]{1,0:T(8,128)(2,1)S(1)}, bf16[32,2048]{1,0:T(8,128)(2,1)S(1)}, u32[]{:S(2)}, u32[]{:S(2)}) %collective-permute-start.45) | collective-permute-done | bytes 131104 | tf_op jit(solution)/shard_map/ppermute | solution.py:37
  188.7 2.5 collective-permute-done.44
  192.7 4.2 %collective-permute-done.41 = bf16[32,2048]{1,0:T(8,128)(2,1)S(1)} collective-permute-done((bf16[32,2048]{1,0:T(8,128)(2,1)S(1)}, bf16[32,2048]{1,0:T(8,128)(2,1)S(1)}, u32[]{:S(2)}, u32[]{:S(2)}) %collective-permute-start.41) | collective-permute-done | bytes 131104 | tf_op jit(solution)/shard_map/ppermute | solution.py:37
  197.2 2.6 collective-permute-done.49
  200.6 3.3 %collective-permute-done.48 = bf16[64,2048]{1,0:T(8,128)(2,1)S(1)} collective-permute-done((bf16[64,2048]{1,0:T(8,128)(2,1)S(1)}, bf16[64,2048]{1,0:T(8,128)(2,1)S(1)}, u32[]{:S(2)}, u32[]{:S(2)}) %collective-permute-start.48) | collective-permute-done | bytes 262176 | tf_op jit(solution)/shard_map/ppermute | solution.py:37
  205.1 2.4 collective-permute-start.50
  207.7 7.1 %collective-permute-done.51 = bf16[128,2048]{1,0:T(8,128)(2,1)S(1)} collective-permute-done((bf16[128,2048]{1,0:T(8,128)(2,1)S(1)}, bf16[128,2048]{1,0:T(8,128)(2,1)S(1)}, u32[]{:S(2)}, u32[]{:S(2)}) %collective-permute-start.51) | collective-permute-done | bytes 524320 | tf_op jit(solution)/shard_map/ppermute | solution.py:37
  214.8 1.8 collective-permute-start.59
  216.6 6.4 %collective-permute-done.50 = bf16[64,2048]{1,0:T(8,128)(2,1)S(1)} collective-permute-done((bf16[64,2048]{1,0:T(8,128)(2,1)S(1)}, bf16[64,2048]{1,0:T(8,128)(2,1)S(1)}, u32[]{:S(2)}, u32[]{:S(2)}) %collective-permute-start.50) | collective-permute-done | bytes 262176 | tf_op jit(solution)/shard_map/ppermute | solution.py:37
  224.3 2.9 %collective-permute-done.55 = bf16[128,2048]{1,0:T(8,128)(2,1)S(1)} collective-permute-done((bf16[128,2048]{1,0:T(8,128)(2,1)S(1)}, bf16[128,2048]{1,0:T(8,128)(2,1)S(1)}, u32[]{:S(2)}, u32[]{:S(2)}) %collective-permute-start.55) | collective-permute-done | bytes 524320 | tf_op jit(solution)/shard_map/ppermute | solution.py:37
  227.4 8.9 %collective-permute-done.54 = bf16[128,2048]{1,0:T(8,128)(2,1)S(1)} collective-permute-done((bf16[128,2048]{1,0:T(8,128)(2,1)S(1)}, bf16[128,2048]{1,0:T(8,128)(2,1)S(1)}, u32[]{:S(2)}, u32[]{:S(2)}) %collective-permute-start.54) | collective-permute-done | bytes 524320 | tf_op jit(solution)/shard_map/ppermute | solution.py:37
  240.8 2.9 %update_columns.4.refs_3_ = f32[512,8192]{1,0:T(8,128)} custom-call(bf16[512,512]{1,0:T(8,128)(2,1)S(1)} %convolution_convert_fusion.6.refs_0_, bf16[256,2048]{1,0:T(8,128)(2,1)S(1)} %constant_dynamic-update-slice_fusion.43.refs_1_, bf16[256,2048]{1,0:T(8,128)(2,1)S(1)} %collective-permute-done.59.refs_2_), custom_call_target="tpu_custom_call" | custom-call | tf_op jit(solution)/shard_map/update_columns/pallas_call | solution.py:330
  243.7 11.9 %collective-permute-done.58.refs_2_ = bf16[256,2048]{1,0:T(8,128)(2,1)S(1)} collective-permute-done((bf16[256,2048]{1,0:T(8,128)(2,1)S(1)}, bf16[256,2048]{1,0:T(8,128)(2,1)S(1)}, u32[]{:S(2)}, u32[]{:S(2)}) %collective-permute-start.58) | collective-permute-done | bytes 1048608 | tf_op jit(solution)/shard_map/ppermute | solution.py:37
  255.6 2.9 %update_columns.5.refs_3_ = f32[512,8192]{1,0:T(8,128)} custom-call(bf16[512,512]{1,0:T(8,128)(2,1)S(1)} %convolution_convert_fusion.5.refs_0_, bf16[256,2048]{1,0:T(8,128)(2,1)S(1)} %constant_dynamic-update-slice_fusion.47.refs_1_, bf16[256,2048]{1,0:T(8,128)(2,1)S(1)} %collective-permute-done.58.refs_2_, ...), custom_call_target="tpu_custom_call", output_to_operand_aliasing={{}: (3, {})} | custom-call | tf_op jit(solution)/shard_map/update_columns/pallas_call | solution.py:330
  258.5 2.9 %update_columns.6.refs_3_ = f32[512,8192]{1,0:T(8,128)} custom-call(bf16[512,512]{1,0:T(8,128)(2,1)S(1)} %convolution_convert_fusion.4.refs_0_, bf16[256,2048]{1,0:T(8,128)(2,1)S(1)} %constant_dynamic-update-slice_fusion.49.refs_1_, bf16[256,2048]{1,0:T(8,128)(2,1)S(1)} %collective-permute-done.57.refs_2_, ...), custom_call_target="tpu_custom_call", output_to_operand_aliasing={{}: (3, {})} | custom-call | tf_op jit(solution)/shard_map/update_columns/pallas_call | solution.py:330
  261.4 2.9 %update_columns.7 = f32[512,8192]{1,0:T(8,128)} custom-call(bf16[512,512]{1,0:T(8,128)(2,1)S(1)} %convolution_convert_fusion.6.refs_0_, bf16[256,2048]{1,0:T(8,128)(2,1)S(1)} %constant_dynamic-update-slice_fusion.51.refs_1_, bf16[256,2048]{1,0:T(8,128)(2,1)S(1)} %collective-permute-done.56.refs_2_, ...), custom_call_target="tpu_custom_call", output_to_operand_aliasing={{}: (3, {})} | custom-call | tf_op jit(solution)/shard_map/update_columns/pallas_call | solution.py:330
  (267 shorter events, 57.8 us)
Async XLA Ops:
  4.0 8.3 %collective-permute-start = (f32[160,128]{1,0:T(8,128)S(1)}, f32[160,128]{1,0:T(8,128)S(1)}, u32[]{:S(2)}, u32[]{:S(2)}) collective-permute-start(f32[160,128]{1,0:T(8,128)S(1)} %get-tuple-element.251), channel_id=1, source_target_pairs={{0,2},{2,0},{4,6},{6,4},{8,10},{10,8},{12,14},{14,12},{16,18},{18,... | collective-permute-start | bytes 245768 | tf_op jit(solution)/shard_map/ppermute | solution.py:64
  8.6 7.9 %collective-permute-start.9 = (bf16[1,128,256]{2,1,0:T(8,128)(2,1)S(1)}, bf16[1,128,256]{2,1,0:T(8,128)(2,1)S(1)}, u32[]{:S(2)}, u32[]{:S(2)}) collective-permute-start(bf16[1,128,256]{2,1,0:T(8,128)(2,1)S(1)} %get-tuple-element.119), channel_id=1, source_target_pairs={{0,16},{2,18},{4,20},{6,22},{8,24},{10,26},{12,28},{14,30},{16,0},... | collective-permute-start | bytes 196616 | tf_op jit(solution)/shard_map/ppermute | solution.py:37
  11.7 70.4 %collective-permute-start.26 = (bf16[512,4096]{1,0:T(8,128)(2,1)}, bf16[512,4096]{1,0:T(8,128)(2,1)}, u32[]{:S(2)}, u32[]{:S(2)}) collective-permute-start(bf16[512,4096]{1,0:T(8,128)(2,1)} %left_ref), channel_id=1, source_target_pairs={{0,1},{1,0},{2,3},{3,2},{4,5},{5,4},{6,7},{7,6},{8,9},{9,8},{10,11... | collective-permute-start | bytes 12582920 | tf_op jit(solution)/shard_map/ppermute | solution.py:368
  12.3 10.9 %collective-permute-start.8 = (bf16[1,128,256]{2,1,0:T(8,128)(2,1)S(1)}, bf16[1,128,256]{2,1,0:T(8,128)(2,1)S(1)}, u32[]{:S(2)}, u32[]{:S(2)}) collective-permute-start(bf16[1,128,256]{2,1,0:T(8,128)(2,1)S(1)} %get-tuple-element.121), channel_id=1, source_target_pairs={{0,16},{2,18},{4,20},{6,22},{8,24},{10,26},{12,28},{14,30},{16,0},... | collective-permute-start | bytes 196616 | tf_op jit(solution)/shard_map/ppermute | solution.py:37
  12.5 13.9 %collective-permute-start.7 = (bf16[1,128,256]{2,1,0:T(8,128)(2,1)S(1)}, bf16[1,128,256]{2,1,0:T(8,128)(2,1)S(1)}, u32[]{:S(2)}, u32[]{:S(2)}) collective-permute-start(bf16[1,128,256]{2,1,0:T(8,128)(2,1)S(1)} %get-tuple-element.123), channel_id=1, source_target_pairs={{0,16},{2,18},{4,20},{6,22},{8,24},{10,26},{12,28},{14,30},{16,0},... | collective-permute-start | bytes 196616 | tf_op jit(solution)/shard_map/ppermute | solution.py:37
  15.3 13.4 %collective-permute-start.6 = (bf16[1,128,256]{2,1,0:T(8,128)(2,1)S(1)}, bf16[1,128,256]{2,1,0:T(8,128)(2,1)S(1)}, u32[]{:S(2)}, u32[]{:S(2)}) collective-permute-start(bf16[1,128,256]{2,1,0:T(8,128)(2,1)S(1)} %get-tuple-element.125), channel_id=1, source_target_pairs={{0,16},{2,18},{4,20},{6,22},{8,24},{10,26},{12,28},{14,30},{16,0},... | collective-permute-start | bytes 196616 | tf_op jit(solution)/shard_map/ppermute | solution.py:37
  16.4 12.3 %collective-permute-start.3 = (f32[160,128]{1,0:T(8,128)S(1)}, f32[160,128]{1,0:T(8,128)S(1)}, u32[]{:S(2)}, u32[]{:S(2)}) collective-permute-start(f32[160,128]{1,0:T(8,128)S(1)} %add_add_fusion), channel_id=1, source_target_pairs={{0,8},{2,10},{4,12},{6,14},{8,16},{10,18},{12,20},{14,22},{16,24},... | collective-permute-start | bytes 245768 | tf_op jit(solution)/shard_map/ppermute | solution.py:64
  23.2 7.6 %collective-permute-start.4 = (f32[160,128]{1,0:T(8,128)S(1)}, f32[160,128]{1,0:T(8,128)S(1)}, u32[]{:S(2)}, u32[]{:S(2)}) collective-permute-start(f32[160,128]{1,0:T(8,128)S(1)} %add_add_fusion), channel_id=1, source_target_pairs={{0,16},{2,18},{4,20},{6,22},{8,24},{10,26},{12,28},{14,30},{16,0},... | collective-permute-start | bytes 245768 | tf_op jit(solution)/shard_map/ppermute | solution.py:64
  28.7 7.9 %collective-permute-start.15 = (bf16[2,128,256]{2,1,0:T(8,128)(2,1)S(1)}, bf16[2,128,256]{2,1,0:T(8,128)(2,1)S(1)}, u32[]{:S(2)}, u32[]{:S(2)}) collective-permute-start(bf16[2,128,256]{2,1,0:T(8,128)(2,1)S(1)} %constant_dynamic-update-slice_fusion.7), channel_id=1, source_target_pairs={{0,8},{2,10},{4,12},{6,14},{8,0},{10,2},{12,4},{14,6},{16,24},{18,... | collective-permute-start | bytes 393224 | tf_op jit(solution)/shard_map/ppermute | solution.py:37
  39.7 9.9 %collective-permute-start.21 = (bf16[4,128,256]{2,1,0:T(8,128)(2,1)S(1)}, bf16[4,128,256]{2,1,0:T(8,128)(2,1)S(1)}, u32[]{:S(2)}, u32[]{:S(2)}) collective-permute-start(bf16[4,128,256]{2,1,0:T(8,128)(2,1)S(1)} %constant_dynamic-update-slice_fusion.13), channel_id=1, source_target_pairs={{0,4},{2,6},{4,0},{6,2},{8,12},{10,14},{12,8},{14,10},{16,20},{18,... | collective-permute-start | bytes 786440 | tf_op jit(solution)/shard_map/ppermute | solution.py:37
  41.3 9.3 %collective-permute-start.20 = (bf16[4,128,256]{2,1,0:T(8,128)(2,1)S(1)}, bf16[4,128,256]{2,1,0:T(8,128)(2,1)S(1)}, u32[]{:S(2)}, u32[]{:S(2)}) collective-permute-start(bf16[4,128,256]{2,1,0:T(8,128)(2,1)S(1)} %constant_dynamic-update-slice_fusion.15), channel_id=1, source_target_pairs={{0,2},{2,0},{4,6},{6,4},{8,10},{10,8},{12,14},{14,12},{16,18},{18,... | collective-permute-start | bytes 786440 | tf_op jit(solution)/shard_map/ppermute | solution.py:37
  42.7 11.4 %collective-permute-start.19 = (bf16[4,128,256]{2,1,0:T(8,128)(2,1)S(1)}, bf16[4,128,256]{2,1,0:T(8,128)(2,1)S(1)}, u32[]{:S(2)}, u32[]{:S(2)}) collective-permute-start(bf16[4,128,256]{2,1,0:T(8,128)(2,1)S(1)} %constant_dynamic-update-slice_fusion.17), channel_id=1, source_target_pairs={{0,4},{2,6},{4,0},{6,2},{8,12},{10,14},{12,8},{14,10},{16,20},{18,... | collective-permute-start | bytes 786440 | tf_op jit(solution)/shard_map/ppermute | solution.py:37
  44.6 10.5 %collective-permute-start.18 = (bf16[4,128,256]{2,1,0:T(8,128)(2,1)S(1)}, bf16[4,128,256]{2,1,0:T(8,128)(2,1)S(1)}, u32[]{:S(2)}, u32[]{:S(2)}) collective-permute-start(bf16[4,128,256]{2,1,0:T(8,128)(2,1)S(1)} %constant_dynamic-update-slice_fusion.19), channel_id=1, source_target_pairs={{0,2},{2,0},{4,6},{6,4},{8,10},{10,8},{12,14},{14,12},{16,18},{18,... | collective-permute-start | bytes 786440 | tf_op jit(solution)/shard_map/ppermute | solution.py:37
  50.6 31.5 %collective-permute-start.22 = (bf16[8,128,256]{2,1,0:T(8,128)(2,1)S(1)}, bf16[8,128,256]{2,1,0:T(8,128)(2,1)S(1)}, u32[]{:S(2)}, u32[]{:S(2)}) collective-permute-start(bf16[8,128,256]{2,1,0:T(8,128)(2,1)S(1)} %constant_dynamic-update-slice_fusion.21.refs_0_.refs_8_), channel_id=1, source_target_pairs={{0,2},{2,0},{4,6},{6,4},{8,10},{10,8},{12,14},{14,12},{16,18},{18,... | collective-permute-start | bytes 1572872 | tf_op jit(solution)/shard_map/ppermute | solution.py:37
  54.1 28.0 %collective-permute-start.23 = (bf16[8,128,256]{2,1,0:T(8,128)(2,1)S(1)}, bf16[8,128,256]{2,1,0:T(8,128)(2,1)S(1)}, u32[]{:S(2)}, u32[]{:S(2)}) collective-permute-start(bf16[8,128,256]{2,1,0:T(8,128)(2,1)S(1)} %constant_dynamic-update-slice_fusion.23.refs_2_.refs_10_), channel_id=1, source_target_pairs={{0,4},{2,6},{4,0},{6,2},{8,12},{10,14},{12,8},{14,10},{16,20},{18,... | collective-permute-start | bytes 1572872 | tf_op jit(solution)/shard_map/ppermute | solution.py:37
  55.0 27.1 %collective-permute-start.24 = (bf16[8,128,256]{2,1,0:T(8,128)(2,1)S(1)}, bf16[8,128,256]{2,1,0:T(8,128)(2,1)S(1)}, u32[]{:S(2)}, u32[]{:S(2)}) collective-permute-start(bf16[8,128,256]{2,1,0:T(8,128)(2,1)S(1)} %constant_dynamic-update-slice_fusion.25.refs_4_.refs_12_), channel_id=1, source_target_pairs={{0,8},{2,10},{4,12},{6,14},{8,0},{10,2},{12,4},{14,6},{16,24},{18,... | collective-permute-start | bytes 1572872 | tf_op jit(solution)/shard_map/ppermute | solution.py:37
  55.1 27.0 %collective-permute-start.25 = (bf16[8,128,256]{2,1,0:T(8,128)(2,1)S(1)}, bf16[8,128,256]{2,1,0:T(8,128)(2,1)S(1)}, u32[]{:S(2)}, u32[]{:S(2)}) collective-permute-start(bf16[8,128,256]{2,1,0:T(8,128)(2,1)S(1)} %constant_dynamic-update-slice_fusion.27.refs_6_.refs_14_), channel_id=1, source_target_pairs={{0,8},{2,10},{4,12},{6,14},{8,0},{10,2},{12,4},{14,6},{16,24},{18,... | collective-permute-start | bytes 1572872 | tf_op jit(solution)/shard_map/ppermute | solution.py:37
  101.8 26.1 %collective-permute-start.29 = (bf16[256,2048]{1,0:T(8,128)(2,1)S(1)}, bf16[256,2048]{1,0:T(8,128)(2,1)S(1)}, u32[]{:S(2)}, u32[]{:S(2)}) collective-permute-start(bf16[256,2048]{1,0:T(8,128)(2,1)S(1)} %convolution_convert_fusion.3), channel_id=1, source_target_pairs={{0,2},{2,0},{4,6},{6,4},{8,10},{10,8},{12,14},{14,12},{16,18},{18,... | collective-permute-start | bytes 3145736 | tf_op jit(solution)/shard_map/ppermute | solution.py:37
  110.4 25.0 %collective-permute-start.32 = (bf16[256,2048]{1,0:T(8,128)(2,1)S(1)}, bf16[256,2048]{1,0:T(8,128)(2,1)S(1)}, u32[]{:S(2)}, u32[]{:S(2)}) collective-permute-start(bf16[256,2048]{1,0:T(8,128)(2,1)S(1)} %convolution_convert_fusion.2), channel_id=1, source_target_pairs={{0,8},{2,10},{4,12},{6,14},{8,0},{10,2},{12,4},{14,6},{16,24},{18,... | collective-permute-start | bytes 3145736 | tf_op jit(solution)/shard_map/ppermute | solution.py:37
  110.5 26.7 %collective-permute-start.31 = (bf16[256,2048]{1,0:T(8,128)(2,1)S(1)}, bf16[256,2048]{1,0:T(8,128)(2,1)S(1)}, u32[]{:S(2)}, u32[]{:S(2)}) collective-permute-start(bf16[256,2048]{1,0:T(8,128)(2,1)S(1)} %convolution_convert_fusion.1), channel_id=1, source_target_pairs={{0,4},{2,6},{4,0},{6,2},{8,12},{10,14},{12,8},{14,10},{16,20},{18,... | collective-permute-start | bytes 3145736 | tf_op jit(solution)/shard_map/ppermute | solution.py:37
  111.3 38.2 %collective-permute-start.28 = (bf16[256,2048]{1,0:T(8,128)(2,1)S(1)}, bf16[256,2048]{1,0:T(8,128)(2,1)S(1)}, u32[]{:S(2)}, u32[]{:S(2)}) collective-permute-start(bf16[256,2048]{1,0:T(8,128)(2,1)S(1)} %convolution_convert_fusion), channel_id=1, source_target_pairs={{0,2},{2,0},{4,6},{6,4},{8,10},{10,8},{12,14},{14,12},{16,18},{18,... | collective-permute-start | bytes 3145736 | tf_op jit(solution)/shard_map/ppermute | solution.py:37
  128.3 18.4 %collective-permute-start.30 = (bf16[128,2048]{1,0:T(8,128)(2,1)S(1)}, bf16[128,2048]{1,0:T(8,128)(2,1)S(1)}, u32[]{:S(2)}, u32[]{:S(2)}) collective-permute-start(bf16[128,2048]{1,0:T(8,128)(2,1)S(1)} %slice.343), channel_id=1, source_target_pairs={{0,4},{2,6},{4,0},{6,2},{8,12},{10,14},{12,8},{14,10},{16,20},{18,... | collective-permute-start | bytes 1572872 | tf_op jit(solution)/shard_map/ppermute | solution.py:37
  135.8 25.1 %collective-permute-start.36 = (bf16[128,2048]{1,0:T(8,128)(2,1)S(1)}, bf16[128,2048]{1,0:T(8,128)(2,1)S(1)}, u32[]{:S(2)}, u32[]{:S(2)}) collective-permute-start(bf16[128,2048]{1,0:T(8,128)(2,1)S(1)} %slice.342), channel_id=1, source_target_pairs={{0,16},{2,18},{4,20},{6,22},{8,24},{10,26},{12,28},{14,30},{16,0},... | collective-permute-start | bytes 1572872 | tf_op jit(solution)/shard_map/ppermute | solution.py:37
  137.7 26.0 %collective-permute-start.35 = (bf16[128,2048]{1,0:T(8,128)(2,1)S(1)}, bf16[128,2048]{1,0:T(8,128)(2,1)S(1)}, u32[]{:S(2)}, u32[]{:S(2)}) collective-permute-start(bf16[128,2048]{1,0:T(8,128)(2,1)S(1)} %slice.341), channel_id=1, source_target_pairs={{0,8},{2,10},{4,12},{6,14},{8,0},{10,2},{12,4},{14,6},{16,24},{18,... | collective-permute-start | bytes 1572872 | tf_op jit(solution)/shard_map/ppermute | solution.py:37
  146.9 20.4 %collective-permute-start.34 = (bf16[64,2048]{1,0:T(8,128)(2,1)S(1)}, bf16[64,2048]{1,0:T(8,128)(2,1)S(1)}, u32[]{:S(2)}, u32[]{:S(2)}) collective-permute-start(bf16[64,2048]{1,0:T(8,128)(2,1)S(1)} %slice.347), channel_id=1, source_target_pairs={{0,8},{2,10},{4,12},{6,14},{8,0},{10,2},{12,4},{14,6},{16,24},{18,... | collective-permute-start | bytes 786440 | tf_op jit(solution)/shard_map/ppermute | solution.py:37
  151.2 16.3 %collective-permute-start.33 = (bf16[128,2048]{1,0:T(8,128)(2,1)S(1)}, bf16[128,2048]{1,0:T(8,128)(2,1)S(1)}, u32[]{:S(2)}, u32[]{:S(2)}) collective-permute-start(bf16[128,2048]{1,0:T(8,128)(2,1)S(1)} %slice.340), channel_id=1, source_target_pairs={{0,4},{2,6},{4,0},{6,2},{8,12},{10,14},{12,8},{14,10},{16,20},{18,... | collective-permute-start | bytes 1572872 | tf_op jit(solution)/shard_map/ppermute | solution.py:37
  161.2 9.1 %collective-permute-start.40 = (bf16[64,2048]{1,0:T(8,128)(2,1)S(1)}, bf16[64,2048]{1,0:T(8,128)(2,1)S(1)}, u32[]{:S(2)}, u32[]{:S(2)}) collective-permute-start(bf16[64,2048]{1,0:T(8,128)(2,1)S(1)} %slice.346), channel_id=1, source_target_pairs={{0,4},{2,6},{4,0},{6,2},{8,12},{10,14},{12,8},{14,10},{16,20},{18,... | collective-permute-start | bytes 786440 | tf_op jit(solution)/shard_map/ppermute | solution.py:37
  163.9 7.6 %collective-permute-start.39 = (bf16[64,2048]{1,0:T(8,128)(2,1)S(1)}, bf16[64,2048]{1,0:T(8,128)(2,1)S(1)}, u32[]{:S(2)}, u32[]{:S(2)}) collective-permute-start(bf16[64,2048]{1,0:T(8,128)(2,1)S(1)} %slice.345), channel_id=1, source_target_pairs={{0,2},{2,0},{4,6},{6,4},{8,10},{10,8},{12,14},{14,12},{16,18},{18,... | collective-permute-start | bytes 786440 | tf_op jit(solution)/shard_map/ppermute | solution.py:37
  167.7 13.1 %collective-permute-start.37 = (bf16[64,2048]{1,0:T(8,128)(2,1)S(1)}, bf16[64,2048]{1,0:T(8,128)(2,1)S(1)}, u32[]{:S(2)}, u32[]{:S(2)}) collective-permute-start(bf16[64,2048]{1,0:T(8,128)(2,1)S(1)} %slice.344), channel_id=1, source_target_pairs={{0,8},{2,10},{4,12},{6,14},{8,0},{10,2},{12,4},{14,6},{16,24},{18,... | collective-permute-start | bytes 786440 | tf_op jit(solution)/shard_map/ppermute | solution.py:37
  170.4 10.7 %collective-permute-start.42 = (bf16[32,2048]{1,0:T(8,128)(2,1)S(1)}, bf16[32,2048]{1,0:T(8,128)(2,1)S(1)}, u32[]{:S(2)}, u32[]{:S(2)}) collective-permute-start(bf16[32,2048]{1,0:T(8,128)(2,1)S(1)} %slice.350), channel_id=1, source_target_pairs={{0,2},{2,0},{4,6},{6,4},{8,10},{10,8},{12,14},{14,12},{16,18},{18,... | collective-permute-start | bytes 393224 | tf_op jit(solution)/shard_map/ppermute | solution.py:37
  171.7 16.8 %collective-permute-start.45 = (bf16[32,2048]{1,0:T(8,128)(2,1)S(1)}, bf16[32,2048]{1,0:T(8,128)(2,1)S(1)}, u32[]{:S(2)}, u32[]{:S(2)}) collective-permute-start(bf16[32,2048]{1,0:T(8,128)(2,1)S(1)} %slice.349), channel_id=1, source_target_pairs={{0,16},{2,18},{4,20},{6,22},{8,24},{10,26},{12,28},{14,30},{16,0},... | collective-permute-start | bytes 393224 | tf_op jit(solution)/shard_map/ppermute | solution.py:37
  175.1 16.2 %collective-permute-start.44 = (bf16[32,2048]{1,0:T(8,128)(2,1)S(1)}, bf16[32,2048]{1,0:T(8,128)(2,1)S(1)}, u32[]{:S(2)}, u32[]{:S(2)}) collective-permute-start(bf16[32,2048]{1,0:T(8,128)(2,1)S(1)} %get-tuple-element.193), channel_id=1, source_target_pairs={{0,16},{2,18},{4,20},{6,22},{8,24},{10,26},{12,28},{14,30},{16,0},... | collective-permute-start | bytes 393224 | tf_op jit(solution)/shard_map/ppermute | solution.py:37
  180.9 16.1 %collective-permute-start.41 = (bf16[32,2048]{1,0:T(8,128)(2,1)S(1)}, bf16[32,2048]{1,0:T(8,128)(2,1)S(1)}, u32[]{:S(2)}, u32[]{:S(2)}) collective-permute-start(bf16[32,2048]{1,0:T(8,128)(2,1)S(1)} %slice.348), channel_id=1, source_target_pairs={{0,16},{2,18},{4,20},{6,22},{8,24},{10,26},{12,28},{14,30},{16,0},... | collective-permute-start | bytes 393224 | tf_op jit(solution)/shard_map/ppermute | solution.py:37
  181.3 10.4 %collective-permute-start.43 = (bf16[32,2048]{1,0:T(8,128)(2,1)S(1)}, bf16[32,2048]{1,0:T(8,128)(2,1)S(1)}, u32[]{:S(2)}, u32[]{:S(2)}) collective-permute-start(bf16[32,2048]{1,0:T(8,128)(2,1)S(1)} %get-tuple-element.195), channel_id=1, source_target_pairs={{0,2},{2,0},{4,6},{6,4},{8,10},{10,8},{12,14},{14,12},{16,18},{18,... | collective-permute-start | bytes 393224 | tf_op jit(solution)/shard_map/ppermute | solution.py:37
  188.7 11.1 %collective-permute-start.49 = (bf16[32,2048]{1,0:T(8,128)(2,1)S(1)}, bf16[32,2048]{1,0:T(8,128)(2,1)S(1)}, u32[]{:S(2)}, u32[]{:S(2)}) collective-permute-start(bf16[32,2048]{1,0:T(8,128)(2,1)S(1)} %get-tuple-element.199), channel_id=1, source_target_pairs={{0,16},{2,18},{4,20},{6,22},{8,24},{10,26},{12,28},{14,30},{16,0},... | collective-permute-start | bytes 393224 | tf_op jit(solution)/shard_map/ppermute | solution.py:37
  191.3 12.6 %collective-permute-start.48 = (bf16[64,2048]{1,0:T(8,128)(2,1)S(1)}, bf16[64,2048]{1,0:T(8,128)(2,1)S(1)}, u32[]{:S(2)}, u32[]{:S(2)}) collective-permute-start(bf16[64,2048]{1,0:T(8,128)(2,1)S(1)} %constant_dynamic-update-slice_fusion.29), channel_id=1, source_target_pairs={{0,8},{2,10},{4,12},{6,14},{8,0},{10,2},{12,4},{14,6},{16,24},{18,... | collective-permute-start | bytes 786440 | tf_op jit(solution)/shard_map/ppermute | solution.py:37
  191.7 13.3 %collective-permute-start.47 = (bf16[64,2048]{1,0:T(8,128)(2,1)S(1)}, bf16[64,2048]{1,0:T(8,128)(2,1)S(1)}, u32[]{:S(2)}, u32[]{:S(2)}) collective-permute-start(bf16[64,2048]{1,0:T(8,128)(2,1)S(1)} %constant_dynamic-update-slice_fusion.31), channel_id=1, source_target_pairs={{0,4},{2,6},{4,0},{6,2},{8,12},{10,14},{12,8},{14,10},{16,20},{18,... | collective-permute-start | bytes 786440 | tf_op jit(solution)/shard_map/ppermute | solution.py:37
  197.1 7.9 %collective-permute-start.46 = (bf16[32,2048]{1,0:T(8,128)(2,1)S(1)}, bf16[32,2048]{1,0:T(8,128)(2,1)S(1)}, u32[]{:S(2)}, u32[]{:S(2)}) collective-permute-start(bf16[32,2048]{1,0:T(8,128)(2,1)S(1)} %get-tuple-element.205), channel_id=1, source_target_pairs={{0,16},{2,18},{4,20},{6,22},{8,24},{10,26},{12,28},{14,30},{16,0},... | collective-permute-start | bytes 393224 | tf_op jit(solution)/shard_map/ppermute | solution.py:37
  199.8 7.7 %collective-permute-start.52 = (bf16[64,2048]{1,0:T(8,128)(2,1)S(1)}, bf16[64,2048]{1,0:T(8,128)(2,1)S(1)}, u32[]{:S(2)}, u32[]{:S(2)}) collective-permute-start(bf16[64,2048]{1,0:T(8,128)(2,1)S(1)} %constant_dynamic-update-slice_fusion.33), channel_id=1, source_target_pairs={{0,2},{2,0},{4,6},{6,4},{8,10},{10,8},{12,14},{14,12},{16,18},{18,... | collective-permute-start | bytes 786440 | tf_op jit(solution)/shard_map/ppermute | solution.py:37
  204.0 10.8 %collective-permute-start.51 = (bf16[128,2048]{1,0:T(8,128)(2,1)S(1)}, bf16[128,2048]{1,0:T(8,128)(2,1)S(1)}, u32[]{:S(2)}, u32[]{:S(2)}) collective-permute-start(bf16[128,2048]{1,0:T(8,128)(2,1)S(1)} %constant_dynamic-update-slice_fusion.35), channel_id=1, source_target_pairs={{0,4},{2,6},{4,0},{6,2},{8,12},{10,14},{12,8},{14,10},{16,20},{18,... | collective-permute-start | bytes 1572872 | tf_op jit(solution)/shard_map/ppermute | solution.py:37
  205.0 22.2 %collective-permute-start.55 = (bf16[128,2048]{1,0:T(8,128)(2,1)S(1)}, bf16[128,2048]{1,0:T(8,128)(2,1)S(1)}, u32[]{:S(2)}, u32[]{:S(2)}) collective-permute-start(bf16[128,2048]{1,0:T(8,128)(2,1)S(1)} %constant_dynamic-update-slice_fusion.37), channel_id=1, source_target_pairs={{0,16},{2,18},{4,20},{6,22},{8,24},{10,26},{12,28},{14,30},{16,0},... | collective-permute-start | bytes 1572872 | tf_op jit(solution)/shard_map/ppermute | solution.py:37
  205.1 17.9 %collective-permute-start.50 = (bf16[64,2048]{1,0:T(8,128)(2,1)S(1)}, bf16[64,2048]{1,0:T(8,128)(2,1)S(1)}, u32[]{:S(2)}, u32[]{:S(2)}) collective-permute-start(bf16[64,2048]{1,0:T(8,128)(2,1)S(1)} %constant_dynamic-update-slice_fusion.39), channel_id=1, source_target_pairs={{0,8},{2,10},{4,12},{6,14},{8,0},{10,2},{12,4},{14,6},{16,24},{18,... | collective-permute-start | bytes 786440 | tf_op jit(solution)/shard_map/ppermute | solution.py:37
  207.6 28.6 %collective-permute-start.54 = (bf16[128,2048]{1,0:T(8,128)(2,1)S(1)}, bf16[128,2048]{1,0:T(8,128)(2,1)S(1)}, u32[]{:S(2)}, u32[]{:S(2)}) collective-permute-start(bf16[128,2048]{1,0:T(8,128)(2,1)S(1)} %constant_dynamic-update-slice_fusion.41), channel_id=1, source_target_pairs={{0,8},{2,10},{4,12},{6,14},{8,0},{10,2},{12,4},{14,6},{16,24},{18,... | collective-permute-start | bytes 1572872 | tf_op jit(solution)/shard_map/ppermute | solution.py:37
  214.8 26.0 %collective-permute-start.59 = (bf16[256,2048]{1,0:T(8,128)(2,1)S(1)}, bf16[256,2048]{1,0:T(8,128)(2,1)S(1)}, u32[]{:S(2)}, u32[]{:S(2)}) collective-permute-start(bf16[256,2048]{1,0:T(8,128)(2,1)S(1)} %constant_dynamic-update-slice_fusion.43.refs_1_), channel_id=1, source_target_pairs={{0,2},{2,0},{4,6},{6,4},{8,10},{10,8},{12,14},{14,12},{16,18},{18,... | collective-permute-start | bytes 3145736 | tf_op jit(solution)/shard_map/ppermute | solution.py:37
  223.1 14.5 %collective-permute-start.53 = (bf16[128,2048]{1,0:T(8,128)(2,1)S(1)}, bf16[128,2048]{1,0:T(8,128)(2,1)S(1)}, u32[]{:S(2)}, u32[]{:S(2)}) collective-permute-start(bf16[128,2048]{1,0:T(8,128)(2,1)S(1)} %constant_dynamic-update-slice_fusion.45), channel_id=1, source_target_pairs={{0,4},{2,6},{4,0},{6,2},{8,12},{10,14},{12,8},{14,10},{16,20},{18,... | collective-permute-start | bytes 1572872 | tf_op jit(solution)/shard_map/ppermute | solution.py:37
  227.3 28.3 %collective-permute-start.58 = (bf16[256,2048]{1,0:T(8,128)(2,1)S(1)}, bf16[256,2048]{1,0:T(8,128)(2,1)S(1)}, u32[]{:S(2)}, u32[]{:S(2)}) collective-permute-start(bf16[256,2048]{1,0:T(8,128)(2,1)S(1)} %constant_dynamic-update-slice_fusion.47.refs_1_), channel_id=1, source_target_pairs={{0,8},{2,10},{4,12},{6,14},{8,0},{10,2},{12,4},{14,6},{16,24},{18,... | collective-permute-start | bytes 3145736 | tf_op jit(solution)/shard_map/ppermute | solution.py:37
  236.3 19.3 %collective-permute-start.57 = (bf16[256,2048]{1,0:T(8,128)(2,1)S(1)}, bf16[256,2048]{1,0:T(8,128)(2,1)S(1)}, u32[]{:S(2)}, u32[]{:S(2)}) collective-permute-start(bf16[256,2048]{1,0:T(8,128)(2,1)S(1)} %constant_dynamic-update-slice_fusion.49.refs_1_), channel_id=1, source_target_pairs={{0,4},{2,6},{4,0},{6,2},{8,12},{10,14},{12,8},{14,10},{16,20},{18,... | collective-permute-start | bytes 3145736 | tf_op jit(solution)/shard_map/ppermute | solution.py:37
  237.7 23.7 %collective-permute-start.56 = (bf16[256,2048]{1,0:T(8,128)(2,1)S(1)}, bf16[256,2048]{1,0:T(8,128)(2,1)S(1)}, u32[]{:S(2)}, u32[]{:S(2)}) collective-permute-start(bf16[256,2048]{1,0:T(8,128)(2,1)S(1)} %constant_dynamic-update-slice_fusion.51.refs_1_), channel_id=1, source_target_pairs={{0,2},{2,0},{4,6},{6,4},{8,10},{10,8},{12,14},{14,12},{16,18},{18,... | collective-permute-start | bytes 3145736 | tf_op jit(solution)/shard_map/ppermute | solution.py:37
  (37 other events, 224.6 us)

commit v4 on v3

--- a/solution.py
+++ b/solution.py
@@ -26,7 +26,7 @@
 STEPS = ((0, 0), (1, 0), (2, 0), (3, 0), (0, 1), (1, 1), (2, 1), (0, 2), (3, 1), (1, 2), (2, 2), (0, 3), (3, 2), (1, 3), (2, 3), (0, 4), (3, 3), (1, 4), (2, 4), (0, 5), (1, 5), (3, 4), (2, 5), (0, 6), (1, 6), (3, 5), (2, 6), (0, 7), (3, 6), (1, 7), (2, 7), (3, 7), (0, 8), (1, 8), (2, 8), (3, 8))
 
 
-GATHER = ((0, 1, 2, 3), (1, 0, 2, 3), (2, 1, 0, 3), (2, 0, 1, 3))
+GATHER = ((3, (0, 1, 2, 3)), (3, (1, 0, 2, 3)), (2, (2, 0, 1, 3)))
 
 
 def flip_pairs(devices, bit):
@@ -120,7 +120,29 @@
     return [(i, j) for i in range(size // BLOCK) for j in range(i + 1)]
 
 
-def factor_kernel(blocks, packed_ref, out_ref, work_ref):
+def factor_steps(first, last, work_ref, out_ref):
+    size = out_ref.shape[0]
+
+    def step(at, carry):
+        base = pl.multiple_of(at * BLOCK, BLOCK)
+        inverse = inverse_factor(work_ref[pl.ds(base, BLOCK), pl.ds(base, BLOCK)])
+        rows = dot_nn(inverse, out_ref[pl.ds(base, BLOCK), :])
+        out_ref[pl.ds(base, BLOCK), :] = rows
+
+        @pl.when(at < size // BLOCK - 1)
+        def _():
+            panel = dot_nt(work_ref[:, pl.ds(base, BLOCK)], inverse)
+            below = lax.broadcasted_iota(jnp.int32, (size, BLOCK), 0) >= base + BLOCK
+            panel = jnp.where(below, panel, 0.0)
+            work_ref[...] -= dot_nt(panel, panel)
+            out_ref[...] -= dot_nn(panel, rows)
+
+        return carry
+
+    lax.fori_loop(first, last, step, 0)
+
+
+def factor_head(blocks, steps, packed_ref, work_ref, out_ref):
     size = out_ref.shape[0]
     work_ref[...] = jnp.zeros_like(work_ref)
     for at, (i, j) in enumerate(blocks):
@@ -133,36 +155,37 @@
         1.0,
         0.0,
     )
-
-    def step(at, carry):
-        base = pl.multiple_of(at * BLOCK, BLOCK)
-        inverse = inverse_factor(work_ref[pl.ds(base, BLOCK), pl.ds(base, BLOCK)])
-        rows = dot_nn(inverse, out_ref[pl.ds(base, BLOCK), :])
-        out_ref[pl.ds(base, BLOCK), :] = rows
-
-        @pl.when(at < size // BLOCK - 1)
-        def _():
-            panel = dot_nt(work_ref[:, pl.ds(base, BLOCK)], inverse)
-            below = lax.broadcasted_iota(jnp.int32, (size, BLOCK), 0) >= base + BLOCK
-            panel = jnp.where(below, panel, 0.0)
-            work_ref[...] -= dot_nt(panel, panel)
-            out_ref[...] -= dot_nn(panel, rows)
-
-        return carry
-
-    lax.fori_loop(0, size // BLOCK, step, 0)
-
-
-def inverse_of_factor(packed, blocks, size):
+    factor_steps(0, steps, work_ref, out_ref)
+
+
+def factor_rest(steps, start_ref, done_ref, out_ref, work_ref):
+    work_ref[...] = start_ref[...]
+    out_ref[...] = done_ref[...]
+    factor_steps(steps, out_ref.shape[0] // BLOCK, work_ref, out_ref)
+
+
+def head_of_factor(packed, blocks, size, steps):
+    square = jax.ShapeDtypeStruct((size, size), F32)
     return pl.pallas_call(
-        functools.partial(factor_kernel, blocks),
-        out_shape=jax.ShapeDtypeStruct((size, size), F32),
+        functools.partial(factor_head, blocks, steps),
+        out_shape=(square, square),
         in_specs=[pl.BlockSpec(memory_space=pltpu.VMEM)],
+        out_specs=(pl.BlockSpec(memory_space=pltpu.VMEM),) * 2,
+        compiler_params=pltpu.CompilerParams(vmem_limit_bytes=VMEM_LIMIT),
+        name="factor_head",
+    )(packed)
+
+
+def rest_of_factor(work, done, steps):
+    return pl.pallas_call(
+        functools.partial(factor_rest, steps),
+        out_shape=jax.ShapeDtypeStruct(work.shape, F32),
+        in_specs=[pl.BlockSpec(memory_space=pltpu.VMEM)] * 2,
         out_specs=pl.BlockSpec(memory_space=pltpu.VMEM),
-        scratch_shapes=[pltpu.VMEM((size, size), F32)],
+        scratch_shapes=[pltpu.VMEM(work.shape, F32)],
         compiler_params=pltpu.CompilerParams(vmem_limit_bytes=VMEM_LIMIT),
-        name="inverse_factor",
-    )(packed)
+        name="factor_rest",
+    )(work, done)
 
 
 def gram_and_sketch(sketch, half, dims, own, core):
@@ -188,23 +211,29 @@
     arrived = [send(piece, dims, (0, a, b)) for (a, b), piece in zip(shifts[1:], outgoing)]
 
     groups = gather_groups(half.shape[0], bits)
-    tall = half.shape[0] // len(groups)
     (half,) = after(outgoing[-1], (half,))
-    gathered = [half[None, g * tall : (g + 1) * tall] for g in range(len(groups))]
-    moving = [flip(rows, devices, order[-1]) for rows, order in zip(gathered, groups)]
-
-    def widen(stage, token):
-        for g, order in enumerate(groups):
-            rows, piece = after(token, (gathered[g], moving[g]))
-            token = gathered[g] = jnp.concatenate([rows, piece])
-            moving[g] = flip(token, devices, order[-1 - stage])
+    parts = [(groups, half[None], flip(half[None], devices, groups[0][1][-1]))]
+
+    def widen(stage, token, chosen=slice(None)):
+        split = []
+        for members, rows, piece in parts[chosen]:
+            rows, piece = after(token, (rows, piece))
+            token = jnp.concatenate([rows, piece])
+            start = 0
+            for bit, same in itertools.groupby(members, lambda m: m[1][-1 - stage]):
+                same = list(same)
+                tall = sum(rows for rows, _ in same)
+                piece = token[:, start : start + tall]
+                start += tall
+                split.append((same, piece, flip(piece, devices, bit)))
+        parts[chosen] = split
         return token
 
     arrived = after(half, arrived)
     for piece in arrived:
         total = total + piece
     arrived = [send(total, dims, (by, 0, 0)) for by in range(1, dims[0])]
-    token = widen(1, total)
+    token = widen(1, arrived[0])
     arrived = after(token, arrived)
     places = jnp.stack([total, *arrived])
     order = [(own[0] - z) % dims[0] for z in range(dims[0])]
@@ -212,7 +241,7 @@
         jnp.add, [lax.dynamic_index_in_dim(places, at, 0, keepdims=False) for at in order]
     )
     arrived = [send(total, dims, (0, -a, -b)) for a, b in shifts[1:]]
-    token = widen(2, total)
+    token = widen(2, arrived[0], slice(0, max(1, len(parts) - 1)))
     arrived = after(token, arrived)
     whole = lax.dynamic_update_slice_in_dim(
         jnp.zeros_like(mine), total, at_of(0, 0), 0
@@ -221,34 +250,42 @@
         whole = lax.dynamic_update_slice_in_dim(whole, piece, at_of(a, b), 0)
     other = lax.ppermute(whole, "tensor", [(0, 1), (1, 0)])
     token = whole
-    for stage in range(3, bits):
+    if len(parts) > 2:
+        token = widen(2, token, slice(-1, None))
+    for stage in range(3, bits - 1):
         token = widen(stage, token)
     whole, other = after(token, (whole, other))
     packed = jnp.where(
         core == 0, jnp.concatenate([whole, other]), jnp.concatenate([other, whole])
     )
-    return packed, blocks, groups, gathered, moving
+    work, done = head_of_factor(packed, blocks, size, 1)
+    token = widen(bits - 1, work)
+    work, done = after(token, (work, done))
+    inverse = rest_of_factor(work, done, 1)
+    orders = [order for _, order in groups]
+    return inverse, orders, [part[1] for part in parts], [part[2] for part in parts]
 
 
 def gather_groups(rows, bits):
-    count = max(1, min(len(GATHER), rows // BLOCK))
-    return [order + tuple(range(4, bits)) for order in GATHER[:count]]
+    chosen = GATHER if rows >= 4 * BLOCK else ((8, GATHER[0][1]),)
+    return [(share * rows // 8, order + tuple(range(4, bits))) for share, order in chosen]
 
 
 def mix_kernel(groups, limit, table_ref, left_ref, right_ref, *refs):
     at = pl.program_id(0)
     out_ref = refs[-1]
-    tall = refs[0].shape[1]
     total = None
     for side, source in enumerate((left_ref, right_ref)):
+        rows = []
         for g in range(groups):
-            near, far = refs[2 * (side * groups + g)], refs[2 * (side * groups + g) + 1]
+            near, far = refs[2 * g], refs[2 * g + 1]
             place = table_ref[side, g, at]
-            rows = jnp.where(place < limit, near[0], far[0])
-            term = jnp.dot(
-                source[:, g * tall : (g + 1) * tall], rows, preferred_element_type=F32
-            )
-            total = term if total is None else total + term
+            far_place = lax.rem(place, limit)
+            rows.append(jnp.where(place < limit, near[far_place], far[far_place]))
+        term = jnp.dot(
+            source[...], jnp.concatenate(rows, axis=0), preferred_element_type=F32
+        )
+        total = term if total is None else total + term
 
     @pl.when(at == 0)
     def _():
@@ -260,7 +297,7 @@
 
 
 def mix(left, right, near, far, groups, dp, core):
-    limit, tall, cols = near[0].shape
+    limit, _, cols = near[0].shape
     bits = limit.bit_length()
     count = len(groups)
     blocks = jnp.arange(limit, dtype=jnp.int32)
@@ -278,14 +315,10 @@
     block = left.shape[1] // limit
     in_specs = [pl.BlockSpec((left.shape[0], block), lambda i, t: (0, i))] * 2
     operands = [left, right]
-    for side in range(2):
-        for g in range(count):
-            spec = pl.BlockSpec(
-                (1, tall, cols),
-                lambda i, t, side=side, g=g: (t[side, g, i] % limit, 0, 0),
-            )
-            in_specs += [spec, spec]
-            operands += [near[g], far[g]]
+    for g in range(count):
+        spec = pl.BlockSpec(near[g].shape, lambda i, t: (0, 0, 0))
+        in_specs += [spec, spec]
+        operands += [near[g], far[g]]
     return pl.pallas_call(
         functools.partial(mix_kernel, count, limit),
         grid_spec=pltpu.PrefetchScalarGridSpec(
@@ -367,8 +400,7 @@
 
     beside = lax.ppermute(activations, "tensor", [(0, 1), (1, 0)])
     half = lax.dynamic_slice_in_dim(sketch, core * (rank // 2), rank // 2, 1).astype(BF16)
-    packed, blocks, groups, near, far = gram_and_sketch(sketch, half, dims, own, core)
-    inverse = inverse_of_factor(packed, blocks, rank)
+    inverse, groups, near, far = gram_and_sketch(sketch, half, dims, own, core)
     *far, activations = after(inverse, (*far, activations))
     mixed_half = mix(activations, beside, near, far, groups, dp, core)
     mixed_other = lax.ppermute(mixed_half, "tensor", [(0, 1), (1, 0)])
@@ -409,11 +441,11 @@
         columns = slice(start, start + cols)
         if step == 0:
             size = rank // 2
-            factor, grads = after(token, (inverse, out_grads))
-            if order not in projected:
+            (grads,) = after(token, (out_grads,))
+            if not projected:
                 turned = lax.dot_general(
                     picks[order].astype(F32),
-                    factor,
+                    inverse,
                     (((1,), (0,)), ((), ())),
                     precision=lax.Precision.HIGH,
                     preferred_element_type=F32,
@@ -425,10 +457,17 @@
                     precision=lax.Precision.HIGH,
                     preferred_element_type=F32,
                 ).astype(BF16)
+            elif order not in projected:
+                base, rows = next(iter(projected.items()))
+                (rows,) = after(token, (rows,))
+                bare = rows.reshape((2,) * bits + (rank // devices, rows.shape[1]))
+                axes = [base.index(bit) for bit in order] + [bits, bits + 1]
+                projected[order] = bare.transpose(axes).reshape(rows.shape)
             left = projected[order]
             outgoing = jnp.dot(
                 left[size:], grads[:, columns], preferred_element_type=F32
             ).astype(BF16)
+            grads, left, outgoing = lax.optimization_barrier((grads, left, outgoing))
             kept[g] = jnp.dot(left[:size], grads[:, columns], preferred_element_type=F32)
             bit = order[0]
         elif step < bits:

time: 265 us -> 257 us (0.970)
  waiting for transfers between devices: 123 us -> 118 us
  matrix products: 20.6 us -> 16.6 us
    ppermute x48 -> x41, waiting for transfers between devices: 120 us -> 113 us  [flip(): return lax.ppermute(value, 'dp', flip_pairs(devices, bit))]
    ppermute x9, waiting for transfers between devices: 1.51 us -> 4.27 us  [send(): return lax.ppermute(value, 'dp', shift_pairs(dims, shift))]
    ppermute x48 -> x41, starting transfers between devices: 49.6 us -> 51.6 us  [flip(): return lax.ppermute(value, 'dp', flip_pairs(devices, bit))]
    pallas_call x1 -> x2, Pallas kernels: 24.8 us -> 24.8 us  [the longest x1 18.2 us: rest_of_factor(): pl.pallas_call(functools.partial(factor_rest, steps), out_shape=jax.Shape...]
  transfers between devices with their start and end apart: 60 -> 53, of which waited for: 30 -> 30; matrix products, arithmetic and copies ran while one was open for 7% -> 6% of each run, Pallas kernels for 13% -> 13%
where the time goes in v4:
time: 257 us
  waiting for transfers between devices  118 us (46%)
  starting transfers between devices  65.5 us (25%)
  Pallas kernels  44.1 us (17%)
  matrix products  16.6 us (6%)
  other arithmetic  5.83 us (2%)
  local copies, waits for them, and re-layouts  4.57 us (2%)
    ppermute x41, waiting for transfers between devices, flip(): return lax.ppermute(value, 'dp', flip_pairs(devices, bit))  113 us
    ppermute x41, starting transfers between devices, flip(): return lax.ppermute(value, 'dp', flip_pairs(devices, bit))  51.6 us
    pallas_call x1, Pallas kernels, rest_of_factor(): pl.pallas_call(functools.partial(factor_rest, steps), out_shape=jax.Shape...  18.2 us
    ppermute x9, starting transfers between devices, send(): return lax.ppermute(value, 'dp', shift_pairs(dims, shift))  13.8 us
    pallas_call x4, Pallas kernels, update_columns(): pl.pallas_call(functools.partial(update_kernel, scale, len(pieces)), grid...  11.7 us
    pallas_call x1, Pallas kernels, mix(): pl.pallas_call(functools.partial(mix_kernel, count, limit), grid_spec=plt...  7.59 us
    pallas_call x1, Pallas kernels, head_of_factor(): pl.pallas_call(functools.partial(factor_head, blocks, steps), out_shape=(...  6.66 us
    dot_general x4, matrix products, local(): jnp.dot(left[size:], grads[:, columns], preferred_element_type=F32)  6.24 us
  transfers between devices with their start and end apart: 53, of which 30 were waited for; matrix products, arithmetic and copies ran while one was open for 6% of the time, Pallas kernels for 13%

profile of v4, /device:TPU:0, one launch (start us, length us, event | category | flops | bytes accessed | tf_op | source)
XLA Modules:
  0.0 256.6 jit_solution(6174262179283593455)
XLA Ops:
  1.9 1.9 fusion.42
  4.0 3.0 %collective-permute-start = (f32[160,128]{1,0:T(8,128)S(1)}, f32[160,128]{1,0:T(8,128)S(1)}, u32[]{:S(2)}, u32[]{:S(2)}) collective-permute-start(f32[160,128]{1,0:T(8,128)S(1)} %get-tuple-element.259), channel_id=1, source_target_pairs={{0,2},{2,0},{4,6},{6,4},{8,10},{10,8},{12,14},{14,12},{16,18},{18,... | collective-permute-start | bytes 245768 | tf_op jit(solution)/shard_map/ppermute | solution.py:64
  8.5 3.1 %collective-permute-start.6 = (bf16[1,512,256]{2,1,0:T(8,128)(2,1)S(1)}, bf16[1,512,256]{2,1,0:T(8,128)(2,1)S(1)}, u32[]{:S(2)}, u32[]{:S(2)}) collective-permute-start(bf16[1,512,256]{2,1,0:T(8,128)(2,1)S(1)} %bitcast.45), channel_id=1, source_target_pairs={{0,16},{2,18},{4,20},{6,22},{8,24},{10,26},{12,28},{14,30},{16,0},... | collective-permute-start | bytes 786440 | tf_op jit(solution)/shard_map/ppermute | solution.py:37
  13.8 1.6 collective-permute-start.3
  15.5 2.7 %collective-permute-start.4 = (f32[160,128]{1,0:T(8,128)S(1)}, f32[160,128]{1,0:T(8,128)S(1)}, u32[]{:S(2)}, u32[]{:S(2)}) collective-permute-start(f32[160,128]{1,0:T(8,128)S(1)} %add_add_fusion), channel_id=1, source_target_pairs={{0,16},{2,18},{4,20},{6,22},{8,24},{10,26},{12,28},{14,30},{16,0},... | collective-permute-start | bytes 245768 | tf_op jit(solution)/shard_map/ppermute | solution.py:64
  19.5 1.6 collective-permute-done.3
  21.1 6.4 %collective-permute-done.6 = bf16[1,512,256]{2,1,0:T(8,128)(2,1)S(1)} collective-permute-done((bf16[1,512,256]{2,1,0:T(8,128)(2,1)S(1)}, bf16[1,512,256]{2,1,0:T(8,128)(2,1)S(1)}, u32[]{:S(2)}, u32[]{:S(2)}) %collective-permute-start.6) | collective-permute-done | bytes 262176 | tf_op jit(solution)/shard_map/ppermute | solution.py:37
  30.7 1.6 collective-permute-start.8
  35.1 3.1 %collective-permute-done.10 = bf16[2,384,256]{2,1,0:T(8,128)(2,1)S(1)} collective-permute-done((bf16[2,384,256]{2,1,0:T(8,128)(2,1)S(1)}, bf16[2,384,256]{2,1,0:T(8,128)(2,1)S(1)}, u32[]{:S(2)}, u32[]{:S(2)}) %collective-permute-start.10) | collective-permute-done | bytes 393248 | tf_op jit(solution)/shard_map/ppermute | solution.py:37
  43.0 6.7 %factor_head.1 = (f32[512,512]{1,0:T(8,128)S(1)}, f32[512,512]{1,0:T(8,128)S(1)}) custom-call(f32[1280,128]{1,0:T(8,128)S(1)} %maximum_select_fusion.2.packed_ref), custom_call_target="tpu_custom_call" | custom-call | tf_op jit(solution)/shard_map/factor_head/pallas_call | solution.py:169
  54.0 4.5 %collective-permute-done.13 = bf16[4,128,256]{2,1,0:T(8,128)(2,1)S(1)} collective-permute-done((bf16[4,128,256]{2,1,0:T(8,128)(2,1)S(1)}, bf16[4,128,256]{2,1,0:T(8,128)(2,1)S(1)}, u32[]{:S(2)}, u32[]{:S(2)}) %collective-permute-start.13) | collective-permute-done | bytes 262176 | tf_op jit(solution)/shard_map/ppermute | solution.py:37
  58.6 1.9 collective-permute-start.18
  60.7 18.2 %factor_rest.1 = f32[512,512]{1,0:T(8,128)S(1)} custom-call(f32[512,512]{1,0:T(8,128)S(1)} %get-tuple-element.144.start_ref, f32[512,512]{1,0:T(8,128)S(1)} %get-tuple-element.145.done_ref), custom_call_target="tpu_custom_call" | custom-call | tf_op jit(solution)/shard_map/factor_rest/pallas_call | solution.py:180
  78.9 7.6 %mix.1 = f32[512,256]{1,0:T(8,128)S(1)} custom-call(s32[2,3,8]{2,1,0:T(4,128)S(1)} %pad_add_fusion.table_ref, bf16[512,4096]{1,0:T(8,128)(2,1)S(1)} %copy-done.2, bf16[512,4096]{1,0:T(8,128)(2,1)} %collective-permute-done.19.right_ref, bf16[8,192,256]{2,1,0:T(8,128)(2,1)S(1)} %constant_dynamic-update-slice_fusion.11.refs_0_, ...), custom_call_target="tpu_custom_call" | custom-call | tf_op jit(solution)/shard_map/mix/pallas_call | solution.py:322
  89.5 2.5 convolution_convert_fusion.3
  92.1 2.3 convolution_convert_fusion.2
  99.4 1.9 convolution_convert_fusion.7
  106.1 14.4 %collective-permute-done.22 = bf16[256,2048]{1,0:T(8,128)(2,1)S(1)} collective-permute-done((bf16[256,2048]{1,0:T(8,128)(2,1)S(1)}, bf16[256,2048]{1,0:T(8,128)(2,1)S(1)}, u32[]{:S(2)}, u32[]{:S(2)}) %collective-permute-start.22) | collective-permute-done | bytes 1048608 | tf_op jit(solution)/shard_map/ppermute | solution.py:37
  122.2 3.4 %collective-permute-start.29 = (bf16[128,2048]{1,0:T(8,128)(2,1)S(1)}, bf16[128,2048]{1,0:T(8,128)(2,1)S(1)}, u32[]{:S(2)}, u32[]{:S(2)}) collective-permute-start(bf16[128,2048]{1,0:T(8,128)(2,1)S(1)} %slice.358), channel_id=1, source_target_pairs={{0,16},{2,18},{4,20},{6,22},{8,24},{10,26},{12,28},{14,30},{16,0},... | collective-permute-start | bytes 1572872 | tf_op jit(solution)/shard_map/ppermute | solution.py:37
  126.2 7.1 %collective-permute-done.23 = bf16[128,2048]{1,0:T(8,128)(2,1)S(1)} collective-permute-done((bf16[128,2048]{1,0:T(8,128)(2,1)S(1)}, bf16[128,2048]{1,0:T(8,128)(2,1)S(1)}, u32[]{:S(2)}, u32[]{:S(2)}) %collective-permute-start.23) | collective-permute-done | bytes 524320 | tf_op jit(solution)/shard_map/ppermute | solution.py:37
  134.3 7.9 %collective-permute-done.21 = bf16[256,2048]{1,0:T(8,128)(2,1)S(1)} collective-permute-done((bf16[256,2048]{1,0:T(8,128)(2,1)S(1)}, bf16[256,2048]{1,0:T(8,128)(2,1)S(1)}, u32[]{:S(2)}, u32[]{:S(2)}) %collective-permute-start.21) | collective-permute-done | bytes 1048608 | tf_op jit(solution)/shard_map/ppermute | solution.py:37
  144.5 2.6 %collective-permute-done.29 = bf16[128,2048]{1,0:T(8,128)(2,1)S(1)} collective-permute-done((bf16[128,2048]{1,0:T(8,128)(2,1)S(1)}, bf16[128,2048]{1,0:T(8,128)(2,1)S(1)}, u32[]{:S(2)}, u32[]{:S(2)}) %collective-permute-start.29) | collective-permute-done | bytes 524320 | tf_op jit(solution)/shard_map/ppermute | solution.py:37
  148.3 3.9 %collective-permute-done.28 = bf16[128,2048]{1,0:T(8,128)(2,1)S(1)} collective-permute-done((bf16[128,2048]{1,0:T(8,128)(2,1)S(1)}, bf16[128,2048]{1,0:T(8,128)(2,1)S(1)}, u32[]{:S(2)}, u32[]{:S(2)}) %collective-permute-start.28) | collective-permute-done | bytes 524320 | tf_op jit(solution)/shard_map/ppermute | solution.py:37
  153.3 1.7 collective-permute-done.27
  155.2 3.5 %collective-permute-done.26 = bf16[128,2048]{1,0:T(8,128)(2,1)S(1)} collective-permute-done((bf16[128,2048]{1,0:T(8,128)(2,1)S(1)}, bf16[128,2048]{1,0:T(8,128)(2,1)S(1)}, u32[]{:S(2)}, u32[]{:S(2)}) %collective-permute-start.26) | collective-permute-done | bytes 524320 | tf_op jit(solution)/shard_map/ppermute | solution.py:37
  159.1 3.5 %collective-permute-done.33 = bf16[64,2048]{1,0:T(8,128)(2,1)S(1)} collective-permute-done((bf16[64,2048]{1,0:T(8,128)(2,1)S(1)}, bf16[64,2048]{1,0:T(8,128)(2,1)S(1)}, u32[]{:S(2)}, u32[]{:S(2)}) %collective-permute-start.33) | collective-permute-done | bytes 262176 | tf_op jit(solution)/shard_map/ppermute | solution.py:37
  163.7 3.5 %collective-permute-start.38 = (bf16[32,2048]{1,0:T(8,128)(2,1)S(1)}, bf16[32,2048]{1,0:T(8,128)(2,1)S(1)}, u32[]{:S(2)}, u32[]{:S(2)}) collective-permute-start(bf16[32,2048]{1,0:T(8,128)(2,1)S(1)} %slice.365), channel_id=1, source_target_pairs={{0,16},{2,18},{4,20},{6,22},{8,24},{10,26},{12,28},{14,30},{16,0},... | collective-permute-start | bytes 393224 | tf_op jit(solution)/shard_map/ppermute | solution.py:37
  168.0 3.1 %collective-permute-start.34 = (bf16[32,2048]{1,0:T(8,128)(2,1)S(1)}, bf16[32,2048]{1,0:T(8,128)(2,1)S(1)}, u32[]{:S(2)}, u32[]{:S(2)}) collective-permute-start(bf16[32,2048]{1,0:T(8,128)(2,1)S(1)} %slice.364), channel_id=1, source_target_pairs={{0,16},{2,18},{4,20},{6,22},{8,24},{10,26},{12,28},{14,30},{16,0},... | collective-permute-start | bytes 393224 | tf_op jit(solution)/shard_map/ppermute | solution.py:37
  172.1 6.5 %collective-permute-done.38 = bf16[32,2048]{1,0:T(8,128)(2,1)S(1)} collective-permute-done((bf16[32,2048]{1,0:T(8,128)(2,1)S(1)}, bf16[32,2048]{1,0:T(8,128)(2,1)S(1)}, u32[]{:S(2)}, u32[]{:S(2)}) %collective-permute-start.38) | collective-permute-done | bytes 131104 | tf_op jit(solution)/shard_map/ppermute | solution.py:37
  178.9 4.0 %collective-permute-done.37 = bf16[32,2048]{1,0:T(8,128)(2,1)S(1)} collective-permute-done((bf16[32,2048]{1,0:T(8,128)(2,1)S(1)}, bf16[32,2048]{1,0:T(8,128)(2,1)S(1)}, u32[]{:S(2)}, u32[]{:S(2)}) %collective-permute-start.37) | collective-permute-done | bytes 131104 | tf_op jit(solution)/shard_map/ppermute | solution.py:37
  184.3 2.8 %collective-permute-done.34 = bf16[32,2048]{1,0:T(8,128)(2,1)S(1)} collective-permute-done((bf16[32,2048]{1,0:T(8,128)(2,1)S(1)}, bf16[32,2048]{1,0:T(8,128)(2,1)S(1)}, u32[]{:S(2)}, u32[]{:S(2)}) %collective-permute-start.34) | collective-permute-done | bytes 131104 | tf_op jit(solution)/shard_map/ppermute | solution.py:37
  187.9 3.4 %collective-permute-done.42 = bf16[32,2048]{1,0:T(8,128)(2,1)S(1)} collective-permute-done((bf16[32,2048]{1,0:T(8,128)(2,1)S(1)}, bf16[32,2048]{1,0:T(8,128)(2,1)S(1)}, u32[]{:S(2)}, u32[]{:S(2)}) %collective-permute-start.42) | collective-permute-done | bytes 131104 | tf_op jit(solution)/shard_map/ppermute | solution.py:37
  192.5 1.8 collective-permute-done.41
  194.4 1.8 collective-permute-start.44
  197.4 2.5 collective-permute-start.43
  200.0 6.3 %collective-permute-done.44 = bf16[128,2048]{1,0:T(8,128)(2,1)S(1)} collective-permute-done((bf16[128,2048]{1,0:T(8,128)(2,1)S(1)}, bf16[128,2048]{1,0:T(8,128)(2,1)S(1)}, u32[]{:S(2)}, u32[]{:S(2)}) %collective-permute-start.44) | collective-permute-done | bytes 524320 | tf_op jit(solution)/shard_map/ppermute | solution.py:37
  206.5 3.3 %collective-permute-start.52 = (bf16[256,2048]{1,0:T(8,128)(2,1)S(1)}, bf16[256,2048]{1,0:T(8,128)(2,1)S(1)}, u32[]{:S(2)}, u32[]{:S(2)}) collective-permute-start(bf16[256,2048]{1,0:T(8,128)(2,1)S(1)} %constant_dynamic-update-slice_fusion.31.refs_1_), channel_id=1, source_target_pairs={{0,2},{2,0},{4,6},{6,4},{8,10},{10,8},{12,14},{14,12},{16,18},{18,... | collective-permute-start | bytes 3145736 | tf_op jit(solution)/shard_map/ppermute | solution.py:37
  209.7 5.6 %collective-permute-done.43 = bf16[64,2048]{1,0:T(8,128)(2,1)S(1)} collective-permute-done((bf16[64,2048]{1,0:T(8,128)(2,1)S(1)}, bf16[64,2048]{1,0:T(8,128)(2,1)S(1)}, u32[]{:S(2)}, u32[]{:S(2)}) %collective-permute-start.43) | collective-permute-done | bytes 262176 | tf_op jit(solution)/shard_map/ppermute | solution.py:37
  215.4 2.1 collective-permute-start.46
  217.4 1.9 collective-permute-done.48
  220.1 8.3 %collective-permute-done.47 = bf16[128,2048]{1,0:T(8,128)(2,1)S(1)} collective-permute-done((bf16[128,2048]{1,0:T(8,128)(2,1)S(1)}, bf16[128,2048]{1,0:T(8,128)(2,1)S(1)}, u32[]{:S(2)}, u32[]{:S(2)}) %collective-permute-start.47) | collective-permute-done | bytes 524320 | tf_op jit(solution)/shard_map/ppermute | solution.py:37
  228.5 1.6 collective-permute-start.50
  230.2 1.6 collective-permute-start.49
  233.9 2.9 %update_columns.4.refs_3_ = f32[512,8192]{1,0:T(8,128)} custom-call(bf16[512,512]{1,0:T(8,128)(2,1)S(1)} %convolution_convert_fusion.6.refs_0_, bf16[256,2048]{1,0:T(8,128)(2,1)S(1)} %constant_dynamic-update-slice_fusion.31.refs_1_, bf16[256,2048]{1,0:T(8,128)(2,1)S(1)} %collective-permute-done.52.refs_2_), custom_call_target="tpu_custom_call" | custom-call | tf_op jit(solution)/shard_map/update_columns/pallas_call | solution.py:363
  236.8 10.9 %collective-permute-done.51.refs_2_ = bf16[256,2048]{1,0:T(8,128)(2,1)S(1)} collective-permute-done((bf16[256,2048]{1,0:T(8,128)(2,1)S(1)}, bf16[256,2048]{1,0:T(8,128)(2,1)S(1)}, u32[]{:S(2)}, u32[]{:S(2)}) %collective-permute-start.51) | collective-permute-done | bytes 1048608 | tf_op jit(solution)/shard_map/ppermute | solution.py:37
  247.7 2.9 %update_columns.5.refs_3_ = f32[512,8192]{1,0:T(8,128)} custom-call(bf16[512,512]{1,0:T(8,128)(2,1)S(1)} %convolution_convert_fusion.5.refs_0_, bf16[256,2048]{1,0:T(8,128)(2,1)S(1)} %constant_dynamic-update-slice_fusion.35.refs_1_, bf16[256,2048]{1,0:T(8,128)(2,1)S(1)} %collective-permute-done.51.refs_2_, ...), custom_call_target="tpu_custom_call", output_to_operand_aliasing={{}: (3, {})} | custom-call | tf_op jit(solution)/shard_map/update_columns/pallas_call | solution.py:363
  250.6 2.9 %update_columns.6.refs_3_ = f32[512,8192]{1,0:T(8,128)} custom-call(bf16[512,512]{1,0:T(8,128)(2,1)S(1)} %convolution_convert_fusion.4.refs_0_, bf16[256,2048]{1,0:T(8,128)(2,1)S(1)} %constant_dynamic-update-slice_fusion.37.refs_1_, bf16[256,2048]{1,0:T(8,128)(2,1)S(1)} %collective-permute-done.50.refs_2_, ...), custom_call_target="tpu_custom_call", output_to_operand_aliasing={{}: (3, {})} | custom-call | tf_op jit(solution)/shard_map/update_columns/pallas_call | solution.py:363
  253.6 2.9 %update_columns.7 = f32[512,8192]{1,0:T(8,128)} custom-call(bf16[512,512]{1,0:T(8,128)(2,1)S(1)} %convolution_convert_fusion.6.refs_0_, bf16[256,2048]{1,0:T(8,128)(2,1)S(1)} %constant_dynamic-update-slice_fusion.39.refs_1_, bf16[256,2048]{1,0:T(8,128)(2,1)S(1)} %collective-permute-done.49.refs_2_, ...), custom_call_target="tpu_custom_call", output_to_operand_aliasing={{}: (3, {})} | custom-call | tf_op jit(solution)/shard_map/update_columns/pallas_call | solution.py:363
  (245 shorter events, 53.4 us)
Async XLA Ops:
  4.0 8.1 %collective-permute-start = (f32[160,128]{1,0:T(8,128)S(1)}, f32[160,128]{1,0:T(8,128)S(1)}, u32[]{:S(2)}, u32[]{:S(2)}) collective-permute-start(f32[160,128]{1,0:T(8,128)S(1)} %get-tuple-element.259), channel_id=1, source_target_pairs={{0,2},{2,0},{4,6},{6,4},{8,10},{10,8},{12,14},{14,12},{16,18},{18,... | collective-permute-start | bytes 245768 | tf_op jit(solution)/shard_map/ppermute | solution.py:64
  8.5 19.0 %collective-permute-start.6 = (bf16[1,512,256]{2,1,0:T(8,128)(2,1)S(1)}, bf16[1,512,256]{2,1,0:T(8,128)(2,1)S(1)}, u32[]{:S(2)}, u32[]{:S(2)}) collective-permute-start(bf16[1,512,256]{2,1,0:T(8,128)(2,1)S(1)} %bitcast.45), channel_id=1, source_target_pairs={{0,16},{2,18},{4,20},{6,22},{8,24},{10,26},{12,28},{14,30},{16,0},... | collective-permute-start | bytes 786440 | tf_op jit(solution)/shard_map/ppermute | solution.py:37
  11.7 67.2 %collective-permute-start.19 = (bf16[512,4096]{1,0:T(8,128)(2,1)}, bf16[512,4096]{1,0:T(8,128)(2,1)}, u32[]{:S(2)}, u32[]{:S(2)}) collective-permute-start(bf16[512,4096]{1,0:T(8,128)(2,1)} %left_ref), channel_id=1, source_target_pairs={{0,1},{1,0},{2,3},{3,2},{4,5},{5,4},{6,7},{7,6},{8,9},{9,8},{10,11... | collective-permute-start | bytes 12582920 | tf_op jit(solution)/shard_map/ppermute | solution.py:401
  13.8 7.3 %collective-permute-start.3 = (f32[160,128]{1,0:T(8,128)S(1)}, f32[160,128]{1,0:T(8,128)S(1)}, u32[]{:S(2)}, u32[]{:S(2)}) collective-permute-start(f32[160,128]{1,0:T(8,128)S(1)} %add_add_fusion), channel_id=1, source_target_pairs={{0,8},{2,10},{4,12},{6,14},{8,16},{10,18},{12,20},{14,22},{16,24},... | collective-permute-start | bytes 245768 | tf_op jit(solution)/shard_map/ppermute | solution.py:64
  15.5 13.5 %collective-permute-start.4 = (f32[160,128]{1,0:T(8,128)S(1)}, f32[160,128]{1,0:T(8,128)S(1)}, u32[]{:S(2)}, u32[]{:S(2)}) collective-permute-start(f32[160,128]{1,0:T(8,128)S(1)} %add_add_fusion), channel_id=1, source_target_pairs={{0,16},{2,18},{4,20},{6,22},{8,24},{10,26},{12,28},{14,30},{16,0},... | collective-permute-start | bytes 245768 | tf_op jit(solution)/shard_map/ppermute | solution.py:64
  18.1 10.8 %collective-permute-start.5 = (f32[160,128]{1,0:T(8,128)S(1)}, f32[160,128]{1,0:T(8,128)S(1)}, u32[]{:S(2)}, u32[]{:S(2)}) collective-permute-start(f32[160,128]{1,0:T(8,128)S(1)} %add_add_fusion), channel_id=1, source_target_pairs={{0,24},{2,26},{4,28},{6,30},{8,0},{10,2},{12,4},{14,6},{16,8},{18,... | collective-permute-start | bytes 245768 | tf_op jit(solution)/shard_map/ppermute | solution.py:64
  27.6 10.6 %collective-permute-start.10 = (bf16[2,384,256]{2,1,0:T(8,128)(2,1)S(1)}, bf16[2,384,256]{2,1,0:T(8,128)(2,1)S(1)}, u32[]{:S(2)}, u32[]{:S(2)}) collective-permute-start(bf16[2,384,256]{2,1,0:T(8,128)(2,1)S(1)} %slice.272), channel_id=1, source_target_pairs={{0,8},{2,10},{4,12},{6,14},{8,0},{10,2},{12,4},{14,6},{16,24},{18,... | collective-permute-start | bytes 1179656 | tf_op jit(solution)/shard_map/ppermute | solution.py:37
  30.7 7.6 %collective-permute-start.8 = (f32[160,128]{1,0:T(8,128)S(1)}, f32[160,128]{1,0:T(8,128)S(1)}, u32[]{:S(2)}, u32[]{:S(2)}) collective-permute-start(f32[160,128]{1,0:T(8,128)S(1)} %get-tuple-element.246), channel_id=1, source_target_pairs={{0,4},{2,6},{4,0},{6,2},{8,12},{10,14},{12,8},{14,10},{16,20},{18,... | collective-permute-start | bytes 245768 | tf_op jit(solution)/shard_map/ppermute | solution.py:64
  32.3 6.0 %collective-permute-start.9 = (f32[160,128]{1,0:T(8,128)S(1)}, f32[160,128]{1,0:T(8,128)S(1)}, u32[]{:S(2)}, u32[]{:S(2)}) collective-permute-start(f32[160,128]{1,0:T(8,128)S(1)} %get-tuple-element.246), channel_id=1, source_target_pairs={{0,6},{2,4},{4,2},{6,0},{8,14},{10,12},{12,10},{14,8},{16,22},{18,... | collective-permute-start | bytes 245768 | tf_op jit(solution)/shard_map/ppermute | solution.py:64
  33.6 6.1 %collective-permute-start.12 = (bf16[2,128,256]{2,1,0:T(8,128)(2,1)S(1)}, bf16[2,128,256]{2,1,0:T(8,128)(2,1)S(1)}, u32[]{:S(2)}, u32[]{:S(2)}) collective-permute-start(bf16[2,128,256]{2,1,0:T(8,128)(2,1)S(1)} %slice.273), channel_id=1, source_target_pairs={{0,4},{2,6},{4,0},{6,2},{8,12},{10,14},{12,8},{14,10},{16,20},{18,... | collective-permute-start | bytes 393224 | tf_op jit(solution)/shard_map/ppermute | solution.py:37
  39.7 10.3 %collective-permute-start.15 = (bf16[4,192,256]{2,1,0:T(8,128)(2,1)S(1)}, bf16[4,192,256]{2,1,0:T(8,128)(2,1)S(1)}, u32[]{:S(2)}, u32[]{:S(2)}) collective-permute-start(bf16[4,192,256]{2,1,0:T(8,128)(2,1)S(1)} %get-tuple-element.138), channel_id=1, source_target_pairs={{0,4},{2,6},{4,0},{6,2},{8,12},{10,14},{12,8},{14,10},{16,20},{18,... | collective-permute-start | bytes 1179656 | tf_op jit(solution)/shard_map/ppermute | solution.py:37
  40.8 12.1 %collective-permute-start.14 = (bf16[4,192,256]{2,1,0:T(8,128)(2,1)S(1)}, bf16[4,192,256]{2,1,0:T(8,128)(2,1)S(1)}, u32[]{:S(2)}, u32[]{:S(2)}) collective-permute-start(bf16[4,192,256]{2,1,0:T(8,128)(2,1)S(1)} %get-tuple-element.140), channel_id=1, source_target_pairs={{0,2},{2,0},{4,6},{6,4},{8,10},{10,8},{12,14},{14,12},{16,18},{18,... | collective-permute-start | bytes 1179656 | tf_op jit(solution)/shard_map/ppermute | solution.py:37
  42.4 16.2 %collective-permute-start.13 = (bf16[4,128,256]{2,1,0:T(8,128)(2,1)S(1)}, bf16[4,128,256]{2,1,0:T(8,128)(2,1)S(1)}, u32[]{:S(2)}, u32[]{:S(2)}) collective-permute-start(bf16[4,128,256]{2,1,0:T(8,128)(2,1)S(1)} %constant_dynamic-update-slice_fusion.9), channel_id=1, source_target_pairs={{0,2},{2,0},{4,6},{6,4},{8,10},{10,8},{12,14},{14,12},{16,18},{18,... | collective-permute-start | bytes 786440 | tf_op jit(solution)/shard_map/ppermute | solution.py:37
  50.1 28.8 %collective-permute-start.16 = (bf16[8,192,256]{2,1,0:T(8,128)(2,1)S(1)}, bf16[8,192,256]{2,1,0:T(8,128)(2,1)S(1)}, u32[]{:S(2)}, u32[]{:S(2)}) collective-permute-start(bf16[8,192,256]{2,1,0:T(8,128)(2,1)S(1)} %constant_dynamic-update-slice_fusion.11.refs_0_), channel_id=1, source_target_pairs={{0,2},{2,0},{4,6},{6,4},{8,10},{10,8},{12,14},{14,12},{16,18},{18,... | collective-permute-start | bytes 2359304 | tf_op jit(solution)/shard_map/ppermute | solution.py:37
  53.0 25.9 %collective-permute-start.17 = (bf16[8,192,256]{2,1,0:T(8,128)(2,1)S(1)}, bf16[8,192,256]{2,1,0:T(8,128)(2,1)S(1)}, u32[]{:S(2)}, u32[]{:S(2)}) collective-permute-start(bf16[8,192,256]{2,1,0:T(8,128)(2,1)S(1)} %constant_dynamic-update-slice_fusion.13.refs_2_), channel_id=1, source_target_pairs={{0,4},{2,6},{4,0},{6,2},{8,12},{10,14},{12,8},{14,10},{16,20},{18,... | collective-permute-start | bytes 2359304 | tf_op jit(solution)/shard_map/ppermute | solution.py:37
  58.6 20.3 %collective-permute-start.18 = (bf16[8,128,256]{2,1,0:T(8,128)(2,1)S(1)}, bf16[8,128,256]{2,1,0:T(8,128)(2,1)S(1)}, u32[]{:S(2)}, u32[]{:S(2)}) collective-permute-start(bf16[8,128,256]{2,1,0:T(8,128)(2,1)S(1)} %constant_dynamic-update-slice_fusion.15.refs_4_), channel_id=1, source_target_pairs={{0,8},{2,10},{4,12},{6,14},{8,0},{10,2},{12,4},{14,6},{16,24},{18,... | collective-permute-start | bytes 1572872 | tf_op jit(solution)/shard_map/ppermute | solution.py:37
  94.4 26.1 %collective-permute-start.22 = (bf16[256,2048]{1,0:T(8,128)(2,1)S(1)}, bf16[256,2048]{1,0:T(8,128)(2,1)S(1)}, u32[]{:S(2)}, u32[]{:S(2)}) collective-permute-start(bf16[256,2048]{1,0:T(8,128)(2,1)S(1)} %convolution_convert_fusion.3), channel_id=1, source_target_pairs={{0,2},{2,0},{4,6},{6,4},{8,10},{10,8},{12,14},{14,12},{16,18},{18,... | collective-permute-start | bytes 3145736 | tf_op jit(solution)/shard_map/ppermute | solution.py:37
  95.2 26.4 %collective-permute-start.25 = (bf16[256,2048]{1,0:T(8,128)(2,1)S(1)}, bf16[256,2048]{1,0:T(8,128)(2,1)S(1)}, u32[]{:S(2)}, u32[]{:S(2)}) collective-permute-start(bf16[256,2048]{1,0:T(8,128)(2,1)S(1)} %convolution_convert_fusion.2), channel_id=1, source_target_pairs={{0,8},{2,10},{4,12},{6,14},{8,0},{10,2},{12,4},{14,6},{16,24},{18,... | collective-permute-start | bytes 3145736 | tf_op jit(solution)/shard_map/ppermute | solution.py:37
  97.0 28.7 %collective-permute-start.24 = (bf16[256,2048]{1,0:T(8,128)(2,1)S(1)}, bf16[256,2048]{1,0:T(8,128)(2,1)S(1)}, u32[]{:S(2)}, u32[]{:S(2)}) collective-permute-start(bf16[256,2048]{1,0:T(8,128)(2,1)S(1)} %convolution_convert_fusion.1), channel_id=1, source_target_pairs={{0,4},{2,6},{4,0},{6,2},{8,12},{10,14},{12,8},{14,10},{16,20},{18,... | collective-permute-start | bytes 3145736 | tf_op jit(solution)/shard_map/ppermute | solution.py:37
  98.3 43.9 %collective-permute-start.21 = (bf16[256,2048]{1,0:T(8,128)(2,1)S(1)}, bf16[256,2048]{1,0:T(8,128)(2,1)S(1)}, u32[]{:S(2)}, u32[]{:S(2)}) collective-permute-start(bf16[256,2048]{1,0:T(8,128)(2,1)S(1)} %convolution_convert_fusion), channel_id=1, source_target_pairs={{0,2},{2,0},{4,6},{6,4},{8,10},{10,8},{12,14},{14,12},{16,18},{18,... | collective-permute-start | bytes 3145736 | tf_op jit(solution)/shard_map/ppermute | solution.py:37
  120.9 12.4 %collective-permute-start.23 = (bf16[128,2048]{1,0:T(8,128)(2,1)S(1)}, bf16[128,2048]{1,0:T(8,128)(2,1)S(1)}, u32[]{:S(2)}, u32[]{:S(2)}) collective-permute-start(bf16[128,2048]{1,0:T(8,128)(2,1)S(1)} %slice.359), channel_id=1, source_target_pairs={{0,4},{2,6},{4,0},{6,2},{8,12},{10,14},{12,8},{14,10},{16,20},{18,... | collective-permute-start | bytes 1572872 | tf_op jit(solution)/shard_map/ppermute | solution.py:37
  122.2 24.8 %collective-permute-start.29 = (bf16[128,2048]{1,0:T(8,128)(2,1)S(1)}, bf16[128,2048]{1,0:T(8,128)(2,1)S(1)}, u32[]{:S(2)}, u32[]{:S(2)}) collective-permute-start(bf16[128,2048]{1,0:T(8,128)(2,1)S(1)} %slice.358), channel_id=1, source_target_pairs={{0,16},{2,18},{4,20},{6,22},{8,24},{10,26},{12,28},{14,30},{16,0},... | collective-permute-start | bytes 1572872 | tf_op jit(solution)/shard_map/ppermute | solution.py:37
  126.2 26.1 %collective-permute-start.28 = (bf16[128,2048]{1,0:T(8,128)(2,1)S(1)}, bf16[128,2048]{1,0:T(8,128)(2,1)S(1)}, u32[]{:S(2)}, u32[]{:S(2)}) collective-permute-start(bf16[128,2048]{1,0:T(8,128)(2,1)S(1)} %slice.357), channel_id=1, source_target_pairs={{0,8},{2,10},{4,12},{6,14},{8,0},{10,2},{12,4},{14,6},{16,24},{18,... | collective-permute-start | bytes 1572872 | tf_op jit(solution)/shard_map/ppermute | solution.py:37
  133.5 21.5 %collective-permute-start.27 = (bf16[64,2048]{1,0:T(8,128)(2,1)S(1)}, bf16[64,2048]{1,0:T(8,128)(2,1)S(1)}, u32[]{:S(2)}, u32[]{:S(2)}) collective-permute-start(bf16[64,2048]{1,0:T(8,128)(2,1)S(1)} %slice.363), channel_id=1, source_target_pairs={{0,8},{2,10},{4,12},{6,14},{8,0},{10,2},{12,4},{14,6},{16,24},{18,... | collective-permute-start | bytes 786440 | tf_op jit(solution)/shard_map/ppermute | solution.py:37
  143.8 14.9 %collective-permute-start.26 = (bf16[128,2048]{1,0:T(8,128)(2,1)S(1)}, bf16[128,2048]{1,0:T(8,128)(2,1)S(1)}, u32[]{:S(2)}, u32[]{:S(2)}) collective-permute-start(bf16[128,2048]{1,0:T(8,128)(2,1)S(1)} %slice.356), channel_id=1, source_target_pairs={{0,4},{2,6},{4,0},{6,2},{8,12},{10,14},{12,8},{14,10},{16,20},{18,... | collective-permute-start | bytes 1572872 | tf_op jit(solution)/shard_map/ppermute | solution.py:37
  147.3 15.3 %collective-permute-start.33 = (bf16[64,2048]{1,0:T(8,128)(2,1)S(1)}, bf16[64,2048]{1,0:T(8,128)(2,1)S(1)}, u32[]{:S(2)}, u32[]{:S(2)}) collective-permute-start(bf16[64,2048]{1,0:T(8,128)(2,1)S(1)} %slice.362), channel_id=1, source_target_pairs={{0,4},{2,6},{4,0},{6,2},{8,12},{10,14},{12,8},{14,10},{16,20},{18,... | collective-permute-start | bytes 786440 | tf_op jit(solution)/shard_map/ppermute | solution.py:37
  152.4 11.1 %collective-permute-start.32 = (bf16[64,2048]{1,0:T(8,128)(2,1)S(1)}, bf16[64,2048]{1,0:T(8,128)(2,1)S(1)}, u32[]{:S(2)}, u32[]{:S(2)}) collective-permute-start(bf16[64,2048]{1,0:T(8,128)(2,1)S(1)} %slice.361), channel_id=1, source_target_pairs={{0,2},{2,0},{4,6},{6,4},{8,10},{10,8},{12,14},{14,12},{16,18},{18,... | collective-permute-start | bytes 786440 | tf_op jit(solution)/shard_map/ppermute | solution.py:37
  155.2 12.1 %collective-permute-start.31 = (bf16[32,2048]{1,0:T(8,128)(2,1)S(1)}, bf16[32,2048]{1,0:T(8,128)(2,1)S(1)}, u32[]{:S(2)}, u32[]{:S(2)}) collective-permute-start(bf16[32,2048]{1,0:T(8,128)(2,1)S(1)} %slice.367), channel_id=1, source_target_pairs={{0,16},{2,18},{4,20},{6,22},{8,24},{10,26},{12,28},{14,30},{16,0},... | collective-permute-start | bytes 393224 | tf_op jit(solution)/shard_map/ppermute | solution.py:37
  158.9 9.0 %collective-permute-start.30 = (bf16[64,2048]{1,0:T(8,128)(2,1)S(1)}, bf16[64,2048]{1,0:T(8,128)(2,1)S(1)}, u32[]{:S(2)}, u32[]{:S(2)}) collective-permute-start(bf16[64,2048]{1,0:T(8,128)(2,1)S(1)} %slice.360), channel_id=1, source_target_pairs={{0,8},{2,10},{4,12},{6,14},{8,0},{10,2},{12,4},{14,6},{16,24},{18,... | collective-permute-start | bytes 786440 | tf_op jit(solution)/shard_map/ppermute | solution.py:37
  162.7 8.4 %collective-permute-start.35 = (bf16[32,2048]{1,0:T(8,128)(2,1)S(1)}, bf16[32,2048]{1,0:T(8,128)(2,1)S(1)}, u32[]{:S(2)}, u32[]{:S(2)}) collective-permute-start(bf16[32,2048]{1,0:T(8,128)(2,1)S(1)} %slice.366), channel_id=1, source_target_pairs={{0,2},{2,0},{4,6},{6,4},{8,10},{10,8},{12,14},{14,12},{16,18},{18,... | collective-permute-start | bytes 393224 | tf_op jit(solution)/shard_map/ppermute | solution.py:37
  163.7 14.9 %collective-permute-start.38 = (bf16[32,2048]{1,0:T(8,128)(2,1)S(1)}, bf16[32,2048]{1,0:T(8,128)(2,1)S(1)}, u32[]{:S(2)}, u32[]{:S(2)}) collective-permute-start(bf16[32,2048]{1,0:T(8,128)(2,1)S(1)} %slice.365), channel_id=1, source_target_pairs={{0,16},{2,18},{4,20},{6,22},{8,24},{10,26},{12,28},{14,30},{16,0},... | collective-permute-start | bytes 393224 | tf_op jit(solution)/shard_map/ppermute | solution.py:37
  167.5 15.5 %collective-permute-start.37 = (bf16[32,2048]{1,0:T(8,128)(2,1)S(1)}, bf16[32,2048]{1,0:T(8,128)(2,1)S(1)}, u32[]{:S(2)}, u32[]{:S(2)}) collective-permute-start(bf16[32,2048]{1,0:T(8,128)(2,1)S(1)} %get-tuple-element.199), channel_id=1, source_target_pairs={{0,16},{2,18},{4,20},{6,22},{8,24},{10,26},{12,28},{14,30},{16,0},... | collective-permute-start | bytes 393224 | tf_op jit(solution)/shard_map/ppermute | solution.py:37
  168.0 19.1 %collective-permute-start.34 = (bf16[32,2048]{1,0:T(8,128)(2,1)S(1)}, bf16[32,2048]{1,0:T(8,128)(2,1)S(1)}, u32[]{:S(2)}, u32[]{:S(2)}) collective-permute-start(bf16[32,2048]{1,0:T(8,128)(2,1)S(1)} %slice.364), channel_id=1, source_target_pairs={{0,16},{2,18},{4,20},{6,22},{8,24},{10,26},{12,28},{14,30},{16,0},... | collective-permute-start | bytes 393224 | tf_op jit(solution)/shard_map/ppermute | solution.py:37
  171.3 12.6 %collective-permute-start.36 = (bf16[32,2048]{1,0:T(8,128)(2,1)S(1)}, bf16[32,2048]{1,0:T(8,128)(2,1)S(1)}, u32[]{:S(2)}, u32[]{:S(2)}) collective-permute-start(bf16[32,2048]{1,0:T(8,128)(2,1)S(1)} %get-tuple-element.201), channel_id=1, source_target_pairs={{0,2},{2,0},{4,6},{6,4},{8,10},{10,8},{12,14},{14,12},{16,18},{18,... | collective-permute-start | bytes 393224 | tf_op jit(solution)/shard_map/ppermute | solution.py:37
  178.9 12.5 %collective-permute-start.42 = (bf16[32,2048]{1,0:T(8,128)(2,1)S(1)}, bf16[32,2048]{1,0:T(8,128)(2,1)S(1)}, u32[]{:S(2)}, u32[]{:S(2)}) collective-permute-start(bf16[32,2048]{1,0:T(8,128)(2,1)S(1)} %get-tuple-element.205), channel_id=1, source_target_pairs={{0,16},{2,18},{4,20},{6,22},{8,24},{10,26},{12,28},{14,30},{16,0},... | collective-permute-start | bytes 393224 | tf_op jit(solution)/shard_map/ppermute | solution.py:37
  183.0 11.3 %collective-permute-start.41 = (bf16[64,2048]{1,0:T(8,128)(2,1)S(1)}, bf16[64,2048]{1,0:T(8,128)(2,1)S(1)}, u32[]{:S(2)}, u32[]{:S(2)}) collective-permute-start(bf16[64,2048]{1,0:T(8,128)(2,1)S(1)} %constant_dynamic-update-slice_fusion.17), channel_id=1, source_target_pairs={{0,8},{2,10},{4,12},{6,14},{8,0},{10,2},{12,4},{14,6},{16,24},{18,... | collective-permute-start | bytes 786440 | tf_op jit(solution)/shard_map/ppermute | solution.py:37
  184.0 12.3 %collective-permute-start.40 = (bf16[64,2048]{1,0:T(8,128)(2,1)S(1)}, bf16[64,2048]{1,0:T(8,128)(2,1)S(1)}, u32[]{:S(2)}, u32[]{:S(2)}) collective-permute-start(bf16[64,2048]{1,0:T(8,128)(2,1)S(1)} %constant_dynamic-update-slice_fusion.19), channel_id=1, source_target_pairs={{0,4},{2,6},{4,0},{6,2},{8,12},{10,14},{12,8},{14,10},{16,20},{18,... | collective-permute-start | bytes 786440 | tf_op jit(solution)/shard_map/ppermute | solution.py:37
  187.3 10.1 %collective-permute-start.39 = (bf16[32,2048]{1,0:T(8,128)(2,1)S(1)}, bf16[32,2048]{1,0:T(8,128)(2,1)S(1)}, u32[]{:S(2)}, u32[]{:S(2)}) collective-permute-start(bf16[32,2048]{1,0:T(8,128)(2,1)S(1)} %get-tuple-element.211), channel_id=1, source_target_pairs={{0,16},{2,18},{4,20},{6,22},{8,24},{10,26},{12,28},{14,30},{16,0},... | collective-permute-start | bytes 393224 | tf_op jit(solution)/shard_map/ppermute | solution.py:37
  191.4 8.5 %collective-permute-start.45 = (bf16[64,2048]{1,0:T(8,128)(2,1)S(1)}, bf16[64,2048]{1,0:T(8,128)(2,1)S(1)}, u32[]{:S(2)}, u32[]{:S(2)}) collective-permute-start(bf16[64,2048]{1,0:T(8,128)(2,1)S(1)} %constant_dynamic-update-slice_fusion.21), channel_id=1, source_target_pairs={{0,2},{2,0},{4,6},{6,4},{8,10},{10,8},{12,14},{14,12},{16,18},{18,... | collective-permute-start | bytes 786440 | tf_op jit(solution)/shard_map/ppermute | solution.py:37
  194.4 12.0 %collective-permute-start.44 = (bf16[128,2048]{1,0:T(8,128)(2,1)S(1)}, bf16[128,2048]{1,0:T(8,128)(2,1)S(1)}, u32[]{:S(2)}, u32[]{:S(2)}) collective-permute-start(bf16[128,2048]{1,0:T(8,128)(2,1)S(1)} %constant_dynamic-update-slice_fusion.23), channel_id=1, source_target_pairs={{0,4},{2,6},{4,0},{6,2},{8,12},{10,14},{12,8},{14,10},{16,20},{18,... | collective-permute-start | bytes 1572872 | tf_op jit(solution)/shard_map/ppermute | solution.py:37
  196.3 23.1 %collective-permute-start.48 = (bf16[128,2048]{1,0:T(8,128)(2,1)S(1)}, bf16[128,2048]{1,0:T(8,128)(2,1)S(1)}, u32[]{:S(2)}, u32[]{:S(2)}) collective-permute-start(bf16[128,2048]{1,0:T(8,128)(2,1)S(1)} %constant_dynamic-update-slice_fusion.25), channel_id=1, source_target_pairs={{0,16},{2,18},{4,20},{6,22},{8,24},{10,26},{12,28},{14,30},{16,0},... | collective-permute-start | bytes 1572872 | tf_op jit(solution)/shard_map/ppermute | solution.py:37
  197.4 18.0 %collective-permute-start.43 = (bf16[64,2048]{1,0:T(8,128)(2,1)S(1)}, bf16[64,2048]{1,0:T(8,128)(2,1)S(1)}, u32[]{:S(2)}, u32[]{:S(2)}) collective-permute-start(bf16[64,2048]{1,0:T(8,128)(2,1)S(1)} %constant_dynamic-update-slice_fusion.27), channel_id=1, source_target_pairs={{0,8},{2,10},{4,12},{6,14},{8,0},{10,2},{12,4},{14,6},{16,24},{18,... | collective-permute-start | bytes 786440 | tf_op jit(solution)/shard_map/ppermute | solution.py:37
  200.0 28.4 %collective-permute-start.47 = (bf16[128,2048]{1,0:T(8,128)(2,1)S(1)}, bf16[128,2048]{1,0:T(8,128)(2,1)S(1)}, u32[]{:S(2)}, u32[]{:S(2)}) collective-permute-start(bf16[128,2048]{1,0:T(8,128)(2,1)S(1)} %constant_dynamic-update-slice_fusion.29), channel_id=1, source_target_pairs={{0,8},{2,10},{4,12},{6,14},{8,0},{10,2},{12,4},{14,6},{16,24},{18,... | collective-permute-start | bytes 1572872 | tf_op jit(solution)/shard_map/ppermute | solution.py:37
  206.5 27.4 %collective-permute-start.52 = (bf16[256,2048]{1,0:T(8,128)(2,1)S(1)}, bf16[256,2048]{1,0:T(8,128)(2,1)S(1)}, u32[]{:S(2)}, u32[]{:S(2)}) collective-permute-start(bf16[256,2048]{1,0:T(8,128)(2,1)S(1)} %constant_dynamic-update-slice_fusion.31.refs_1_), channel_id=1, source_target_pairs={{0,2},{2,0},{4,6},{6,4},{8,10},{10,8},{12,14},{14,12},{16,18},{18,... | collective-permute-start | bytes 3145736 | tf_op jit(solution)/shard_map/ppermute | solution.py:37
  215.4 14.7 %collective-permute-start.46 = (bf16[128,2048]{1,0:T(8,128)(2,1)S(1)}, bf16[128,2048]{1,0:T(8,128)(2,1)S(1)}, u32[]{:S(2)}, u32[]{:S(2)}) collective-permute-start(bf16[128,2048]{1,0:T(8,128)(2,1)S(1)} %constant_dynamic-update-slice_fusion.33), channel_id=1, source_target_pairs={{0,4},{2,6},{4,0},{6,2},{8,12},{10,14},{12,8},{14,10},{16,20},{18,... | collective-permute-start | bytes 1572872 | tf_op jit(solution)/shard_map/ppermute | solution.py:37
  219.4 28.3 %collective-permute-start.51 = (bf16[256,2048]{1,0:T(8,128)(2,1)S(1)}, bf16[256,2048]{1,0:T(8,128)(2,1)S(1)}, u32[]{:S(2)}, u32[]{:S(2)}) collective-permute-start(bf16[256,2048]{1,0:T(8,128)(2,1)S(1)} %constant_dynamic-update-slice_fusion.35.refs_1_), channel_id=1, source_target_pairs={{0,8},{2,10},{4,12},{6,14},{8,0},{10,2},{12,4},{14,6},{16,24},{18,... | collective-permute-start | bytes 3145736 | tf_op jit(solution)/shard_map/ppermute | solution.py:37
  228.5 19.3 %collective-permute-start.50 = (bf16[256,2048]{1,0:T(8,128)(2,1)S(1)}, bf16[256,2048]{1,0:T(8,128)(2,1)S(1)}, u32[]{:S(2)}, u32[]{:S(2)}) collective-permute-start(bf16[256,2048]{1,0:T(8,128)(2,1)S(1)} %constant_dynamic-update-slice_fusion.37.refs_1_), channel_id=1, source_target_pairs={{0,4},{2,6},{4,0},{6,2},{8,12},{10,14},{12,8},{14,10},{16,20},{18,... | collective-permute-start | bytes 3145736 | tf_op jit(solution)/shard_map/ppermute | solution.py:37
  230.2 23.5 %collective-permute-start.49 = (bf16[256,2048]{1,0:T(8,128)(2,1)S(1)}, bf16[256,2048]{1,0:T(8,128)(2,1)S(1)}, u32[]{:S(2)}, u32[]{:S(2)}) collective-permute-start(bf16[256,2048]{1,0:T(8,128)(2,1)S(1)} %constant_dynamic-update-slice_fusion.39.refs_1_), channel_id=1, source_target_pairs={{0,2},{2,0},{4,6},{6,4},{8,10},{10,8},{12,14},{14,12},{16,18},{18,... | collective-permute-start | bytes 3145736 | tf_op jit(solution)/shard_map/ppermute | solution.py:37
  (30 other events, 179.3 us)

commit v5 on v4

--- a/solution.py
+++ b/solution.py
@@ -22,11 +22,11 @@
 PIVOTS = 8
 VMEM_LIMIT = 40 << 20
 
-GROUPS = ((2, (0, 1, 2, 3)), (2, (2, 3, 1, 0)), (2, (1, 2, 0, 3)), (2, (0, 1, 2, 3)))
-STEPS = ((0, 0), (1, 0), (2, 0), (3, 0), (0, 1), (1, 1), (2, 1), (0, 2), (3, 1), (1, 2), (2, 2), (0, 3), (3, 2), (1, 3), (2, 3), (0, 4), (3, 3), (1, 4), (2, 4), (0, 5), (1, 5), (3, 4), (2, 5), (0, 6), (1, 6), (3, 5), (2, 6), (0, 7), (3, 6), (1, 7), (2, 7), (3, 7), (0, 8), (1, 8), (2, 8), (3, 8))
-
-
-GATHER = ((3, (0, 1, 2, 3)), (3, (1, 0, 2, 3)), (2, (2, 0, 1, 3)))
+GROUPS = ((2, (2, 1, 0, 3)), (2, (1, 0, 2, 3)), (2, (0, 1, 2, 3)), (2, (2, 0, 1, 3)))
+STEPS = ((0, 0), (1, 0), (2, 0), (3, 0), (0, 1), (1, 1), (2, 1), (0, 2), (1, 2), (3, 1), (0, 3), (2, 2), (1, 3), (0, 4), (2, 3), (3, 2), (1, 4), (3, 3), (0, 5), (2, 4), (0, 6), (1, 5), (3, 4), (2, 5), (0, 7), (1, 6), (3, 5), (2, 6), (3, 6), (1, 7), (2, 7), (3, 7), (0, 8), (1, 8), (2, 8), (3, 8))
+
+
+GATHER = ((3, (0, 1, 2, 3)), (3, (1, 0, 2, 3)), (2, (2, 1, 0, 3)))
 
 
 def flip_pairs(devices, bit):

time: 257 us -> 264 us (1.027)
  waiting for transfers between devices: 118 us -> 105 us
  Pallas kernels: 44.1 us -> 56.4 us
  starting transfers between devices: 65.5 us -> 69 us
    ppermute x41, waiting for transfers between devices: 113 us -> 99.9 us  [flip(): return lax.ppermute(value, 'dp', flip_pairs(devices, bit))]
    pallas_call x1, Pallas kernels: 18.2 us -> 30.5 us  [rest_of_factor(): pl.pallas_call(functools.partial(factor_rest, steps), out_shape=jax.Shape...]
    ppermute x41, starting transfers between devices: 51.6 us -> 55.1 us  [flip(): return lax.ppermute(value, 'dp', flip_pairs(devices, bit))]
  transfers between devices with their start and end apart: 53 -> 53, of which waited for: 30 -> 31; matrix products, arithmetic and copies ran while one was open for 6% -> 6% of each run, Pallas kernels for 13% -> 18%
where the time goes in v5:
time: 264 us; the launch traced here: 262 us
  waiting for transfers between devices  105 us (40%)
  starting transfers between devices  69 us (26%)
  Pallas kernels  56.4 us (21%)
  matrix products  17.2 us (7%)
  local copies, waits for them, and re-layouts  6.42 us (2%)
  other arithmetic  5.89 us (2%)
    ppermute x41, waiting for transfers between devices, flip(): return lax.ppermute(value, 'dp', flip_pairs(devices, bit))  99.9 us
    ppermute x41, starting transfers between devices, flip(): return lax.ppermute(value, 'dp', flip_pairs(devices, bit))  55.1 us
    pallas_call x1, Pallas kernels, rest_of_factor(): pl.pallas_call(functools.partial(factor_rest, steps), out_shape=jax.Shape...  30.5 us
    ppermute x9, starting transfers between devices, send(): return lax.ppermute(value, 'dp', shift_pairs(dims, shift))  13.8 us
    pallas_call x4, Pallas kernels, update_columns(): pl.pallas_call(functools.partial(update_kernel, scale, len(pieces)), grid...  11.7 us
    pallas_call x1, Pallas kernels, mix(): pl.pallas_call(functools.partial(mix_kernel, count, limit), grid_spec=plt...  7.59 us
    pallas_call x1, Pallas kernels, head_of_factor(): pl.pallas_call(functools.partial(factor_head, blocks, steps), out_shape=(...  6.66 us
    dot_general x4, matrix products, local(): jnp.dot(left[size:], grads[:, columns], preferred_element_type=F32)  6.27 us
  transfers between devices with their start and end apart: 53, of which 31 were waited for; matrix products, arithmetic and copies ran while one was open for 6% of the time, Pallas kernels for 18%

profile of v5, /device:TPU:0, one launch (start us, length us, event | category | flops | bytes accessed | tf_op | source)
XLA Modules:
  0.0 262.0 jit_solution(14543089071825774303)
XLA Ops:
  1.9 1.9 fusion.40
  4.0 3.0 %collective-permute-start = (f32[160,128]{1,0:T(8,128)S(1)}, f32[160,128]{1,0:T(8,128)S(1)}, u32[]{:S(2)}, u32[]{:S(2)}) collective-permute-start(f32[160,128]{1,0:T(8,128)S(1)} %get-tuple-element.263), channel_id=1, source_target_pairs={{0,2},{2,0},{4,6},{6,4},{8,10},{10,8},{12,14},{14,12},{16,18},{18,... | collective-permute-start | bytes 245768 | tf_op jit(solution)/shard_map/ppermute | solution.py:64
  8.5 3.1 %collective-permute-start.6 = (bf16[1,512,256]{2,1,0:T(8,128)(2,1)S(1)}, bf16[1,512,256]{2,1,0:T(8,128)(2,1)S(1)}, u32[]{:S(2)}, u32[]{:S(2)}) collective-permute-start(bf16[1,512,256]{2,1,0:T(8,128)(2,1)S(1)} %bitcast.57), channel_id=1, source_target_pairs={{0,16},{2,18},{4,20},{6,22},{8,24},{10,26},{12,28},{14,30},{16,0},... | collective-permute-start | bytes 786440 | tf_op jit(solution)/shard_map/ppermute | solution.py:37
  15.5 2.6 %collective-permute-start.4 = (f32[160,128]{1,0:T(8,128)S(1)}, f32[160,128]{1,0:T(8,128)S(1)}, u32[]{:S(2)}, u32[]{:S(2)}) collective-permute-start(f32[160,128]{1,0:T(8,128)S(1)} %add_add_fusion), channel_id=1, source_target_pairs={{0,16},{2,18},{4,20},{6,22},{8,24},{10,26},{12,28},{14,30},{16,0},... | collective-permute-start | bytes 245768 | tf_op jit(solution)/shard_map/ppermute | solution.py:64
  21.1 6.4 %collective-permute-done.6 = bf16[1,512,256]{2,1,0:T(8,128)(2,1)S(1)} collective-permute-done((bf16[1,512,256]{2,1,0:T(8,128)(2,1)S(1)}, bf16[1,512,256]{2,1,0:T(8,128)(2,1)S(1)}, u32[]{:S(2)}, u32[]{:S(2)}) %collective-permute-start.6) | collective-permute-done | bytes 262176 | tf_op jit(solution)/shard_map/ppermute | solution.py:37
  33.6 2.2 collective-permute-start.12
  35.8 2.4 collective-permute-done.10
  40.3 2.1 collective-permute-start.14
  43.0 6.7 %factor_head.1 = (f32[512,512]{1,0:T(8,128)S(1)}, f32[512,512]{1,0:T(8,128)S(1)}) custom-call(f32[1280,128]{1,0:T(8,128)S(1)} %maximum_select_fusion.2.packed_ref), custom_call_target="tpu_custom_call" | custom-call | tf_op jit(solution)/shard_map/factor_head/pallas_call | solution.py:169
  50.7 2.2 collective-permute-start.16
  54.6 1.7 collective-permute-done.13
  56.3 1.9 collective-permute-start.18
  58.4 30.5 %factor_rest.1 = f32[512,512]{1,0:T(8,128)S(1)} custom-call(f32[512,512]{1,0:T(8,128)S(1)} %get-tuple-element.145.start_ref, f32[512,512]{1,0:T(8,128)S(1)} %get-tuple-element.146.done_ref), custom_call_target="tpu_custom_call" | custom-call | tf_op jit(solution)/shard_map/factor_rest/pallas_call | solution.py:180
  88.9 7.6 %mix.1 = f32[512,256]{1,0:T(8,128)S(1)} custom-call(s32[2,3,8]{2,1,0:T(4,128)S(1)} %pad_add_fusion.table_ref, bf16[512,4096]{1,0:T(8,128)(2,1)S(1)} %copy-done.2, bf16[512,4096]{1,0:T(8,128)(2,1)} %collective-permute-done.19.right_ref, bf16[8,192,256]{2,1,0:T(8,128)(2,1)S(1)} %constant_dynamic-update-slice_fusion.11.refs_0_, ...), custom_call_target="tpu_custom_call" | custom-call | tf_op jit(solution)/shard_map/mix/pallas_call | solution.py:322
  99.6 2.5 convolution_convert_fusion.3
  102.1 2.3 convolution_convert_fusion.2
  107.1 2.1 collective-permute-start.26
  111.1 1.9 convolution_convert_fusion.8
  118.4 12.9 %collective-permute-done.23 = bf16[256,2048]{1,0:T(8,128)(2,1)S(1)} collective-permute-done((bf16[256,2048]{1,0:T(8,128)(2,1)S(1)}, bf16[256,2048]{1,0:T(8,128)(2,1)S(1)}, u32[]{:S(2)}, u32[]{:S(2)}) %collective-permute-start.23) | collective-permute-done | bytes 1048608 | tf_op jit(solution)/shard_map/ppermute | solution.py:37
  137.5 9.2 %collective-permute-done.25 = bf16[128,2048]{1,0:T(8,128)(2,1)S(1)} collective-permute-done((bf16[128,2048]{1,0:T(8,128)(2,1)S(1)}, bf16[128,2048]{1,0:T(8,128)(2,1)S(1)}, u32[]{:S(2)}, u32[]{:S(2)}) %collective-permute-start.25) | collective-permute-done | bytes 524320 | tf_op jit(solution)/shard_map/ppermute | solution.py:37
  149.8 4.1 %collective-permute-done.21 = bf16[256,2048]{1,0:T(8,128)(2,1)S(1)} collective-permute-done((bf16[256,2048]{1,0:T(8,128)(2,1)S(1)}, bf16[256,2048]{1,0:T(8,128)(2,1)S(1)}, u32[]{:S(2)}, u32[]{:S(2)}) %collective-permute-start.21) | collective-permute-done | bytes 1048608 | tf_op jit(solution)/shard_map/ppermute | solution.py:37
  157.0 3.6 %collective-permute-start.31 = (bf16[32,2048]{1,0:T(8,128)(2,1)S(1)}, bf16[32,2048]{1,0:T(8,128)(2,1)S(1)}, u32[]{:S(2)}, u32[]{:S(2)}) collective-permute-start(bf16[32,2048]{1,0:T(8,128)(2,1)S(1)} %slice.373), channel_id=1, source_target_pairs={{0,16},{2,18},{4,20},{6,22},{8,24},{10,26},{12,28},{14,30},{16,0},... | collective-permute-start | bytes 393224 | tf_op jit(solution)/shard_map/ppermute | solution.py:37
  161.3 1.8 collective-permute-start.34
  163.1 3.9 %collective-permute-done.31 = bf16[32,2048]{1,0:T(8,128)(2,1)S(1)} collective-permute-done((bf16[32,2048]{1,0:T(8,128)(2,1)S(1)}, bf16[32,2048]{1,0:T(8,128)(2,1)S(1)}, u32[]{:S(2)}, u32[]{:S(2)}) %collective-permute-start.31) | collective-permute-done | bytes 131104 | tf_op jit(solution)/shard_map/ppermute | solution.py:37
  168.2 4.6 %collective-permute-done.30 = bf16[64,2048]{1,0:T(8,128)(2,1)S(1)} collective-permute-done((bf16[64,2048]{1,0:T(8,128)(2,1)S(1)}, bf16[64,2048]{1,0:T(8,128)(2,1)S(1)}, u32[]{:S(2)}, u32[]{:S(2)}) %collective-permute-start.30) | collective-permute-done | bytes 262176 | tf_op jit(solution)/shard_map/ppermute | solution.py:37
  175.4 2.5 collective-permute-start.36
  177.9 2.2 collective-permute-done.33
  180.2 2.5 collective-permute-start.35
  182.7 2.6 collective-permute-done.37
  185.4 5.5 %collective-permute-done.39 = bf16[32,2048]{1,0:T(8,128)(2,1)S(1)} collective-permute-done((bf16[32,2048]{1,0:T(8,128)(2,1)S(1)}, bf16[32,2048]{1,0:T(8,128)(2,1)S(1)}, u32[]{:S(2)}, u32[]{:S(2)}) %collective-permute-start.39) | collective-permute-done | bytes 131104 | tf_op jit(solution)/shard_map/ppermute | solution.py:37
  193.7 1.8 collective-permute-start.41
  195.5 2.5 collective-permute-done.35
  198.3 3.9 %collective-permute-done.43 = bf16[32,2048]{1,0:T(8,128)(2,1)S(1)} collective-permute-done((bf16[32,2048]{1,0:T(8,128)(2,1)S(1)}, bf16[32,2048]{1,0:T(8,128)(2,1)S(1)}, u32[]{:S(2)}, u32[]{:S(2)}) %collective-permute-start.43) | collective-permute-done | bytes 131104 | tf_op jit(solution)/shard_map/ppermute | solution.py:37
  202.4 2.1 collective-permute-start.52
  204.5 3.4 %collective-permute-done.41 = bf16[64,2048]{1,0:T(8,128)(2,1)S(1)} collective-permute-done((bf16[64,2048]{1,0:T(8,128)(2,1)S(1)}, bf16[64,2048]{1,0:T(8,128)(2,1)S(1)}, u32[]{:S(2)}, u32[]{:S(2)}) %collective-permute-start.41) | collective-permute-done | bytes 262176 | tf_op jit(solution)/shard_map/ppermute | solution.py:37
  211.2 2.3 collective-permute-done.45
  213.5 1.7 collective-permute-start.47
  215.2 3.4 %collective-permute-done.44 = bf16[64,2048]{1,0:T(8,128)(2,1)S(1)} collective-permute-done((bf16[64,2048]{1,0:T(8,128)(2,1)S(1)}, bf16[64,2048]{1,0:T(8,128)(2,1)S(1)}, u32[]{:S(2)}, u32[]{:S(2)}) %collective-permute-start.44) | collective-permute-done | bytes 262176 | tf_op jit(solution)/shard_map/ppermute | solution.py:37
  218.7 4.1 %collective-permute-done.48 = bf16[128,2048]{1,0:T(8,128)(2,1)S(1)} collective-permute-done((bf16[128,2048]{1,0:T(8,128)(2,1)S(1)}, bf16[128,2048]{1,0:T(8,128)(2,1)S(1)}, u32[]{:S(2)}, u32[]{:S(2)}) %collective-permute-start.48) | collective-permute-done | bytes 524320 | tf_op jit(solution)/shard_map/ppermute | solution.py:37
  222.9 1.7 collective-permute-start.51
  224.6 5.2 %collective-permute-done.47 = bf16[128,2048]{1,0:T(8,128)(2,1)S(1)} collective-permute-done((bf16[128,2048]{1,0:T(8,128)(2,1)S(1)}, bf16[128,2048]{1,0:T(8,128)(2,1)S(1)}, u32[]{:S(2)}, u32[]{:S(2)}) %collective-permute-start.47) | collective-permute-done | bytes 524320 | tf_op jit(solution)/shard_map/ppermute | solution.py:37
  230.2 2.8 %collective-permute-done.46 = bf16[128,2048]{1,0:T(8,128)(2,1)S(1)} collective-permute-done((bf16[128,2048]{1,0:T(8,128)(2,1)S(1)}, bf16[128,2048]{1,0:T(8,128)(2,1)S(1)}, u32[]{:S(2)}, u32[]{:S(2)}) %collective-permute-start.46) | collective-permute-done | bytes 524320 | tf_op jit(solution)/shard_map/ppermute | solution.py:37
  236.0 2.9 %update_columns.4.refs_3_ = f32[512,8192]{1,0:T(8,128)} custom-call(bf16[512,512]{1,0:T(8,128)(2,1)S(1)} %convolution_convert_fusion.6.refs_0_, bf16[256,2048]{1,0:T(8,128)(2,1)S(1)} %constant_dynamic-update-slice_fusion.25.refs_1_, bf16[256,2048]{1,0:T(8,128)(2,1)S(1)} %collective-permute-done.52.refs_2_), custom_call_target="tpu_custom_call" | custom-call | tf_op jit(solution)/shard_map/update_columns/pallas_call | solution.py:363
  238.9 10.9 %collective-permute-done.51.refs_2_ = bf16[256,2048]{1,0:T(8,128)(2,1)S(1)} collective-permute-done((bf16[256,2048]{1,0:T(8,128)(2,1)S(1)}, bf16[256,2048]{1,0:T(8,128)(2,1)S(1)}, u32[]{:S(2)}, u32[]{:S(2)}) %collective-permute-start.51) | collective-permute-done | bytes 1048608 | tf_op jit(solution)/shard_map/ppermute | solution.py:37
  249.8 3.0 %collective-permute-done.50.refs_2_ = bf16[256,2048]{1,0:T(8,128)(2,1)S(1)} collective-permute-done((bf16[256,2048]{1,0:T(8,128)(2,1)S(1)}, bf16[256,2048]{1,0:T(8,128)(2,1)S(1)}, u32[]{:S(2)}, u32[]{:S(2)}) %collective-permute-start.50) | collective-permute-done | bytes 1048608 | tf_op jit(solution)/shard_map/ppermute | solution.py:37
  252.8 2.9 %update_columns.5.refs_3_ = f32[512,8192]{1,0:T(8,128)} custom-call(bf16[512,512]{1,0:T(8,128)(2,1)S(1)} %convolution_convert_fusion.5.refs_0_, bf16[256,2048]{1,0:T(8,128)(2,1)S(1)} %constant_dynamic-update-slice_fusion.35.refs_1_, bf16[256,2048]{1,0:T(8,128)(2,1)S(1)} %collective-permute-done.51.refs_2_, ...), custom_call_target="tpu_custom_call", output_to_operand_aliasing={{}: (3, {})} | custom-call | tf_op jit(solution)/shard_map/update_columns/pallas_call | solution.py:363
  255.7 2.9 %update_columns.6.refs_3_ = f32[512,8192]{1,0:T(8,128)} custom-call(bf16[512,512]{1,0:T(8,128)(2,1)S(1)} %convolution_convert_fusion.4.refs_0_, bf16[256,2048]{1,0:T(8,128)(2,1)S(1)} %constant_dynamic-update-slice_fusion.37.refs_1_, bf16[256,2048]{1,0:T(8,128)(2,1)S(1)} %collective-permute-done.50.refs_2_, ...), custom_call_target="tpu_custom_call", output_to_operand_aliasing={{}: (3, {})} | custom-call | tf_op jit(solution)/shard_map/update_columns/pallas_call | solution.py:363
  258.6 2.9 %update_columns.7 = f32[512,8192]{1,0:T(8,128)} custom-call(bf16[512,512]{1,0:T(8,128)(2,1)S(1)} %convolution_convert_fusion.7.refs_0_, bf16[256,2048]{1,0:T(8,128)(2,1)S(1)} %constant_dynamic-update-slice_fusion.39.refs_1_, bf16[256,2048]{1,0:T(8,128)(2,1)S(1)} %collective-permute-done.49.refs_2_, ...), custom_call_target="tpu_custom_call", output_to_operand_aliasing={{}: (3, {})} | custom-call | tf_op jit(solution)/shard_map/update_columns/pallas_call | solution.py:363
  (246 shorter events, 60.8 us)
Async XLA Ops:
  4.0 8.1 %collective-permute-start = (f32[160,128]{1,0:T(8,128)S(1)}, f32[160,128]{1,0:T(8,128)S(1)}, u32[]{:S(2)}, u32[]{:S(2)}) collective-permute-start(f32[160,128]{1,0:T(8,128)S(1)} %get-tuple-element.263), channel_id=1, source_target_pairs={{0,2},{2,0},{4,6},{6,4},{8,10},{10,8},{12,14},{14,12},{16,18},{18,... | collective-permute-start | bytes 245768 | tf_op jit(solution)/shard_map/ppermute | solution.py:64
  8.5 5.3 %collective-permute-start.2 = (f32[160,128]{1,0:T(8,128)S(1)}, f32[160,128]{1,0:T(8,128)S(1)}, u32[]{:S(2)}, u32[]{:S(2)}) collective-permute-start(f32[160,128]{1,0:T(8,128)S(1)} %get-tuple-element.261), channel_id=1, source_target_pairs={{0,6},{2,4},{4,2},{6,0},{8,14},{10,12},{12,10},{14,8},{16,22},{18,... | collective-permute-start | bytes 245768 | tf_op jit(solution)/shard_map/ppermute | solution.py:64
  8.5 19.0 %collective-permute-start.6 = (bf16[1,512,256]{2,1,0:T(8,128)(2,1)S(1)}, bf16[1,512,256]{2,1,0:T(8,128)(2,1)S(1)}, u32[]{:S(2)}, u32[]{:S(2)}) collective-permute-start(bf16[1,512,256]{2,1,0:T(8,128)(2,1)S(1)} %bitcast.57), channel_id=1, source_target_pairs={{0,16},{2,18},{4,20},{6,22},{8,24},{10,26},{12,28},{14,30},{16,0},... | collective-permute-start | bytes 786440 | tf_op jit(solution)/shard_map/ppermute | solution.py:37
  11.7 77.2 %collective-permute-start.19 = (bf16[512,4096]{1,0:T(8,128)(2,1)}, bf16[512,4096]{1,0:T(8,128)(2,1)}, u32[]{:S(2)}, u32[]{:S(2)}) collective-permute-start(bf16[512,4096]{1,0:T(8,128)(2,1)} %left_ref), channel_id=1, source_target_pairs={{0,1},{1,0},{2,3},{3,2},{4,5},{5,4},{6,7},{7,6},{8,9},{9,8},{10,11... | collective-permute-start | bytes 12582920 | tf_op jit(solution)/shard_map/ppermute | solution.py:401
  13.8 7.2 %collective-permute-start.3 = (f32[160,128]{1,0:T(8,128)S(1)}, f32[160,128]{1,0:T(8,128)S(1)}, u32[]{:S(2)}, u32[]{:S(2)}) collective-permute-start(f32[160,128]{1,0:T(8,128)S(1)} %add_add_fusion), channel_id=1, source_target_pairs={{0,8},{2,10},{4,12},{6,14},{8,16},{10,18},{12,20},{14,22},{16,24},... | collective-permute-start | bytes 245768 | tf_op jit(solution)/shard_map/ppermute | solution.py:64
  15.5 13.5 %collective-permute-start.4 = (f32[160,128]{1,0:T(8,128)S(1)}, f32[160,128]{1,0:T(8,128)S(1)}, u32[]{:S(2)}, u32[]{:S(2)}) collective-permute-start(f32[160,128]{1,0:T(8,128)S(1)} %add_add_fusion), channel_id=1, source_target_pairs={{0,16},{2,18},{4,20},{6,22},{8,24},{10,26},{12,28},{14,30},{16,0},... | collective-permute-start | bytes 245768 | tf_op jit(solution)/shard_map/ppermute | solution.py:64
  18.1 10.9 %collective-permute-start.5 = (f32[160,128]{1,0:T(8,128)S(1)}, f32[160,128]{1,0:T(8,128)S(1)}, u32[]{:S(2)}, u32[]{:S(2)}) collective-permute-start(f32[160,128]{1,0:T(8,128)S(1)} %add_add_fusion), channel_id=1, source_target_pairs={{0,24},{2,26},{4,28},{6,30},{8,0},{10,2},{12,4},{14,6},{16,8},{18,... | collective-permute-start | bytes 245768 | tf_op jit(solution)/shard_map/ppermute | solution.py:64
  27.6 10.6 %collective-permute-start.10 = (bf16[2,384,256]{2,1,0:T(8,128)(2,1)S(1)}, bf16[2,384,256]{2,1,0:T(8,128)(2,1)S(1)}, u32[]{:S(2)}, u32[]{:S(2)}) collective-permute-start(bf16[2,384,256]{2,1,0:T(8,128)(2,1)S(1)} %slice.279), channel_id=1, source_target_pairs={{0,8},{2,10},{4,12},{6,14},{8,0},{10,2},{12,4},{14,6},{16,24},{18,... | collective-permute-start | bytes 1179656 | tf_op jit(solution)/shard_map/ppermute | solution.py:37
  30.7 7.6 %collective-permute-start.8 = (f32[160,128]{1,0:T(8,128)S(1)}, f32[160,128]{1,0:T(8,128)S(1)}, u32[]{:S(2)}, u32[]{:S(2)}) collective-permute-start(f32[160,128]{1,0:T(8,128)S(1)} %get-tuple-element.248), channel_id=1, source_target_pairs={{0,4},{2,6},{4,0},{6,2},{8,12},{10,14},{12,8},{14,10},{16,20},{18,... | collective-permute-start | bytes 245768 | tf_op jit(solution)/shard_map/ppermute | solution.py:64
  32.3 6.0 %collective-permute-start.9 = (f32[160,128]{1,0:T(8,128)S(1)}, f32[160,128]{1,0:T(8,128)S(1)}, u32[]{:S(2)}, u32[]{:S(2)}) collective-permute-start(f32[160,128]{1,0:T(8,128)S(1)} %get-tuple-element.248), channel_id=1, source_target_pairs={{0,6},{2,4},{4,2},{6,0},{8,14},{10,12},{12,10},{14,8},{16,22},{18,... | collective-permute-start | bytes 245768 | tf_op jit(solution)/shard_map/ppermute | solution.py:64
  38.7 11.9 %collective-permute-start.15 = (bf16[4,192,256]{2,1,0:T(8,128)(2,1)S(1)}, bf16[4,192,256]{2,1,0:T(8,128)(2,1)S(1)}, u32[]{:S(2)}, u32[]{:S(2)}) collective-permute-start(bf16[4,192,256]{2,1,0:T(8,128)(2,1)S(1)} %get-tuple-element.139), channel_id=1, source_target_pairs={{0,4},{2,6},{4,0},{6,2},{8,12},{10,14},{12,8},{14,10},{16,20},{18,... | collective-permute-start | bytes 1179656 | tf_op jit(solution)/shard_map/ppermute | solution.py:37
  40.3 12.6 %collective-permute-start.14 = (bf16[4,192,256]{2,1,0:T(8,128)(2,1)S(1)}, bf16[4,192,256]{2,1,0:T(8,128)(2,1)S(1)}, u32[]{:S(2)}, u32[]{:S(2)}) collective-permute-start(bf16[4,192,256]{2,1,0:T(8,128)(2,1)S(1)} %get-tuple-element.141), channel_id=1, source_target_pairs={{0,2},{2,0},{4,6},{6,4},{8,10},{10,8},{12,14},{14,12},{16,18},{18,... | collective-permute-start | bytes 1179656 | tf_op jit(solution)/shard_map/ppermute | solution.py:37
  42.4 13.9 %collective-permute-start.13 = (bf16[4,128,256]{2,1,0:T(8,128)(2,1)S(1)}, bf16[4,128,256]{2,1,0:T(8,128)(2,1)S(1)}, u32[]{:S(2)}, u32[]{:S(2)}) collective-permute-start(bf16[4,128,256]{2,1,0:T(8,128)(2,1)S(1)} %constant_dynamic-update-slice_fusion.9), channel_id=1, source_target_pairs={{0,4},{2,6},{4,0},{6,2},{8,12},{10,14},{12,8},{14,10},{16,20},{18,... | collective-permute-start | bytes 786440 | tf_op jit(solution)/shard_map/ppermute | solution.py:37
  50.7 38.1 %collective-permute-start.16 = (bf16[8,192,256]{2,1,0:T(8,128)(2,1)S(1)}, bf16[8,192,256]{2,1,0:T(8,128)(2,1)S(1)}, u32[]{:S(2)}, u32[]{:S(2)}) collective-permute-start(bf16[8,192,256]{2,1,0:T(8,128)(2,1)S(1)} %constant_dynamic-update-slice_fusion.11.refs_0_), channel_id=1, source_target_pairs={{0,2},{2,0},{4,6},{6,4},{8,10},{10,8},{12,14},{14,12},{16,18},{18,... | collective-permute-start | bytes 2359304 | tf_op jit(solution)/shard_map/ppermute | solution.py:37
  53.0 35.9 %collective-permute-start.17 = (bf16[8,192,256]{2,1,0:T(8,128)(2,1)S(1)}, bf16[8,192,256]{2,1,0:T(8,128)(2,1)S(1)}, u32[]{:S(2)}, u32[]{:S(2)}) collective-permute-start(bf16[8,192,256]{2,1,0:T(8,128)(2,1)S(1)} %constant_dynamic-update-slice_fusion.13.refs_2_), channel_id=1, source_target_pairs={{0,4},{2,6},{4,0},{6,2},{8,12},{10,14},{12,8},{14,10},{16,20},{18,... | collective-permute-start | bytes 2359304 | tf_op jit(solution)/shard_map/ppermute | solution.py:37
  56.3 32.5 %collective-permute-start.18 = (bf16[8,128,256]{2,1,0:T(8,128)(2,1)S(1)}, bf16[8,128,256]{2,1,0:T(8,128)(2,1)S(1)}, u32[]{:S(2)}, u32[]{:S(2)}) collective-permute-start(bf16[8,128,256]{2,1,0:T(8,128)(2,1)S(1)} %constant_dynamic-update-slice_fusion.15.refs_4_), channel_id=1, source_target_pairs={{0,8},{2,10},{4,12},{6,14},{8,0},{10,2},{12,4},{14,6},{16,24},{18,... | collective-permute-start | bytes 1572872 | tf_op jit(solution)/shard_map/ppermute | solution.py:37
  105.3 26.1 %collective-permute-start.23 = (bf16[256,2048]{1,0:T(8,128)(2,1)S(1)}, bf16[256,2048]{1,0:T(8,128)(2,1)S(1)}, u32[]{:S(2)}, u32[]{:S(2)}) collective-permute-start(bf16[256,2048]{1,0:T(8,128)(2,1)S(1)} %convolution_convert_fusion.3), channel_id=1, source_target_pairs={{0,8},{2,10},{4,12},{6,14},{8,0},{10,2},{12,4},{14,6},{16,24},{18,... | collective-permute-start | bytes 3145736 | tf_op jit(solution)/shard_map/ppermute | solution.py:37
  105.6 27.8 %collective-permute-start.22 = (bf16[256,2048]{1,0:T(8,128)(2,1)S(1)}, bf16[256,2048]{1,0:T(8,128)(2,1)S(1)}, u32[]{:S(2)}, u32[]{:S(2)}) collective-permute-start(bf16[256,2048]{1,0:T(8,128)(2,1)S(1)} %convolution_convert_fusion.2), channel_id=1, source_target_pairs={{0,4},{2,6},{4,0},{6,2},{8,12},{10,14},{12,8},{14,10},{16,20},{18,... | collective-permute-start | bytes 3145736 | tf_op jit(solution)/shard_map/ppermute | solution.py:37
  107.1 28.2 %collective-permute-start.26 = (bf16[256,2048]{1,0:T(8,128)(2,1)S(1)}, bf16[256,2048]{1,0:T(8,128)(2,1)S(1)}, u32[]{:S(2)}, u32[]{:S(2)}) collective-permute-start(bf16[256,2048]{1,0:T(8,128)(2,1)S(1)} %convolution_convert_fusion.1), channel_id=1, source_target_pairs={{0,2},{2,0},{4,6},{6,4},{8,10},{10,8},{12,14},{14,12},{16,18},{18,... | collective-permute-start | bytes 3145736 | tf_op jit(solution)/shard_map/ppermute | solution.py:37
  110.0 43.8 %collective-permute-start.21 = (bf16[256,2048]{1,0:T(8,128)(2,1)S(1)}, bf16[256,2048]{1,0:T(8,128)(2,1)S(1)}, u32[]{:S(2)}, u32[]{:S(2)}) collective-permute-start(bf16[256,2048]{1,0:T(8,128)(2,1)S(1)} %convolution_convert_fusion), channel_id=1, source_target_pairs={{0,8},{2,10},{4,12},{6,14},{8,0},{10,2},{12,4},{14,6},{16,24},{18,... | collective-permute-start | bytes 3145736 | tf_op jit(solution)/shard_map/ppermute | solution.py:37
  131.8 14.9 %collective-permute-start.25 = (bf16[128,2048]{1,0:T(8,128)(2,1)S(1)}, bf16[128,2048]{1,0:T(8,128)(2,1)S(1)}, u32[]{:S(2)}, u32[]{:S(2)}) collective-permute-start(bf16[128,2048]{1,0:T(8,128)(2,1)S(1)} %slice.365), channel_id=1, source_target_pairs={{0,4},{2,6},{4,0},{6,2},{8,12},{10,14},{12,8},{14,10},{16,20},{18,... | collective-permute-start | bytes 1572872 | tf_op jit(solution)/shard_map/ppermute | solution.py:37
  133.8 14.7 %collective-permute-start.24 = (bf16[128,2048]{1,0:T(8,128)(2,1)S(1)}, bf16[128,2048]{1,0:T(8,128)(2,1)S(1)}, u32[]{:S(2)}, u32[]{:S(2)}) collective-permute-start(bf16[128,2048]{1,0:T(8,128)(2,1)S(1)} %slice.364), channel_id=1, source_target_pairs={{0,2},{2,0},{4,6},{6,4},{8,10},{10,8},{12,14},{14,12},{16,18},{18,... | collective-permute-start | bytes 1572872 | tf_op jit(solution)/shard_map/ppermute | solution.py:37
  137.0 23.7 %collective-permute-start.28 = (bf16[128,2048]{1,0:T(8,128)(2,1)S(1)}, bf16[128,2048]{1,0:T(8,128)(2,1)S(1)}, u32[]{:S(2)}, u32[]{:S(2)}) collective-permute-start(bf16[128,2048]{1,0:T(8,128)(2,1)S(1)} %slice.363), channel_id=1, source_target_pairs={{0,4},{2,6},{4,0},{6,2},{8,12},{10,14},{12,8},{14,10},{16,20},{18,... | collective-permute-start | bytes 1572872 | tf_op jit(solution)/shard_map/ppermute | solution.py:37
  147.1 9.8 %collective-permute-start.29 = (bf16[64,2048]{1,0:T(8,128)(2,1)S(1)}, bf16[64,2048]{1,0:T(8,128)(2,1)S(1)}, u32[]{:S(2)}, u32[]{:S(2)}) collective-permute-start(bf16[64,2048]{1,0:T(8,128)(2,1)S(1)} %slice.369), channel_id=1, source_target_pairs={{0,2},{2,0},{4,6},{6,4},{8,10},{10,8},{12,14},{14,12},{16,18},{18,... | collective-permute-start | bytes 786440 | tf_op jit(solution)/shard_map/ppermute | solution.py:37
  148.8 12.4 %collective-permute-start.32 = (bf16[64,2048]{1,0:T(8,128)(2,1)S(1)}, bf16[64,2048]{1,0:T(8,128)(2,1)S(1)}, u32[]{:S(2)}, u32[]{:S(2)}) collective-permute-start(bf16[64,2048]{1,0:T(8,128)(2,1)S(1)} %slice.368), channel_id=1, source_target_pairs={{0,8},{2,10},{4,12},{6,14},{8,0},{10,2},{12,4},{14,6},{16,24},{18,... | collective-permute-start | bytes 786440 | tf_op jit(solution)/shard_map/ppermute | solution.py:37
  155.5 17.4 %collective-permute-start.27 = (bf16[128,2048]{1,0:T(8,128)(2,1)S(1)}, bf16[128,2048]{1,0:T(8,128)(2,1)S(1)}, u32[]{:S(2)}, u32[]{:S(2)}) collective-permute-start(bf16[128,2048]{1,0:T(8,128)(2,1)S(1)} %slice.362), channel_id=1, source_target_pairs={{0,2},{2,0},{4,6},{6,4},{8,10},{10,8},{12,14},{14,12},{16,18},{18,... | collective-permute-start | bytes 1572872 | tf_op jit(solution)/shard_map/ppermute | solution.py:37
  157.0 10.0 %collective-permute-start.31 = (bf16[32,2048]{1,0:T(8,128)(2,1)S(1)}, bf16[32,2048]{1,0:T(8,128)(2,1)S(1)}, u32[]{:S(2)}, u32[]{:S(2)}) collective-permute-start(bf16[32,2048]{1,0:T(8,128)(2,1)S(1)} %slice.373), channel_id=1, source_target_pairs={{0,16},{2,18},{4,20},{6,22},{8,24},{10,26},{12,28},{14,30},{16,0},... | collective-permute-start | bytes 393224 | tf_op jit(solution)/shard_map/ppermute | solution.py:37
  160.8 12.0 %collective-permute-start.30 = (bf16[64,2048]{1,0:T(8,128)(2,1)S(1)}, bf16[64,2048]{1,0:T(8,128)(2,1)S(1)}, u32[]{:S(2)}, u32[]{:S(2)}) collective-permute-start(bf16[64,2048]{1,0:T(8,128)(2,1)S(1)} %slice.367), channel_id=1, source_target_pairs={{0,8},{2,10},{4,12},{6,14},{8,0},{10,2},{12,4},{14,6},{16,24},{18,... | collective-permute-start | bytes 786440 | tf_op jit(solution)/shard_map/ppermute | solution.py:37
  161.3 13.9 %collective-permute-start.34 = (bf16[32,2048]{1,0:T(8,128)(2,1)S(1)}, bf16[32,2048]{1,0:T(8,128)(2,1)S(1)}, u32[]{:S(2)}, u32[]{:S(2)}) collective-permute-start(bf16[32,2048]{1,0:T(8,128)(2,1)S(1)} %slice.372), channel_id=1, source_target_pairs={{0,16},{2,18},{4,20},{6,22},{8,24},{10,26},{12,28},{14,30},{16,0},... | collective-permute-start | bytes 393224 | tf_op jit(solution)/shard_map/ppermute | solution.py:37
  167.2 18.1 %collective-permute-start.37 = (bf16[32,2048]{1,0:T(8,128)(2,1)S(1)}, bf16[32,2048]{1,0:T(8,128)(2,1)S(1)}, u32[]{:S(2)}, u32[]{:S(2)}) collective-permute-start(bf16[32,2048]{1,0:T(8,128)(2,1)S(1)} %get-tuple-element.199), channel_id=1, source_target_pairs={{0,16},{2,18},{4,20},{6,22},{8,24},{10,26},{12,28},{14,30},{16,0},... | collective-permute-start | bytes 393224 | tf_op jit(solution)/shard_map/ppermute | solution.py:37
  173.2 17.7 %collective-permute-start.39 = (bf16[32,2048]{1,0:T(8,128)(2,1)S(1)}, bf16[32,2048]{1,0:T(8,128)(2,1)S(1)}, u32[]{:S(2)}, u32[]{:S(2)}) collective-permute-start(bf16[32,2048]{1,0:T(8,128)(2,1)S(1)} %slice.371), channel_id=1, source_target_pairs={{0,16},{2,18},{4,20},{6,22},{8,24},{10,26},{12,28},{14,30},{16,0},... | collective-permute-start | bytes 393224 | tf_op jit(solution)/shard_map/ppermute | solution.py:37
  173.7 6.4 %collective-permute-start.33 = (bf16[64,2048]{1,0:T(8,128)(2,1)S(1)}, bf16[64,2048]{1,0:T(8,128)(2,1)S(1)}, u32[]{:S(2)}, u32[]{:S(2)}) collective-permute-start(bf16[64,2048]{1,0:T(8,128)(2,1)S(1)} %slice.366), channel_id=1, source_target_pairs={{0,4},{2,6},{4,0},{6,2},{8,12},{10,14},{12,8},{14,10},{16,20},{18,... | collective-permute-start | bytes 786440 | tf_op jit(solution)/shard_map/ppermute | solution.py:37
  175.4 18.3 %collective-permute-start.36 = (bf16[32,2048]{1,0:T(8,128)(2,1)S(1)}, bf16[32,2048]{1,0:T(8,128)(2,1)S(1)}, u32[]{:S(2)}, u32[]{:S(2)}) collective-permute-start(bf16[32,2048]{1,0:T(8,128)(2,1)S(1)} %get-tuple-element.205), channel_id=1, source_target_pairs={{0,16},{2,18},{4,20},{6,22},{8,24},{10,26},{12,28},{14,30},{16,0},... | collective-permute-start | bytes 393224 | tf_op jit(solution)/shard_map/ppermute | solution.py:37
  180.2 17.8 %collective-permute-start.35 = (bf16[32,2048]{1,0:T(8,128)(2,1)S(1)}, bf16[32,2048]{1,0:T(8,128)(2,1)S(1)}, u32[]{:S(2)}, u32[]{:S(2)}) collective-permute-start(bf16[32,2048]{1,0:T(8,128)(2,1)S(1)} %slice.370), channel_id=1, source_target_pairs={{0,16},{2,18},{4,20},{6,22},{8,24},{10,26},{12,28},{14,30},{16,0},... | collective-permute-start | bytes 393224 | tf_op jit(solution)/shard_map/ppermute | solution.py:37
  185.3 6.4 %collective-permute-start.38 = (bf16[64,2048]{1,0:T(8,128)(2,1)S(1)}, bf16[64,2048]{1,0:T(8,128)(2,1)S(1)}, u32[]{:S(2)}, u32[]{:S(2)}) collective-permute-start(bf16[64,2048]{1,0:T(8,128)(2,1)S(1)} %constant_dynamic-update-slice_fusion.17), channel_id=1, source_target_pairs={{0,2},{2,0},{4,6},{6,4},{8,10},{10,8},{12,14},{14,12},{16,18},{18,... | collective-permute-start | bytes 786440 | tf_op jit(solution)/shard_map/ppermute | solution.py:37
  191.1 11.1 %collective-permute-start.43 = (bf16[32,2048]{1,0:T(8,128)(2,1)S(1)}, bf16[32,2048]{1,0:T(8,128)(2,1)S(1)}, u32[]{:S(2)}, u32[]{:S(2)}) collective-permute-start(bf16[32,2048]{1,0:T(8,128)(2,1)S(1)} %get-tuple-element.209), channel_id=1, source_target_pairs={{0,16},{2,18},{4,20},{6,22},{8,24},{10,26},{12,28},{14,30},{16,0},... | collective-permute-start | bytes 393224 | tf_op jit(solution)/shard_map/ppermute | solution.py:37
  191.8 10.5 %collective-permute-start.42 = (bf16[128,2048]{1,0:T(8,128)(2,1)S(1)}, bf16[128,2048]{1,0:T(8,128)(2,1)S(1)}, u32[]{:S(2)}, u32[]{:S(2)}) collective-permute-start(bf16[128,2048]{1,0:T(8,128)(2,1)S(1)} %constant_dynamic-update-slice_fusion.19), channel_id=1, source_target_pairs={{0,4},{2,6},{4,0},{6,2},{8,12},{10,14},{12,8},{14,10},{16,20},{18,... | collective-permute-start | bytes 1572872 | tf_op jit(solution)/shard_map/ppermute | solution.py:37
  193.7 14.1 %collective-permute-start.41 = (bf16[64,2048]{1,0:T(8,128)(2,1)S(1)}, bf16[64,2048]{1,0:T(8,128)(2,1)S(1)}, u32[]{:S(2)}, u32[]{:S(2)}) collective-permute-start(bf16[64,2048]{1,0:T(8,128)(2,1)S(1)} %constant_dynamic-update-slice_fusion.21), channel_id=1, source_target_pairs={{0,8},{2,10},{4,12},{6,14},{8,0},{10,2},{12,4},{14,6},{16,24},{18,... | collective-permute-start | bytes 786440 | tf_op jit(solution)/shard_map/ppermute | solution.py:37
  198.2 11.4 %collective-permute-start.40 = (bf16[32,2048]{1,0:T(8,128)(2,1)S(1)}, bf16[32,2048]{1,0:T(8,128)(2,1)S(1)}, u32[]{:S(2)}, u32[]{:S(2)}) collective-permute-start(bf16[32,2048]{1,0:T(8,128)(2,1)S(1)} %get-tuple-element.215), channel_id=1, source_target_pairs={{0,16},{2,18},{4,20},{6,22},{8,24},{10,26},{12,28},{14,30},{16,0},... | collective-permute-start | bytes 393224 | tf_op jit(solution)/shard_map/ppermute | solution.py:37
  202.2 11.3 %collective-permute-start.45 = (bf16[64,2048]{1,0:T(8,128)(2,1)S(1)}, bf16[64,2048]{1,0:T(8,128)(2,1)S(1)}, u32[]{:S(2)}, u32[]{:S(2)}) collective-permute-start(bf16[64,2048]{1,0:T(8,128)(2,1)S(1)} %constant_dynamic-update-slice_fusion.23), channel_id=1, source_target_pairs={{0,8},{2,10},{4,12},{6,14},{8,0},{10,2},{12,4},{14,6},{16,24},{18,... | collective-permute-start | bytes 786440 | tf_op jit(solution)/shard_map/ppermute | solution.py:37
  202.4 33.6 %collective-permute-start.52 = (bf16[256,2048]{1,0:T(8,128)(2,1)S(1)}, bf16[256,2048]{1,0:T(8,128)(2,1)S(1)}, u32[]{:S(2)}, u32[]{:S(2)}) collective-permute-start(bf16[256,2048]{1,0:T(8,128)(2,1)S(1)} %constant_dynamic-update-slice_fusion.25.refs_1_), channel_id=1, source_target_pairs={{0,8},{2,10},{4,12},{6,14},{8,0},{10,2},{12,4},{14,6},{16,24},{18,... | collective-permute-start | bytes 3145736 | tf_op jit(solution)/shard_map/ppermute | solution.py:37
  207.9 14.9 %collective-permute-start.48 = (bf16[128,2048]{1,0:T(8,128)(2,1)S(1)}, bf16[128,2048]{1,0:T(8,128)(2,1)S(1)}, u32[]{:S(2)}, u32[]{:S(2)}) collective-permute-start(bf16[128,2048]{1,0:T(8,128)(2,1)S(1)} %constant_dynamic-update-slice_fusion.27), channel_id=1, source_target_pairs={{0,2},{2,0},{4,6},{6,4},{8,10},{10,8},{12,14},{14,12},{16,18},{18,... | collective-permute-start | bytes 1572872 | tf_op jit(solution)/shard_map/ppermute | solution.py:37
  209.6 9.0 %collective-permute-start.44 = (bf16[64,2048]{1,0:T(8,128)(2,1)S(1)}, bf16[64,2048]{1,0:T(8,128)(2,1)S(1)}, u32[]{:S(2)}, u32[]{:S(2)}) collective-permute-start(bf16[64,2048]{1,0:T(8,128)(2,1)S(1)} %constant_dynamic-update-slice_fusion.29), channel_id=1, source_target_pairs={{0,4},{2,6},{4,0},{6,2},{8,12},{10,14},{12,8},{14,10},{16,20},{18,... | collective-permute-start | bytes 786440 | tf_op jit(solution)/shard_map/ppermute | solution.py:37
  213.5 16.3 %collective-permute-start.47 = (bf16[128,2048]{1,0:T(8,128)(2,1)S(1)}, bf16[128,2048]{1,0:T(8,128)(2,1)S(1)}, u32[]{:S(2)}, u32[]{:S(2)}) collective-permute-start(bf16[128,2048]{1,0:T(8,128)(2,1)S(1)} %constant_dynamic-update-slice_fusion.31), channel_id=1, source_target_pairs={{0,4},{2,6},{4,0},{6,2},{8,12},{10,14},{12,8},{14,10},{16,20},{18,... | collective-permute-start | bytes 1572872 | tf_op jit(solution)/shard_map/ppermute | solution.py:37
  218.7 14.4 %collective-permute-start.46 = (bf16[128,2048]{1,0:T(8,128)(2,1)S(1)}, bf16[128,2048]{1,0:T(8,128)(2,1)S(1)}, u32[]{:S(2)}, u32[]{:S(2)}) collective-permute-start(bf16[128,2048]{1,0:T(8,128)(2,1)S(1)} %constant_dynamic-update-slice_fusion.33), channel_id=1, source_target_pairs={{0,2},{2,0},{4,6},{6,4},{8,10},{10,8},{12,14},{14,12},{16,18},{18,... | collective-permute-start | bytes 1572872 | tf_op jit(solution)/shard_map/ppermute | solution.py:37
  222.9 26.8 %collective-permute-start.51 = (bf16[256,2048]{1,0:T(8,128)(2,1)S(1)}, bf16[256,2048]{1,0:T(8,128)(2,1)S(1)}, u32[]{:S(2)}, u32[]{:S(2)}) collective-permute-start(bf16[256,2048]{1,0:T(8,128)(2,1)S(1)} %constant_dynamic-update-slice_fusion.35.refs_1_), channel_id=1, source_target_pairs={{0,4},{2,6},{4,0},{6,2},{8,12},{10,14},{12,8},{14,10},{16,20},{18,... | collective-permute-start | bytes 3145736 | tf_op jit(solution)/shard_map/ppermute | solution.py:37
  229.9 22.9 %collective-permute-start.50 = (bf16[256,2048]{1,0:T(8,128)(2,1)S(1)}, bf16[256,2048]{1,0:T(8,128)(2,1)S(1)}, u32[]{:S(2)}, u32[]{:S(2)}) collective-permute-start(bf16[256,2048]{1,0:T(8,128)(2,1)S(1)} %constant_dynamic-update-slice_fusion.37.refs_1_), channel_id=1, source_target_pairs={{0,2},{2,0},{4,6},{6,4},{8,10},{10,8},{12,14},{14,12},{16,18},{18,... | collective-permute-start | bytes 3145736 | tf_op jit(solution)/shard_map/ppermute | solution.py:37
  233.1 25.5 %collective-permute-start.49 = (bf16[256,2048]{1,0:T(8,128)(2,1)S(1)}, bf16[256,2048]{1,0:T(8,128)(2,1)S(1)}, u32[]{:S(2)}, u32[]{:S(2)}) collective-permute-start(bf16[256,2048]{1,0:T(8,128)(2,1)S(1)} %constant_dynamic-update-slice_fusion.39.refs_1_), channel_id=1, source_target_pairs={{0,8},{2,10},{4,12},{6,14},{8,0},{10,2},{12,4},{14,6},{16,24},{18,... | collective-permute-start | bytes 3145736 | tf_op jit(solution)/shard_map/ppermute | solution.py:37
  (28 other events, 181.7 us)

commit v6 on v5

--- a/solution.py
+++ b/solution.py
@@ -258,10 +258,10 @@
     packed = jnp.where(
         core == 0, jnp.concatenate([whole, other]), jnp.concatenate([other, whole])
     )
-    work, done = head_of_factor(packed, blocks, size, 1)
+    work, done = head_of_factor(packed, blocks, size, 2)
     token = widen(bits - 1, work)
     work, done = after(token, (work, done))
-    inverse = rest_of_factor(work, done, 1)
+    inverse = rest_of_factor(work, done, 2)
     orders = [order for _, order in groups]
     return inverse, orders, [part[1] for part in parts], [part[2] for part in parts]
 

time: 264 us -> 249 us (0.943)
  Pallas kernels: 56.4 us -> 44.6 us
  waiting for transfers between devices: 105 us -> 102 us
    pallas_call x1, Pallas kernels: 30.5 us -> 11.3 us  [rest_of_factor(): pl.pallas_call(functools.partial(factor_rest, steps), out_shape=jax.Shape...]
    pallas_call x1, Pallas kernels: 6.66 us -> 13.8 us  [head_of_factor(): pl.pallas_call(functools.partial(factor_head, blocks, steps), out_shape=(...]
    ppermute x41, waiting for transfers between devices: 99.9 us -> 97.2 us  [flip(): return lax.ppermute(value, 'dp', flip_pairs(devices, bit))]
  transfers between devices with their start and end apart: 53 -> 53, of which waited for: 31 -> 28; matrix products, arithmetic and copies ran while one was open for 6% -> 7% of each run, Pallas kernels for 18% -> 14%
where the time goes in v6:
time: 249 us
  waiting for transfers between devices  102 us (41%)
  starting transfers between devices  71.2 us (29%)
  Pallas kernels  44.6 us (18%)
  matrix products  17.2 us (7%)
  local copies, waits for them, and re-layouts  6.1 us (2%)
  other arithmetic  5.89 us (2%)
    ppermute x41, waiting for transfers between devices, flip(): return lax.ppermute(value, 'dp', flip_pairs(devices, bit))  97.2 us
    ppermute x41, starting transfers between devices, flip(): return lax.ppermute(value, 'dp', flip_pairs(devices, bit))  57.3 us
    pallas_call x1, Pallas kernels, head_of_factor(): pl.pallas_call(functools.partial(factor_head, blocks, steps), out_shape=(...  13.8 us
    ppermute x9, starting transfers between devices, send(): return lax.ppermute(value, 'dp', shift_pairs(dims, shift))  13.8 us
    pallas_call x4, Pallas kernels, update_columns(): pl.pallas_call(functools.partial(update_kernel, scale, len(pieces)), grid...  11.7 us
    pallas_call x1, Pallas kernels, rest_of_factor(): pl.pallas_call(functools.partial(factor_rest, steps), out_shape=jax.Shape...  11.3 us
    pallas_call x1, Pallas kernels, mix(): pl.pallas_call(functools.partial(mix_kernel, count, limit), grid_spec=plt...  7.81 us
    dot_general x4, matrix products, local(): jnp.dot(left[size:], grads[:, columns], preferred_element_type=F32)  6.28 us
  transfers between devices with their start and end apart: 53, of which 28 were waited for; matrix products, arithmetic and copies ran while one was open for 7% of the time, Pallas kernels for 14%

profile of v6, /device:TPU:0, one launch (start us, length us, event | category | flops | bytes accessed | tf_op | source)
XLA Modules:
  0.0 249.0 jit_solution(11431849460779070175)
XLA Ops:
  1.9 1.9 fusion.40
  4.0 3.0 %collective-permute-start = (f32[160,128]{1,0:T(8,128)S(1)}, f32[160,128]{1,0:T(8,128)S(1)}, u32[]{:S(2)}, u32[]{:S(2)}) collective-permute-start(f32[160,128]{1,0:T(8,128)S(1)} %get-tuple-element.263), channel_id=1, source_target_pairs={{0,2},{2,0},{4,6},{6,4},{8,10},{10,8},{12,14},{14,12},{16,18},{18,... | collective-permute-start | bytes 245768 | tf_op jit(solution)/shard_map/ppermute | solution.py:64
  8.5 3.1 %collective-permute-start.6 = (bf16[1,512,256]{2,1,0:T(8,128)(2,1)S(1)}, bf16[1,512,256]{2,1,0:T(8,128)(2,1)S(1)}, u32[]{:S(2)}, u32[]{:S(2)}) collective-permute-start(bf16[1,512,256]{2,1,0:T(8,128)(2,1)S(1)} %bitcast.57), channel_id=1, source_target_pairs={{0,16},{2,18},{4,20},{6,22},{8,24},{10,26},{12,28},{14,30},{16,0},... | collective-permute-start | bytes 786440 | tf_op jit(solution)/shard_map/ppermute | solution.py:37
  13.8 1.6 collective-permute-start.3
  15.5 2.7 %collective-permute-start.4 = (f32[160,128]{1,0:T(8,128)S(1)}, f32[160,128]{1,0:T(8,128)S(1)}, u32[]{:S(2)}, u32[]{:S(2)}) collective-permute-start(f32[160,128]{1,0:T(8,128)S(1)} %add_add_fusion), channel_id=1, source_target_pairs={{0,16},{2,18},{4,20},{6,22},{8,24},{10,26},{12,28},{14,30},{16,0},... | collective-permute-start | bytes 245768 | tf_op jit(solution)/shard_map/ppermute | solution.py:64
  21.1 6.5 %collective-permute-done.6 = bf16[1,512,256]{2,1,0:T(8,128)(2,1)S(1)} collective-permute-done((bf16[1,512,256]{2,1,0:T(8,128)(2,1)S(1)}, bf16[1,512,256]{2,1,0:T(8,128)(2,1)S(1)}, u32[]{:S(2)}, u32[]{:S(2)}) %collective-permute-start.6) | collective-permute-done | bytes 262176 | tf_op jit(solution)/shard_map/ppermute | solution.py:37
  33.6 2.2 collective-permute-start.12
  35.8 2.4 collective-permute-done.10
  40.3 2.1 collective-permute-start.14
  43.0 13.8 %factor_head.1 = (f32[512,512]{1,0:T(8,128)S(1)}, f32[512,512]{1,0:T(8,128)S(1)}) custom-call(f32[1280,128]{1,0:T(8,128)S(1)} %maximum_select_fusion.2.packed_ref), custom_call_target="tpu_custom_call" | custom-call | tf_op jit(solution)/shard_map/factor_head/pallas_call | solution.py:169
  57.1 1.6 collective-permute-start.17
  58.7 1.8 collective-permute-start.18
  60.7 11.3 %factor_rest.1 = f32[512,512]{1,0:T(8,128)S(1)} custom-call(f32[512,512]{1,0:T(8,128)S(1)} %get-tuple-element.145.start_ref, f32[512,512]{1,0:T(8,128)S(1)} %get-tuple-element.146.done_ref), custom_call_target="tpu_custom_call" | custom-call | tf_op jit(solution)/shard_map/factor_rest/pallas_call | solution.py:180
  72.0 3.8 %collective-permute-done.17.refs_3_ = bf16[8,192,256]{2,1,0:T(8,128)(2,1)S(1)} collective-permute-done((bf16[8,192,256]{2,1,0:T(8,128)(2,1)S(1)}, bf16[8,192,256]{2,1,0:T(8,128)(2,1)S(1)}, u32[]{:S(2)}, u32[]{:S(2)}) %collective-permute-start.17) | collective-permute-done | bytes 786464 | tf_op jit(solution)/shard_map/ppermute | solution.py:37
  75.8 7.8 %mix.1 = f32[512,256]{1,0:T(8,128)S(1)} custom-call(s32[2,3,8]{2,1,0:T(4,128)S(1)} %pad_add_fusion.table_ref, bf16[512,4096]{1,0:T(8,128)(2,1)S(1)} %copy-done.2, bf16[512,4096]{1,0:T(8,128)(2,1)} %collective-permute-done.19.right_ref, bf16[8,192,256]{2,1,0:T(8,128)(2,1)S(1)} %constant_dynamic-update-slice_fusion.11.refs_0_, ...), custom_call_target="tpu_custom_call" | custom-call | tf_op jit(solution)/shard_map/mix/pallas_call | solution.py:322
  86.7 2.5 convolution_convert_fusion.3
  89.2 2.3 convolution_convert_fusion.2
  92.4 1.8 collective-permute-start.23
  98.4 1.9 convolution_convert_fusion.8
  105.7 12.8 %collective-permute-done.23 = bf16[256,2048]{1,0:T(8,128)(2,1)S(1)} collective-permute-done((bf16[256,2048]{1,0:T(8,128)(2,1)S(1)}, bf16[256,2048]{1,0:T(8,128)(2,1)S(1)}, u32[]{:S(2)}, u32[]{:S(2)}) %collective-permute-start.23) | collective-permute-done | bytes 1048608 | tf_op jit(solution)/shard_map/ppermute | solution.py:37
  124.7 9.2 %collective-permute-done.25 = bf16[128,2048]{1,0:T(8,128)(2,1)S(1)} collective-permute-done((bf16[128,2048]{1,0:T(8,128)(2,1)S(1)}, bf16[128,2048]{1,0:T(8,128)(2,1)S(1)}, u32[]{:S(2)}, u32[]{:S(2)}) %collective-permute-start.25) | collective-permute-done | bytes 524320 | tf_op jit(solution)/shard_map/ppermute | solution.py:37
  136.0 1.8 collective-permute-start.32
  137.8 3.1 %collective-permute-done.21 = bf16[256,2048]{1,0:T(8,128)(2,1)S(1)} collective-permute-done((bf16[256,2048]{1,0:T(8,128)(2,1)S(1)}, bf16[256,2048]{1,0:T(8,128)(2,1)S(1)}, u32[]{:S(2)}, u32[]{:S(2)}) %collective-permute-start.21) | collective-permute-done | bytes 1048608 | tf_op jit(solution)/shard_map/ppermute | solution.py:37
  144.2 3.7 %collective-permute-start.31 = (bf16[32,2048]{1,0:T(8,128)(2,1)S(1)}, bf16[32,2048]{1,0:T(8,128)(2,1)S(1)}, u32[]{:S(2)}, u32[]{:S(2)}) collective-permute-start(bf16[32,2048]{1,0:T(8,128)(2,1)S(1)} %slice.373), channel_id=1, source_target_pairs={{0,16},{2,18},{4,20},{6,22},{8,24},{10,26},{12,28},{14,30},{16,0},... | collective-permute-start | bytes 393224 | tf_op jit(solution)/shard_map/ppermute | solution.py:37
  150.4 3.9 %collective-permute-done.31 = bf16[32,2048]{1,0:T(8,128)(2,1)S(1)} collective-permute-done((bf16[32,2048]{1,0:T(8,128)(2,1)S(1)}, bf16[32,2048]{1,0:T(8,128)(2,1)S(1)}, u32[]{:S(2)}, u32[]{:S(2)}) %collective-permute-start.31) | collective-permute-done | bytes 131104 | tf_op jit(solution)/shard_map/ppermute | solution.py:37
  155.6 4.6 %collective-permute-done.30 = bf16[64,2048]{1,0:T(8,128)(2,1)S(1)} collective-permute-done((bf16[64,2048]{1,0:T(8,128)(2,1)S(1)}, bf16[64,2048]{1,0:T(8,128)(2,1)S(1)}, u32[]{:S(2)}, u32[]{:S(2)}) %collective-permute-start.30) | collective-permute-done | bytes 262176 | tf_op jit(solution)/shard_map/ppermute | solution.py:37
  162.8 2.5 %collective-permute-start.36 = (bf16[32,2048]{1,0:T(8,128)(2,1)S(1)}, bf16[32,2048]{1,0:T(8,128)(2,1)S(1)}, u32[]{:S(2)}, u32[]{:S(2)}) collective-permute-start(bf16[32,2048]{1,0:T(8,128)(2,1)S(1)} %get-tuple-element.205), channel_id=1, source_target_pairs={{0,16},{2,18},{4,20},{6,22},{8,24},{10,26},{12,28},{14,30},{16,0},... | collective-permute-start | bytes 393224 | tf_op jit(solution)/shard_map/ppermute | solution.py:37
  165.3 2.1 collective-permute-done.33
  167.5 2.5 %collective-permute-start.35 = (bf16[32,2048]{1,0:T(8,128)(2,1)S(1)}, bf16[32,2048]{1,0:T(8,128)(2,1)S(1)}, u32[]{:S(2)}, u32[]{:S(2)}) collective-permute-start(bf16[32,2048]{1,0:T(8,128)(2,1)S(1)} %slice.370), channel_id=1, source_target_pairs={{0,16},{2,18},{4,20},{6,22},{8,24},{10,26},{12,28},{14,30},{16,0},... | collective-permute-start | bytes 393224 | tf_op jit(solution)/shard_map/ppermute | solution.py:37
  171.4 6.9 %collective-permute-done.39 = bf16[32,2048]{1,0:T(8,128)(2,1)S(1)} collective-permute-done((bf16[32,2048]{1,0:T(8,128)(2,1)S(1)}, bf16[32,2048]{1,0:T(8,128)(2,1)S(1)}, u32[]{:S(2)}, u32[]{:S(2)}) %collective-permute-start.39) | collective-permute-done | bytes 131104 | tf_op jit(solution)/shard_map/ppermute | solution.py:37
  178.6 2.1 collective-permute-start.42
  181.1 2.0 collective-permute-start.41
  183.1 2.2 collective-permute-done.35
  185.5 4.0 %collective-permute-done.43 = bf16[32,2048]{1,0:T(8,128)(2,1)S(1)} collective-permute-done((bf16[32,2048]{1,0:T(8,128)(2,1)S(1)}, bf16[32,2048]{1,0:T(8,128)(2,1)S(1)}, u32[]{:S(2)}, u32[]{:S(2)}) %collective-permute-start.43) | collective-permute-done | bytes 131104 | tf_op jit(solution)/shard_map/ppermute | solution.py:37
  189.7 2.1 collective-permute-start.52
  191.8 3.3 %collective-permute-done.41 = bf16[64,2048]{1,0:T(8,128)(2,1)S(1)} collective-permute-done((bf16[64,2048]{1,0:T(8,128)(2,1)S(1)}, bf16[64,2048]{1,0:T(8,128)(2,1)S(1)}, u32[]{:S(2)}, u32[]{:S(2)}) %collective-permute-start.41) | collective-permute-done | bytes 262176 | tf_op jit(solution)/shard_map/ppermute | solution.py:37
  196.2 2.4 collective-permute-start.44
  198.5 2.2 collective-permute-done.45
  202.3 2.7 %collective-permute-done.44 = bf16[64,2048]{1,0:T(8,128)(2,1)S(1)} collective-permute-done((bf16[64,2048]{1,0:T(8,128)(2,1)S(1)}, bf16[64,2048]{1,0:T(8,128)(2,1)S(1)}, u32[]{:S(2)}, u32[]{:S(2)}) %collective-permute-start.44) | collective-permute-done | bytes 262176 | tf_op jit(solution)/shard_map/ppermute | solution.py:37
  205.5 4.5 %collective-permute-done.48 = bf16[128,2048]{1,0:T(8,128)(2,1)S(1)} collective-permute-done((bf16[128,2048]{1,0:T(8,128)(2,1)S(1)}, bf16[128,2048]{1,0:T(8,128)(2,1)S(1)}, u32[]{:S(2)}, u32[]{:S(2)}) %collective-permute-start.48) | collective-permute-done | bytes 524320 | tf_op jit(solution)/shard_map/ppermute | solution.py:37
  211.7 4.6 %collective-permute-done.47 = bf16[128,2048]{1,0:T(8,128)(2,1)S(1)} collective-permute-done((bf16[128,2048]{1,0:T(8,128)(2,1)S(1)}, bf16[128,2048]{1,0:T(8,128)(2,1)S(1)}, u32[]{:S(2)}, u32[]{:S(2)}) %collective-permute-start.47) | collective-permute-done | bytes 524320 | tf_op jit(solution)/shard_map/ppermute | solution.py:37
  217.0 3.4 %collective-permute-done.46 = bf16[128,2048]{1,0:T(8,128)(2,1)S(1)} collective-permute-done((bf16[128,2048]{1,0:T(8,128)(2,1)S(1)}, bf16[128,2048]{1,0:T(8,128)(2,1)S(1)}, u32[]{:S(2)}, u32[]{:S(2)}) %collective-permute-start.46) | collective-permute-done | bytes 524320 | tf_op jit(solution)/shard_map/ppermute | solution.py:37
  223.2 2.9 %update_columns.4.refs_3_ = f32[512,8192]{1,0:T(8,128)} custom-call(bf16[512,512]{1,0:T(8,128)(2,1)S(1)} %convolution_convert_fusion.6.refs_0_, bf16[256,2048]{1,0:T(8,128)(2,1)S(1)} %constant_dynamic-update-slice_fusion.25.refs_1_, bf16[256,2048]{1,0:T(8,128)(2,1)S(1)} %collective-permute-done.52.refs_2_), custom_call_target="tpu_custom_call" | custom-call | tf_op jit(solution)/shard_map/update_columns/pallas_call | solution.py:363
  226.1 10.5 %collective-permute-done.51.refs_2_ = bf16[256,2048]{1,0:T(8,128)(2,1)S(1)} collective-permute-done((bf16[256,2048]{1,0:T(8,128)(2,1)S(1)}, bf16[256,2048]{1,0:T(8,128)(2,1)S(1)}, u32[]{:S(2)}, u32[]{:S(2)}) %collective-permute-start.51) | collective-permute-done | bytes 1048608 | tf_op jit(solution)/shard_map/ppermute | solution.py:37
  236.6 3.6 %collective-permute-done.50.refs_2_ = bf16[256,2048]{1,0:T(8,128)(2,1)S(1)} collective-permute-done((bf16[256,2048]{1,0:T(8,128)(2,1)S(1)}, bf16[256,2048]{1,0:T(8,128)(2,1)S(1)}, u32[]{:S(2)}, u32[]{:S(2)}) %collective-permute-start.50) | collective-permute-done | bytes 1048608 | tf_op jit(solution)/shard_map/ppermute | solution.py:37
  240.2 2.9 %update_columns.5.refs_3_ = f32[512,8192]{1,0:T(8,128)} custom-call(bf16[512,512]{1,0:T(8,128)(2,1)S(1)} %convolution_convert_fusion.5.refs_0_, bf16[256,2048]{1,0:T(8,128)(2,1)S(1)} %constant_dynamic-update-slice_fusion.35.refs_1_, bf16[256,2048]{1,0:T(8,128)(2,1)S(1)} %collective-permute-done.51.refs_2_, ...), custom_call_target="tpu_custom_call", output_to_operand_aliasing={{}: (3, {})} | custom-call | tf_op jit(solution)/shard_map/update_columns/pallas_call | solution.py:363
  243.1 2.9 %update_columns.6.refs_3_ = f32[512,8192]{1,0:T(8,128)} custom-call(bf16[512,512]{1,0:T(8,128)(2,1)S(1)} %convolution_convert_fusion.4.refs_0_, bf16[256,2048]{1,0:T(8,128)(2,1)S(1)} %constant_dynamic-update-slice_fusion.37.refs_1_, bf16[256,2048]{1,0:T(8,128)(2,1)S(1)} %collective-permute-done.50.refs_2_, ...), custom_call_target="tpu_custom_call", output_to_operand_aliasing={{}: (3, {})} | custom-call | tf_op jit(solution)/shard_map/update_columns/pallas_call | solution.py:363
  246.1 2.9 %update_columns.7 = f32[512,8192]{1,0:T(8,128)} custom-call(bf16[512,512]{1,0:T(8,128)(2,1)S(1)} %convolution_convert_fusion.7.refs_0_, bf16[256,2048]{1,0:T(8,128)(2,1)S(1)} %constant_dynamic-update-slice_fusion.39.refs_1_, bf16[256,2048]{1,0:T(8,128)(2,1)S(1)} %collective-permute-done.49.refs_2_, ...), custom_call_target="tpu_custom_call", output_to_operand_aliasing={{}: (3, {})} | custom-call | tf_op jit(solution)/shard_map/update_columns/pallas_call | solution.py:363
  (246 shorter events, 58.8 us)
Async XLA Ops:
  4.0 8.1 %collective-permute-start = (f32[160,128]{1,0:T(8,128)S(1)}, f32[160,128]{1,0:T(8,128)S(1)}, u32[]{:S(2)}, u32[]{:S(2)}) collective-permute-start(f32[160,128]{1,0:T(8,128)S(1)} %get-tuple-element.263), channel_id=1, source_target_pairs={{0,2},{2,0},{4,6},{6,4},{8,10},{10,8},{12,14},{14,12},{16,18},{18,... | collective-permute-start | bytes 245768 | tf_op jit(solution)/shard_map/ppermute | solution.py:64
  8.5 5.3 %collective-permute-start.2 = (f32[160,128]{1,0:T(8,128)S(1)}, f32[160,128]{1,0:T(8,128)S(1)}, u32[]{:S(2)}, u32[]{:S(2)}) collective-permute-start(f32[160,128]{1,0:T(8,128)S(1)} %get-tuple-element.261), channel_id=1, source_target_pairs={{0,6},{2,4},{4,2},{6,0},{8,14},{10,12},{12,10},{14,8},{16,22},{18,... | collective-permute-start | bytes 245768 | tf_op jit(solution)/shard_map/ppermute | solution.py:64
  8.5 19.0 %collective-permute-start.6 = (bf16[1,512,256]{2,1,0:T(8,128)(2,1)S(1)}, bf16[1,512,256]{2,1,0:T(8,128)(2,1)S(1)}, u32[]{:S(2)}, u32[]{:S(2)}) collective-permute-start(bf16[1,512,256]{2,1,0:T(8,128)(2,1)S(1)} %bitcast.57), channel_id=1, source_target_pairs={{0,16},{2,18},{4,20},{6,22},{8,24},{10,26},{12,28},{14,30},{16,0},... | collective-permute-start | bytes 786440 | tf_op jit(solution)/shard_map/ppermute | solution.py:37
  11.7 64.1 %collective-permute-start.19 = (bf16[512,4096]{1,0:T(8,128)(2,1)}, bf16[512,4096]{1,0:T(8,128)(2,1)}, u32[]{:S(2)}, u32[]{:S(2)}) collective-permute-start(bf16[512,4096]{1,0:T(8,128)(2,1)} %left_ref), channel_id=1, source_target_pairs={{0,1},{1,0},{2,3},{3,2},{4,5},{5,4},{6,7},{7,6},{8,9},{9,8},{10,11... | collective-permute-start | bytes 12582920 | tf_op jit(solution)/shard_map/ppermute | solution.py:401
  13.8 7.2 %collective-permute-start.3 = (f32[160,128]{1,0:T(8,128)S(1)}, f32[160,128]{1,0:T(8,128)S(1)}, u32[]{:S(2)}, u32[]{:S(2)}) collective-permute-start(f32[160,128]{1,0:T(8,128)S(1)} %add_add_fusion), channel_id=1, source_target_pairs={{0,8},{2,10},{4,12},{6,14},{8,16},{10,18},{12,20},{14,22},{16,24},... | collective-permute-start | bytes 245768 | tf_op jit(solution)/shard_map/ppermute | solution.py:64
  15.5 13.5 %collective-permute-start.4 = (f32[160,128]{1,0:T(8,128)S(1)}, f32[160,128]{1,0:T(8,128)S(1)}, u32[]{:S(2)}, u32[]{:S(2)}) collective-permute-start(f32[160,128]{1,0:T(8,128)S(1)} %add_add_fusion), channel_id=1, source_target_pairs={{0,16},{2,18},{4,20},{6,22},{8,24},{10,26},{12,28},{14,30},{16,0},... | collective-permute-start | bytes 245768 | tf_op jit(solution)/shard_map/ppermute | solution.py:64
  18.1 10.8 %collective-permute-start.5 = (f32[160,128]{1,0:T(8,128)S(1)}, f32[160,128]{1,0:T(8,128)S(1)}, u32[]{:S(2)}, u32[]{:S(2)}) collective-permute-start(f32[160,128]{1,0:T(8,128)S(1)} %add_add_fusion), channel_id=1, source_target_pairs={{0,24},{2,26},{4,28},{6,30},{8,0},{10,2},{12,4},{14,6},{16,8},{18,... | collective-permute-start | bytes 245768 | tf_op jit(solution)/shard_map/ppermute | solution.py:64
  27.6 10.6 %collective-permute-start.10 = (bf16[2,384,256]{2,1,0:T(8,128)(2,1)S(1)}, bf16[2,384,256]{2,1,0:T(8,128)(2,1)S(1)}, u32[]{:S(2)}, u32[]{:S(2)}) collective-permute-start(bf16[2,384,256]{2,1,0:T(8,128)(2,1)S(1)} %slice.279), channel_id=1, source_target_pairs={{0,8},{2,10},{4,12},{6,14},{8,0},{10,2},{12,4},{14,6},{16,24},{18,... | collective-permute-start | bytes 1179656 | tf_op jit(solution)/shard_map/ppermute | solution.py:37
  30.7 7.6 %collective-permute-start.8 = (f32[160,128]{1,0:T(8,128)S(1)}, f32[160,128]{1,0:T(8,128)S(1)}, u32[]{:S(2)}, u32[]{:S(2)}) collective-permute-start(f32[160,128]{1,0:T(8,128)S(1)} %get-tuple-element.248), channel_id=1, source_target_pairs={{0,4},{2,6},{4,0},{6,2},{8,12},{10,14},{12,8},{14,10},{16,20},{18,... | collective-permute-start | bytes 245768 | tf_op jit(solution)/shard_map/ppermute | solution.py:64
  32.3 6.0 %collective-permute-start.9 = (f32[160,128]{1,0:T(8,128)S(1)}, f32[160,128]{1,0:T(8,128)S(1)}, u32[]{:S(2)}, u32[]{:S(2)}) collective-permute-start(f32[160,128]{1,0:T(8,128)S(1)} %get-tuple-element.248), channel_id=1, source_target_pairs={{0,6},{2,4},{4,2},{6,0},{8,14},{10,12},{12,10},{14,8},{16,22},{18,... | collective-permute-start | bytes 245768 | tf_op jit(solution)/shard_map/ppermute | solution.py:64
  38.7 18.1 %collective-permute-start.15 = (bf16[4,192,256]{2,1,0:T(8,128)(2,1)S(1)}, bf16[4,192,256]{2,1,0:T(8,128)(2,1)S(1)}, u32[]{:S(2)}, u32[]{:S(2)}) collective-permute-start(bf16[4,192,256]{2,1,0:T(8,128)(2,1)S(1)} %get-tuple-element.139), channel_id=1, source_target_pairs={{0,4},{2,6},{4,0},{6,2},{8,12},{10,14},{12,8},{14,10},{16,20},{18,... | collective-permute-start | bytes 1179656 | tf_op jit(solution)/shard_map/ppermute | solution.py:37
  40.3 16.7 %collective-permute-start.14 = (bf16[4,192,256]{2,1,0:T(8,128)(2,1)S(1)}, bf16[4,192,256]{2,1,0:T(8,128)(2,1)S(1)}, u32[]{:S(2)}, u32[]{:S(2)}) collective-permute-start(bf16[4,192,256]{2,1,0:T(8,128)(2,1)S(1)} %get-tuple-element.141), channel_id=1, source_target_pairs={{0,2},{2,0},{4,6},{6,4},{8,10},{10,8},{12,14},{14,12},{16,18},{18,... | collective-permute-start | bytes 1179656 | tf_op jit(solution)/shard_map/ppermute | solution.py:37
  42.4 16.3 %collective-permute-start.13 = (bf16[4,128,256]{2,1,0:T(8,128)(2,1)S(1)}, bf16[4,128,256]{2,1,0:T(8,128)(2,1)S(1)}, u32[]{:S(2)}, u32[]{:S(2)}) collective-permute-start(bf16[4,128,256]{2,1,0:T(8,128)(2,1)S(1)} %constant_dynamic-update-slice_fusion.9), channel_id=1, source_target_pairs={{0,4},{2,6},{4,0},{6,2},{8,12},{10,14},{12,8},{14,10},{16,20},{18,... | collective-permute-start | bytes 786440 | tf_op jit(solution)/shard_map/ppermute | solution.py:37
  56.9 18.9 %collective-permute-start.16 = (bf16[8,192,256]{2,1,0:T(8,128)(2,1)S(1)}, bf16[8,192,256]{2,1,0:T(8,128)(2,1)S(1)}, u32[]{:S(2)}, u32[]{:S(2)}) collective-permute-start(bf16[8,192,256]{2,1,0:T(8,128)(2,1)S(1)} %constant_dynamic-update-slice_fusion.11.refs_0_), channel_id=1, source_target_pairs={{0,2},{2,0},{4,6},{6,4},{8,10},{10,8},{12,14},{14,12},{16,18},{18,... | collective-permute-start | bytes 2359304 | tf_op jit(solution)/shard_map/ppermute | solution.py:37
  57.1 18.7 %collective-permute-start.17 = (bf16[8,192,256]{2,1,0:T(8,128)(2,1)S(1)}, bf16[8,192,256]{2,1,0:T(8,128)(2,1)S(1)}, u32[]{:S(2)}, u32[]{:S(2)}) collective-permute-start(bf16[8,192,256]{2,1,0:T(8,128)(2,1)S(1)} %constant_dynamic-update-slice_fusion.13.refs_2_), channel_id=1, source_target_pairs={{0,4},{2,6},{4,0},{6,2},{8,12},{10,14},{12,8},{14,10},{16,20},{18,... | collective-permute-start | bytes 2359304 | tf_op jit(solution)/shard_map/ppermute | solution.py:37
  58.7 13.3 %collective-permute-start.18 = (bf16[8,128,256]{2,1,0:T(8,128)(2,1)S(1)}, bf16[8,128,256]{2,1,0:T(8,128)(2,1)S(1)}, u32[]{:S(2)}, u32[]{:S(2)}) collective-permute-start(bf16[8,128,256]{2,1,0:T(8,128)(2,1)S(1)} %constant_dynamic-update-slice_fusion.15.refs_4_), channel_id=1, source_target_pairs={{0,8},{2,10},{4,12},{6,14},{8,0},{10,2},{12,4},{14,6},{16,24},{18,... | collective-permute-start | bytes 1572872 | tf_op jit(solution)/shard_map/ppermute | solution.py:37
  92.4 26.1 %collective-permute-start.23 = (bf16[256,2048]{1,0:T(8,128)(2,1)S(1)}, bf16[256,2048]{1,0:T(8,128)(2,1)S(1)}, u32[]{:S(2)}, u32[]{:S(2)}) collective-permute-start(bf16[256,2048]{1,0:T(8,128)(2,1)S(1)} %convolution_convert_fusion.3), channel_id=1, source_target_pairs={{0,8},{2,10},{4,12},{6,14},{8,0},{10,2},{12,4},{14,6},{16,24},{18,... | collective-permute-start | bytes 3145736 | tf_op jit(solution)/shard_map/ppermute | solution.py:37
  94.2 26.3 %collective-permute-start.22 = (bf16[256,2048]{1,0:T(8,128)(2,1)S(1)}, bf16[256,2048]{1,0:T(8,128)(2,1)S(1)}, u32[]{:S(2)}, u32[]{:S(2)}) collective-permute-start(bf16[256,2048]{1,0:T(8,128)(2,1)S(1)} %convolution_convert_fusion.2), channel_id=1, source_target_pairs={{0,4},{2,6},{4,0},{6,2},{8,12},{10,14},{12,8},{14,10},{16,20},{18,... | collective-permute-start | bytes 3145736 | tf_op jit(solution)/shard_map/ppermute | solution.py:37
  95.7 26.8 %collective-permute-start.26 = (bf16[256,2048]{1,0:T(8,128)(2,1)S(1)}, bf16[256,2048]{1,0:T(8,128)(2,1)S(1)}, u32[]{:S(2)}, u32[]{:S(2)}) collective-permute-start(bf16[256,2048]{1,0:T(8,128)(2,1)S(1)} %convolution_convert_fusion.1), channel_id=1, source_target_pairs={{0,2},{2,0},{4,6},{6,4},{8,10},{10,8},{12,14},{14,12},{16,18},{18,... | collective-permute-start | bytes 3145736 | tf_op jit(solution)/shard_map/ppermute | solution.py:37
  98.0 42.9 %collective-permute-start.21 = (bf16[256,2048]{1,0:T(8,128)(2,1)S(1)}, bf16[256,2048]{1,0:T(8,128)(2,1)S(1)}, u32[]{:S(2)}, u32[]{:S(2)}) collective-permute-start(bf16[256,2048]{1,0:T(8,128)(2,1)S(1)} %convolution_convert_fusion), channel_id=1, source_target_pairs={{0,8},{2,10},{4,12},{6,14},{8,0},{10,2},{12,4},{14,6},{16,24},{18,... | collective-permute-start | bytes 3145736 | tf_op jit(solution)/shard_map/ppermute | solution.py:37
  118.9 14.9 %collective-permute-start.25 = (bf16[128,2048]{1,0:T(8,128)(2,1)S(1)}, bf16[128,2048]{1,0:T(8,128)(2,1)S(1)}, u32[]{:S(2)}, u32[]{:S(2)}) collective-permute-start(bf16[128,2048]{1,0:T(8,128)(2,1)S(1)} %slice.365), channel_id=1, source_target_pairs={{0,4},{2,6},{4,0},{6,2},{8,12},{10,14},{12,8},{14,10},{16,20},{18,... | collective-permute-start | bytes 1572872 | tf_op jit(solution)/shard_map/ppermute | solution.py:37
  120.9 14.9 %collective-permute-start.24 = (bf16[128,2048]{1,0:T(8,128)(2,1)S(1)}, bf16[128,2048]{1,0:T(8,128)(2,1)S(1)}, u32[]{:S(2)}, u32[]{:S(2)}) collective-permute-start(bf16[128,2048]{1,0:T(8,128)(2,1)S(1)} %slice.364), channel_id=1, source_target_pairs={{0,2},{2,0},{4,6},{6,4},{8,10},{10,8},{12,14},{14,12},{16,18},{18,... | collective-permute-start | bytes 1572872 | tf_op jit(solution)/shard_map/ppermute | solution.py:37
  124.2 23.8 %collective-permute-start.28 = (bf16[128,2048]{1,0:T(8,128)(2,1)S(1)}, bf16[128,2048]{1,0:T(8,128)(2,1)S(1)}, u32[]{:S(2)}, u32[]{:S(2)}) collective-permute-start(bf16[128,2048]{1,0:T(8,128)(2,1)S(1)} %slice.363), channel_id=1, source_target_pairs={{0,4},{2,6},{4,0},{6,2},{8,12},{10,14},{12,8},{14,10},{16,20},{18,... | collective-permute-start | bytes 1572872 | tf_op jit(solution)/shard_map/ppermute | solution.py:37
  134.3 9.8 %collective-permute-start.29 = (bf16[64,2048]{1,0:T(8,128)(2,1)S(1)}, bf16[64,2048]{1,0:T(8,128)(2,1)S(1)}, u32[]{:S(2)}, u32[]{:S(2)}) collective-permute-start(bf16[64,2048]{1,0:T(8,128)(2,1)S(1)} %slice.369), channel_id=1, source_target_pairs={{0,2},{2,0},{4,6},{6,4},{8,10},{10,8},{12,14},{14,12},{16,18},{18,... | collective-permute-start | bytes 786440 | tf_op jit(solution)/shard_map/ppermute | solution.py:37
  136.0 12.7 %collective-permute-start.32 = (bf16[64,2048]{1,0:T(8,128)(2,1)S(1)}, bf16[64,2048]{1,0:T(8,128)(2,1)S(1)}, u32[]{:S(2)}, u32[]{:S(2)}) collective-permute-start(bf16[64,2048]{1,0:T(8,128)(2,1)S(1)} %slice.368), channel_id=1, source_target_pairs={{0,8},{2,10},{4,12},{6,14},{8,0},{10,2},{12,4},{14,6},{16,24},{18,... | collective-permute-start | bytes 786440 | tf_op jit(solution)/shard_map/ppermute | solution.py:37
  142.6 17.7 %collective-permute-start.27 = (bf16[128,2048]{1,0:T(8,128)(2,1)S(1)}, bf16[128,2048]{1,0:T(8,128)(2,1)S(1)}, u32[]{:S(2)}, u32[]{:S(2)}) collective-permute-start(bf16[128,2048]{1,0:T(8,128)(2,1)S(1)} %slice.362), channel_id=1, source_target_pairs={{0,2},{2,0},{4,6},{6,4},{8,10},{10,8},{12,14},{14,12},{16,18},{18,... | collective-permute-start | bytes 1572872 | tf_op jit(solution)/shard_map/ppermute | solution.py:37
  144.2 10.1 %collective-permute-start.31 = (bf16[32,2048]{1,0:T(8,128)(2,1)S(1)}, bf16[32,2048]{1,0:T(8,128)(2,1)S(1)}, u32[]{:S(2)}, u32[]{:S(2)}) collective-permute-start(bf16[32,2048]{1,0:T(8,128)(2,1)S(1)} %slice.373), channel_id=1, source_target_pairs={{0,16},{2,18},{4,20},{6,22},{8,24},{10,26},{12,28},{14,30},{16,0},... | collective-permute-start | bytes 393224 | tf_op jit(solution)/shard_map/ppermute | solution.py:37
  148.2 12.0 %collective-permute-start.30 = (bf16[64,2048]{1,0:T(8,128)(2,1)S(1)}, bf16[64,2048]{1,0:T(8,128)(2,1)S(1)}, u32[]{:S(2)}, u32[]{:S(2)}) collective-permute-start(bf16[64,2048]{1,0:T(8,128)(2,1)S(1)} %slice.367), channel_id=1, source_target_pairs={{0,8},{2,10},{4,12},{6,14},{8,0},{10,2},{12,4},{14,6},{16,24},{18,... | collective-permute-start | bytes 786440 | tf_op jit(solution)/shard_map/ppermute | solution.py:37
  148.9 13.7 %collective-permute-start.34 = (bf16[32,2048]{1,0:T(8,128)(2,1)S(1)}, bf16[32,2048]{1,0:T(8,128)(2,1)S(1)}, u32[]{:S(2)}, u32[]{:S(2)}) collective-permute-start(bf16[32,2048]{1,0:T(8,128)(2,1)S(1)} %slice.372), channel_id=1, source_target_pairs={{0,16},{2,18},{4,20},{6,22},{8,24},{10,26},{12,28},{14,30},{16,0},... | collective-permute-start | bytes 393224 | tf_op jit(solution)/shard_map/ppermute | solution.py:37
  154.5 15.5 %collective-permute-start.37 = (bf16[32,2048]{1,0:T(8,128)(2,1)S(1)}, bf16[32,2048]{1,0:T(8,128)(2,1)S(1)}, u32[]{:S(2)}, u32[]{:S(2)}) collective-permute-start(bf16[32,2048]{1,0:T(8,128)(2,1)S(1)} %get-tuple-element.199), channel_id=1, source_target_pairs={{0,16},{2,18},{4,20},{6,22},{8,24},{10,26},{12,28},{14,30},{16,0},... | collective-permute-start | bytes 393224 | tf_op jit(solution)/shard_map/ppermute | solution.py:37
  160.5 17.7 %collective-permute-start.39 = (bf16[32,2048]{1,0:T(8,128)(2,1)S(1)}, bf16[32,2048]{1,0:T(8,128)(2,1)S(1)}, u32[]{:S(2)}, u32[]{:S(2)}) collective-permute-start(bf16[32,2048]{1,0:T(8,128)(2,1)S(1)} %slice.371), channel_id=1, source_target_pairs={{0,16},{2,18},{4,20},{6,22},{8,24},{10,26},{12,28},{14,30},{16,0},... | collective-permute-start | bytes 393224 | tf_op jit(solution)/shard_map/ppermute | solution.py:37
  161.0 6.4 %collective-permute-start.33 = (bf16[64,2048]{1,0:T(8,128)(2,1)S(1)}, bf16[64,2048]{1,0:T(8,128)(2,1)S(1)}, u32[]{:S(2)}, u32[]{:S(2)}) collective-permute-start(bf16[64,2048]{1,0:T(8,128)(2,1)S(1)} %slice.366), channel_id=1, source_target_pairs={{0,4},{2,6},{4,0},{6,2},{8,12},{10,14},{12,8},{14,10},{16,20},{18,... | collective-permute-start | bytes 786440 | tf_op jit(solution)/shard_map/ppermute | solution.py:37
  162.8 18.3 %collective-permute-start.36 = (bf16[32,2048]{1,0:T(8,128)(2,1)S(1)}, bf16[32,2048]{1,0:T(8,128)(2,1)S(1)}, u32[]{:S(2)}, u32[]{:S(2)}) collective-permute-start(bf16[32,2048]{1,0:T(8,128)(2,1)S(1)} %get-tuple-element.205), channel_id=1, source_target_pairs={{0,16},{2,18},{4,20},{6,22},{8,24},{10,26},{12,28},{14,30},{16,0},... | collective-permute-start | bytes 393224 | tf_op jit(solution)/shard_map/ppermute | solution.py:37
  167.5 17.7 %collective-permute-start.35 = (bf16[32,2048]{1,0:T(8,128)(2,1)S(1)}, bf16[32,2048]{1,0:T(8,128)(2,1)S(1)}, u32[]{:S(2)}, u32[]{:S(2)}) collective-permute-start(bf16[32,2048]{1,0:T(8,128)(2,1)S(1)} %slice.370), channel_id=1, source_target_pairs={{0,16},{2,18},{4,20},{6,22},{8,24},{10,26},{12,28},{14,30},{16,0},... | collective-permute-start | bytes 393224 | tf_op jit(solution)/shard_map/ppermute | solution.py:37
  170.1 8.4 %collective-permute-start.38 = (bf16[64,2048]{1,0:T(8,128)(2,1)S(1)}, bf16[64,2048]{1,0:T(8,128)(2,1)S(1)}, u32[]{:S(2)}, u32[]{:S(2)}) collective-permute-start(bf16[64,2048]{1,0:T(8,128)(2,1)S(1)} %constant_dynamic-update-slice_fusion.17), channel_id=1, source_target_pairs={{0,2},{2,0},{4,6},{6,4},{8,10},{10,8},{12,14},{14,12},{16,18},{18,... | collective-permute-start | bytes 786440 | tf_op jit(solution)/shard_map/ppermute | solution.py:37
  178.4 11.1 %collective-permute-start.43 = (bf16[32,2048]{1,0:T(8,128)(2,1)S(1)}, bf16[32,2048]{1,0:T(8,128)(2,1)S(1)}, u32[]{:S(2)}, u32[]{:S(2)}) collective-permute-start(bf16[32,2048]{1,0:T(8,128)(2,1)S(1)} %get-tuple-element.209), channel_id=1, source_target_pairs={{0,16},{2,18},{4,20},{6,22},{8,24},{10,26},{12,28},{14,30},{16,0},... | collective-permute-start | bytes 393224 | tf_op jit(solution)/shard_map/ppermute | solution.py:37
  178.6 11.1 %collective-permute-start.42 = (bf16[128,2048]{1,0:T(8,128)(2,1)S(1)}, bf16[128,2048]{1,0:T(8,128)(2,1)S(1)}, u32[]{:S(2)}, u32[]{:S(2)}) collective-permute-start(bf16[128,2048]{1,0:T(8,128)(2,1)S(1)} %constant_dynamic-update-slice_fusion.19), channel_id=1, source_target_pairs={{0,4},{2,6},{4,0},{6,2},{8,12},{10,14},{12,8},{14,10},{16,20},{18,... | collective-permute-start | bytes 1572872 | tf_op jit(solution)/shard_map/ppermute | solution.py:37
  181.1 14.0 %collective-permute-start.41 = (bf16[64,2048]{1,0:T(8,128)(2,1)S(1)}, bf16[64,2048]{1,0:T(8,128)(2,1)S(1)}, u32[]{:S(2)}, u32[]{:S(2)}) collective-permute-start(bf16[64,2048]{1,0:T(8,128)(2,1)S(1)} %constant_dynamic-update-slice_fusion.21), channel_id=1, source_target_pairs={{0,8},{2,10},{4,12},{6,14},{8,0},{10,2},{12,4},{14,6},{16,24},{18,... | collective-permute-start | bytes 786440 | tf_op jit(solution)/shard_map/ppermute | solution.py:37
  185.5 10.7 %collective-permute-start.40 = (bf16[32,2048]{1,0:T(8,128)(2,1)S(1)}, bf16[32,2048]{1,0:T(8,128)(2,1)S(1)}, u32[]{:S(2)}, u32[]{:S(2)}) collective-permute-start(bf16[32,2048]{1,0:T(8,128)(2,1)S(1)} %get-tuple-element.215), channel_id=1, source_target_pairs={{0,16},{2,18},{4,20},{6,22},{8,24},{10,26},{12,28},{14,30},{16,0},... | collective-permute-start | bytes 393224 | tf_op jit(solution)/shard_map/ppermute | solution.py:37
  189.5 11.2 %collective-permute-start.45 = (bf16[64,2048]{1,0:T(8,128)(2,1)S(1)}, bf16[64,2048]{1,0:T(8,128)(2,1)S(1)}, u32[]{:S(2)}, u32[]{:S(2)}) collective-permute-start(bf16[64,2048]{1,0:T(8,128)(2,1)S(1)} %constant_dynamic-update-slice_fusion.23), channel_id=1, source_target_pairs={{0,8},{2,10},{4,12},{6,14},{8,0},{10,2},{12,4},{14,6},{16,24},{18,... | collective-permute-start | bytes 786440 | tf_op jit(solution)/shard_map/ppermute | solution.py:37
  189.7 33.4 %collective-permute-start.52 = (bf16[256,2048]{1,0:T(8,128)(2,1)S(1)}, bf16[256,2048]{1,0:T(8,128)(2,1)S(1)}, u32[]{:S(2)}, u32[]{:S(2)}) collective-permute-start(bf16[256,2048]{1,0:T(8,128)(2,1)S(1)} %constant_dynamic-update-slice_fusion.25.refs_1_), channel_id=1, source_target_pairs={{0,8},{2,10},{4,12},{6,14},{8,0},{10,2},{12,4},{14,6},{16,24},{18,... | collective-permute-start | bytes 3145736 | tf_op jit(solution)/shard_map/ppermute | solution.py:37
  195.1 14.9 %collective-permute-start.48 = (bf16[128,2048]{1,0:T(8,128)(2,1)S(1)}, bf16[128,2048]{1,0:T(8,128)(2,1)S(1)}, u32[]{:S(2)}, u32[]{:S(2)}) collective-permute-start(bf16[128,2048]{1,0:T(8,128)(2,1)S(1)} %constant_dynamic-update-slice_fusion.27), channel_id=1, source_target_pairs={{0,2},{2,0},{4,6},{6,4},{8,10},{10,8},{12,14},{14,12},{16,18},{18,... | collective-permute-start | bytes 1572872 | tf_op jit(solution)/shard_map/ppermute | solution.py:37
  196.2 8.8 %collective-permute-start.44 = (bf16[64,2048]{1,0:T(8,128)(2,1)S(1)}, bf16[64,2048]{1,0:T(8,128)(2,1)S(1)}, u32[]{:S(2)}, u32[]{:S(2)}) collective-permute-start(bf16[64,2048]{1,0:T(8,128)(2,1)S(1)} %constant_dynamic-update-slice_fusion.29), channel_id=1, source_target_pairs={{0,4},{2,6},{4,0},{6,2},{8,12},{10,14},{12,8},{14,10},{16,20},{18,... | collective-permute-start | bytes 786440 | tf_op jit(solution)/shard_map/ppermute | solution.py:37
  200.7 15.5 %collective-permute-start.47 = (bf16[128,2048]{1,0:T(8,128)(2,1)S(1)}, bf16[128,2048]{1,0:T(8,128)(2,1)S(1)}, u32[]{:S(2)}, u32[]{:S(2)}) collective-permute-start(bf16[128,2048]{1,0:T(8,128)(2,1)S(1)} %constant_dynamic-update-slice_fusion.31), channel_id=1, source_target_pairs={{0,4},{2,6},{4,0},{6,2},{8,12},{10,14},{12,8},{14,10},{16,20},{18,... | collective-permute-start | bytes 1572872 | tf_op jit(solution)/shard_map/ppermute | solution.py:37
  205.0 15.4 %collective-permute-start.46 = (bf16[128,2048]{1,0:T(8,128)(2,1)S(1)}, bf16[128,2048]{1,0:T(8,128)(2,1)S(1)}, u32[]{:S(2)}, u32[]{:S(2)}) collective-permute-start(bf16[128,2048]{1,0:T(8,128)(2,1)S(1)} %constant_dynamic-update-slice_fusion.33), channel_id=1, source_target_pairs={{0,2},{2,0},{4,6},{6,4},{8,10},{10,8},{12,14},{14,12},{16,18},{18,... | collective-permute-start | bytes 1572872 | tf_op jit(solution)/shard_map/ppermute | solution.py:37
  210.1 26.5 %collective-permute-start.51 = (bf16[256,2048]{1,0:T(8,128)(2,1)S(1)}, bf16[256,2048]{1,0:T(8,128)(2,1)S(1)}, u32[]{:S(2)}, u32[]{:S(2)}) collective-permute-start(bf16[256,2048]{1,0:T(8,128)(2,1)S(1)} %constant_dynamic-update-slice_fusion.35.refs_1_), channel_id=1, source_target_pairs={{0,4},{2,6},{4,0},{6,2},{8,12},{10,14},{12,8},{14,10},{16,20},{18,... | collective-permute-start | bytes 3145736 | tf_op jit(solution)/shard_map/ppermute | solution.py:37
  216.3 23.9 %collective-permute-start.50 = (bf16[256,2048]{1,0:T(8,128)(2,1)S(1)}, bf16[256,2048]{1,0:T(8,128)(2,1)S(1)}, u32[]{:S(2)}, u32[]{:S(2)}) collective-permute-start(bf16[256,2048]{1,0:T(8,128)(2,1)S(1)} %constant_dynamic-update-slice_fusion.37.refs_1_), channel_id=1, source_target_pairs={{0,2},{2,0},{4,6},{6,4},{8,10},{10,8},{12,14},{14,12},{16,18},{18,... | collective-permute-start | bytes 3145736 | tf_op jit(solution)/shard_map/ppermute | solution.py:37
  220.5 25.5 %collective-permute-start.49 = (bf16[256,2048]{1,0:T(8,128)(2,1)S(1)}, bf16[256,2048]{1,0:T(8,128)(2,1)S(1)}, u32[]{:S(2)}, u32[]{:S(2)}) collective-permute-start(bf16[256,2048]{1,0:T(8,128)(2,1)S(1)} %constant_dynamic-update-slice_fusion.39.refs_1_), channel_id=1, source_target_pairs={{0,8},{2,10},{4,12},{6,14},{8,0},{10,2},{12,4},{14,6},{16,24},{18,... | collective-permute-start | bytes 3145736 | tf_op jit(solution)/shard_map/ppermute | solution.py:37
  (28 other events, 165.0 us)
